TPU v7x, 512 devices: a whole 4x8x8 slice. The times are simulated.
512 devices in a mesh: gx: 64 (over y, z_lo, core), gy: 8 (over z_hi, x).
Axes of the slice: x: 4, y: 8, z: 8 (z_hi: 2, z_lo: 4; z = z_hi * 4 + z_lo), core: 2. Of those that a mesh axis runs over, the one named last changes fastest.
Arguments:
- pops: float32 [19, 256, 64, 128], P(None, 'gx', 'gy'), may hold values from 0.005 to 0.5, as said below
- label: int32 [256, 64, 128], P('gx', 'gy'), may hold values from 0 to 2, as said below
- drive: float32 [3, 256, 64, 128], P(None, 'gx', 'gy'), may hold values from -0.3 to 0.3
Outputs:
- momentum: float32 [3, 256, 64, 128], P(None, 'gx', 'gy')
- running: float32 [3, 64, 16, 32], P(None, 'gx', 'gy')
Inputs may be any that keep to these rules, and one draw needn't show every extreme that they name: `pops`: populations near a local equilibrium with density 0.8 to 1.2 and each velocity component within 0.1. `label`: 2 marks walls: every cell with z index 0 or 127, and scattered obstacle cells; elsewhere 1 marks the second solution, 0 the first.
All inputs are finite; a program needn't handle non-finite values.
Results may differ from a plain program's by a relative error of at most 0.0003.
Values sent between devices are 32-bit elements; how exact they have to be, the bound alone decides.
No kernel may reach another device: no remote copies, remote signals or barrier semaphores. Data moves between devices by JAX's collectives and lax.ppermute only.
A program may use at most 64 MiB of HBM per device.

v0:
```python
import math

import jax
import jax.numpy as jnp
from jax import lax
from jax.sharding import PartitionSpec as P

NZ = 128
STEPS = 4


VELOCITY = [
    [0, 0, 0],
    [1, 0, 0],
    [-1, 0, 0],
    [0, 1, 0],
    [0, -1, 0],
    [0, 0, 1],
    [0, 0, -1],
    [1, 1, 0],
    [-1, -1, 0],
    [1, -1, 0],
    [-1, 1, 0],
    [1, 0, 1],
    [-1, 0, -1],
    [1, 0, -1],
    [-1, 0, 1],
    [0, 1, 1],
    [0, -1, -1],
    [0, 1, -1],
    [0, -1, 1],
]
OPPOSITE = [0, 2, 1, 4, 3, 6, 5, 8, 7, 10, 9, 12, 11, 14, 13, 16, 15, 18, 17]
WEIGHTS = [1.0 / 3.0] + [1.0 / 18.0] * 6 + [1.0 / 36.0] * 12
PAIRS = [(0, 0), (1, 1), (2, 2), (0, 1), (0, 2), (1, 2)]
COMPONENT = [[0, 3, 4], [3, 1, 5], [4, 5, 2]]
SLOW_VISCOSITY = 0.0004


def with_halo(cells, sides, width):
    for axis, dim in sides:
        count = lax.axis_size(axis)
        head = lax.slice_in_dim(cells, 0, width, axis=dim)
        tail = lax.slice_in_dim(cells, cells.shape[dim] - width, cells.shape[dim], axis=dim)
        cells = jnp.concatenate(
            [
                lax.ppermute(tail, axis, [(i, (i + 1) % count) for i in range(count)]),
                cells,
                lax.ppermute(head, axis, [((i + 1) % count, i) for i in range(count)]),
            ],
            axis=dim,
        )
    return cells


def collide(pops, label, drive, phase):
    columns = [
        jnp.array([row[axis_id] for row in VELOCITY], jnp.float32).reshape(19, 1, 1, 1)
        for axis_id in range(3)
    ]
    weights = jnp.array(WEIGHTS, jnp.float32).reshape(19, 1, 1, 1)
    density = jnp.sum(pops, axis=0)
    moment = [jnp.sum(columns[axis_id] * pops, axis=0) for axis_id in range(3)]
    speed = [moment[axis_id] / density for axis_id in range(3)]
    along = columns[0] * speed[0] + columns[1] * speed[1] + columns[2] * speed[2]
    square = speed[0] * speed[0] + speed[1] * speed[1] + speed[2] * speed[2]
    balance = weights * density * (1.0 + 3.0 * along + 4.5 * along * along - 1.5 * square)
    second = label == 1
    solid = label == 2
    omega = jnp.where(second, 1.1, 1.6)
    strength = jnp.where(second, 0.6, 1.0) * phase
    push = columns[0] * drive[0] + columns[1] * drive[1] + columns[2] * drive[2]
    relaxed = pops - omega * (pops - balance) + 3.0 * weights * strength * push
    bounced = jnp.stack([pops[other] for other in OPPOSITE])
    post = jnp.where(solid, bounced, relaxed)
    fluid = jnp.where(solid, 0.0, 1.0)
    stress = jnp.stack([moment[first] * moment[later] / density * fluid for first, later in PAIRS])
    return (post, stress)


def momentum_of(pops):
    columns = [
        jnp.array([row[axis_id] for row in VELOCITY], jnp.float32).reshape(19, 1, 1, 1)
        for axis_id in range(3)
    ]
    return jnp.stack([jnp.sum(columns[axis_id] * pops, axis=0) for axis_id in range(3)])


def tables(length):
    index = jnp.arange(length, dtype=jnp.int32)
    turns = index[:, None] * index[None, :] % length
    angle = turns.astype(jnp.float32) * (2.0 * math.pi / length)
    return (jnp.cos(angle), jnp.sin(angle))


def product(values, table):
    return jnp.matmul(values, table, precision=lax.Precision.HIGHEST)


def transform(real, imag, axis_id, inverse):
    length = real.shape[axis_id]
    cosine, sine = tables(length)
    real_last = jnp.moveaxis(real, axis_id, -1)
    imag_last = jnp.moveaxis(imag, axis_id, -1)
    if inverse:
        out_real = (product(real_last, cosine) - product(imag_last, sine)) / length
        out_imag = (product(imag_last, cosine) + product(real_last, sine)) / length
    else:
        out_real = product(real_last, cosine) + product(imag_last, sine)
        out_imag = product(imag_last, cosine) - product(real_last, sine)
    return (jnp.moveaxis(out_real, -1, axis_id), jnp.moveaxis(out_imag, -1, axis_id))


def wavenumber(index, length):
    shifted = index - length * (index >= (length + 1) // 2).astype(jnp.int32)
    return shifted.astype(jnp.float32) * (2.0 * math.pi / length)


def local(pops, label, drive):
    width = pops.shape[1]
    height = pops.shape[2]
    state = pops
    total = jnp.zeros((6,) + pops.shape[1:], jnp.float32)
    for step in range(STEPS):
        phase = math.cos(2.0 * math.pi * (step + 0.5) / STEPS)
        post, stress = collide(state, label, drive, phase)
        total = total + stress
        padded = with_halo(post, (("gx", 1), ("gy", 2)), 1)
        moved = []
        for index in range(19):
            start_x = 1 - VELOCITY[index][0]
            start_y = 1 - VELOCITY[index][1]
            piece = padded[index, start_x : start_x + width, start_y : start_y + height, :]
            moved.append(jnp.roll(piece, VELOCITY[index][2], axis=2))
        state = jnp.stack(moved)
    momentum = momentum_of(state)
    block_x = width // 4
    block_y = height // 4
    slow_z = NZ // 4
    slow = (total / STEPS).reshape(6, block_x, 4, block_y, 4, slow_z, 4).mean(axis=(2, 4, 6))
    cosine_z, sine_z = tables(slow_z)
    spectrum = jnp.stack([product(slow, cosine_z), -product(slow, sine_z)])
    spectrum = lax.all_to_all(spectrum, "gy", split_axis=4, concat_axis=3, tiled=True)
    full_y = spectrum.shape[3]
    part_z = spectrum.shape[4]
    real, imag = transform(spectrum[0], spectrum[1], 2, False)
    spectrum = jnp.stack([real, imag]).reshape(2, 6, block_x, full_y * part_z)
    spectrum = lax.all_to_all(spectrum, "gx", split_axis=3, concat_axis=2, tiled=True)
    full_x = spectrum.shape[2]
    part_m = spectrum.shape[3]
    real, imag = transform(spectrum[0], spectrum[1], 1, False)
    wave_x = wavenumber(jnp.arange(full_x, dtype=jnp.int32), full_x).reshape(full_x, 1)
    flat = lax.axis_index("gx") * part_m + jnp.arange(part_m, dtype=jnp.int32)
    row_y = flat // part_z
    index_z = lax.axis_index("gy") * part_z + flat % part_z
    wave_y = wavenumber(row_y, full_y).reshape(1, part_m)
    wave_z = wavenumber(index_z, slow_z).reshape(1, part_m)
    waves = [wave_x, wave_y, wave_z]
    force_real = [
        waves[0] * imag[COMPONENT[first][0]]
        + waves[1] * imag[COMPONENT[first][1]]
        + waves[2] * imag[COMPONENT[first][2]]
        for first in range(3)
    ]
    force_imag = [
        -(
            waves[0] * real[COMPONENT[first][0]]
            + waves[1] * real[COMPONENT[first][1]]
            + waves[2] * real[COMPONENT[first][2]]
        )
        for first in range(3)
    ]
    wave_sq = wave_x * wave_x + wave_y * wave_y + wave_z * wave_z
    positive = wave_sq > 0
    safe = jnp.where(positive, wave_sq, 1.0)
    inner_real = waves[0] * force_real[0] + waves[1] * force_real[1] + waves[2] * force_real[2]
    inner_imag = waves[0] * force_imag[0] + waves[1] * force_imag[1] + waves[2] * force_imag[2]
    speed_real = jnp.stack(
        [
            jnp.where(
                positive,
                (force_real[first] - waves[first] * inner_real / safe) / (SLOW_VISCOSITY * safe),
                0.0,
            )
            for first in range(3)
        ]
    )
    speed_imag = jnp.stack(
        [
            jnp.where(
                positive,
                (force_imag[first] - waves[first] * inner_imag / safe) / (SLOW_VISCOSITY * safe),
                0.0,
            )
            for first in range(3)
        ]
    )
    real, imag = transform(speed_real, speed_imag, 1, True)
    result = lax.all_to_all(jnp.stack([real, imag]), "gx", split_axis=2, concat_axis=3, tiled=True)
    result = result.reshape(2, 3, block_x, full_y, part_z)
    real, imag = transform(result[0], result[1], 2, True)
    result = lax.all_to_all(jnp.stack([real, imag]), "gy", split_axis=3, concat_axis=4, tiled=True)
    running = (product(result[0], cosine_z) - product(result[1], sine_z)) / slow_z
    return (momentum, running)


def solution(mesh):
    in_specs = (P(None, "gx", "gy", None), P("gx", "gy", None), P(None, "gx", "gy", None))
    out_specs = (P(None, "gx", "gy", None), P(None, "gx", "gy", None))
    return jax.shard_map(local, mesh=mesh, in_specs=in_specs, out_specs=out_specs, check_vma=False)
```

profile of v0, /device:TPU:6, one launch (start us, length us, event | category | flops | bytes accessed | tf_op | source)
XLA Modules:
  0.0 232.1 jit_solution(13145048456317366882)
XLA Ops:
  11.3 10.2 %collective-permute-start = (f32[19,1,8,128]{3,2,1,0:T(8,128)S(1)}, f32[19,1,8,128]{3,2,1,0:T(8,128)S(1)}, u32[]{:S(2)}, u32[]{:S(2)}) collective-permute-start(f32[19,1,8,128]{3,2,1,0:T(8,128)S(1)} %get-tuple-element.234), channel_id=1, source_target_pairs={{8,0},{16,8},{24,16},{32,24},{40,32},{48,40},{56,48},{64,56},{72,6... | collective-permute-start | bytes 233480 | tf_op jit(solution)/shard_map/ppermute | solution.py:49
  28.6 2.6 %collective-permute-done.1 = f32[19,1,8,128]{3,2,1,0:T(8,128)S(1)} collective-permute-done((f32[19,1,8,128]{3,2,1,0:T(8,128)S(1)}, f32[19,1,8,128]{3,2,1,0:T(8,128)S(1)}, u32[]{:S(2)}, u32[]{:S(2)}) %collective-permute-start.1) | collective-permute-done | bytes 77856 | tf_op jit(solution)/shard_map/ppermute | solution.py:47
  31.2 8.1 %collective-permute-start.3 = (f32[19,6,1,128]{3,2,1,0:T(1,128)S(1)}, f32[19,6,1,128]{3,2,1,0:T(1,128)S(1)}, u32[]{:S(2)}, u32[]{:S(2)}) collective-permute-start(f32[19,6,1,128]{3,2,1,0:T(1,128)S(1)} %get-tuple-element.202), channel_id=1, source_target_pairs={{0,1},{1,2},{2,3},{3,4},{4,5},{5,6},{6,7},{7,0},{8,9},{9,10},{10,1... | collective-permute-start | bytes 175112 | tf_op jit(solution)/shard_map/ppermute | solution.py:47
  41.5 9.9 %collective-permute-done.2 = f32[19,6,1,128]{3,2,1,0:T(1,128)S(1)} collective-permute-done((f32[19,6,1,128]{3,2,1,0:T(1,128)S(1)}, f32[19,6,1,128]{3,2,1,0:T(1,128)S(1)}, u32[]{:S(2)}, u32[]{:S(2)}) %collective-permute-start.2) | collective-permute-done | bytes 58400 | tf_op jit(solution)/shard_map/ppermute | solution.py:49
  53.8 3.5 %collective-permute-start.4 = (f32[19,1,8,128]{3,2,1,0:T(8,128)S(1)}, f32[19,1,8,128]{3,2,1,0:T(8,128)S(1)}, u32[]{:S(2)}, u32[]{:S(2)}) collective-permute-start(f32[19,1,8,128]{3,2,1,0:T(8,128)S(1)} %get-tuple-element.230), channel_id=1, source_target_pairs={{8,0},{16,8},{24,16},{32,24},{40,32},{48,40},{56,48},{64,56},{72,6... | collective-permute-start | bytes 233480 | tf_op jit(solution)/shard_map/ppermute | solution.py:49
  60.1 7.0 %collective-permute-done.5 = f32[19,1,8,128]{3,2,1,0:T(8,128)S(1)} collective-permute-done((f32[19,1,8,128]{3,2,1,0:T(8,128)S(1)}, f32[19,1,8,128]{3,2,1,0:T(8,128)S(1)}, u32[]{:S(2)}, u32[]{:S(2)}) %collective-permute-start.5) | collective-permute-done | bytes 77856 | tf_op jit(solution)/shard_map/ppermute | solution.py:47
  69.1 3.9 %collective-permute-start.6 = (f32[19,6,1,128]{3,2,1,0:T(1,128)S(1)}, f32[19,6,1,128]{3,2,1,0:T(1,128)S(1)}, u32[]{:S(2)}, u32[]{:S(2)}) collective-permute-start(f32[19,6,1,128]{3,2,1,0:T(1,128)S(1)} %get-tuple-element.199), channel_id=1, source_target_pairs={{1,0},{2,1},{3,2},{4,3},{5,4},{6,5},{7,6},{0,7},{9,8},{10,9},{11,1... | collective-permute-start | bytes 175112 | tf_op jit(solution)/shard_map/ppermute | solution.py:49
  73.4 7.8 %collective-permute-done.6 = f32[19,6,1,128]{3,2,1,0:T(1,128)S(1)} collective-permute-done((f32[19,6,1,128]{3,2,1,0:T(1,128)S(1)}, f32[19,6,1,128]{3,2,1,0:T(1,128)S(1)}, u32[]{:S(2)}, u32[]{:S(2)}) %collective-permute-start.6) | collective-permute-done | bytes 58400 | tf_op jit(solution)/shard_map/ppermute | solution.py:49
  85.4 2.4 %collective-permute-start.9 = (f32[19,1,8,128]{3,2,1,0:T(8,128)S(1)}, f32[19,1,8,128]{3,2,1,0:T(8,128)S(1)}, u32[]{:S(2)}, u32[]{:S(2)}) collective-permute-start(f32[19,1,8,128]{3,2,1,0:T(8,128)S(1)} %get-tuple-element.227), channel_id=1, source_target_pairs={{0,8},{8,16},{16,24},{24,32},{32,40},{40,48},{48,56},{56,64},{64,7... | collective-permute-start | bytes 233480 | tf_op jit(solution)/shard_map/ppermute | solution.py:47
  88.6 6.4 %collective-permute-done.9 = f32[19,1,8,128]{3,2,1,0:T(8,128)S(1)} collective-permute-done((f32[19,1,8,128]{3,2,1,0:T(8,128)S(1)}, f32[19,1,8,128]{3,2,1,0:T(8,128)S(1)}, u32[]{:S(2)}, u32[]{:S(2)}) %collective-permute-start.9) | collective-permute-done | bytes 77856 | tf_op jit(solution)/shard_map/ppermute | solution.py:47
  97.0 4.1 %collective-permute-start.10 = (f32[19,6,1,128]{3,2,1,0:T(1,128)S(1)}, f32[19,6,1,128]{3,2,1,0:T(1,128)S(1)}, u32[]{:S(2)}, u32[]{:S(2)}) collective-permute-start(f32[19,6,1,128]{3,2,1,0:T(1,128)S(1)} %get-tuple-element.197), channel_id=1, source_target_pairs={{1,0},{2,1},{3,2},{4,3},{5,4},{6,5},{7,6},{0,7},{9,8},{10,9},{11,1... | collective-permute-start | bytes 175112 | tf_op jit(solution)/shard_map/ppermute | solution.py:49
  101.3 7.8 %collective-permute-done.10 = f32[19,6,1,128]{3,2,1,0:T(1,128)S(1)} collective-permute-done((f32[19,6,1,128]{3,2,1,0:T(1,128)S(1)}, f32[19,6,1,128]{3,2,1,0:T(1,128)S(1)}, u32[]{:S(2)}, u32[]{:S(2)}) %collective-permute-start.10) | collective-permute-done | bytes 58400 | tf_op jit(solution)/shard_map/ppermute | solution.py:49
  141.7 4.8 %all-to-all-start = ((f32[2,6,1,2,32]{1,3,2,0,4:T(2,128)}), f32[2,6,1,2,32]{1,3,2,0,4:T(2,128)S(1)}, u32[]{:S(2)}, u32[]{:S(2)}) async-start(f32[2,6,1,2,32]{1,3,2,0,4:T(2,128)} %copy.171), calls=%async_computation | async-start | bytes 131072 | tf_op jit(solution)/shard_map/all_to_all | solution.py:143
  146.6 8.2 %all-to-all-done = f32[2,6,1,2,32]{1,3,2,0,4:T(2,128)S(1)} async-done(((f32[2,6,1,2,32]{1,3,2,0,4:T(2,128)}), f32[2,6,1,2,32]{1,3,2,0,4:T(2,128)S(1)}, u32[]{:S(2)}, u32[]{:S(2)}) %all-to-all-start) | async-done | bytes 3104 | tf_op jit(solution)/shard_map/all_to_all | solution.py:143
  157.8 5.6 %all-to-all-start.1 = ((f32[2,6,1,64]{1,0,2,3:T(2,128)}), f32[2,6,1,64]{1,0,2,3:T(2,128)S(1)}, u32[]{:S(2)}, u32[]{:S(2)}) async-start(f32[2,6,1,64]{1,0,2,3:T(2,128)} %copy.179), calls=%async_computation.1 | async-start | bytes 131072 | tf_op jit(solution)/shard_map/all_to_all | solution.py:148
  164.5 8.8 %all-to-all-done.1 = f32[2,6,1,64]{1,0,2,3:T(2,128)S(1)} async-done(((f32[2,6,1,64]{1,0,2,3:T(2,128)}), f32[2,6,1,64]{1,0,2,3:T(2,128)S(1)}, u32[]{:S(2)}, u32[]{:S(2)}) %all-to-all-start.1) | async-done | bytes 3104 | tf_op jit(solution)/shard_map/all_to_all | solution.py:148
  176.5 4.6 %all-to-all-start.2 = ((f32[2,3,64,1]{1,3,0,2:T(1,128)}), f32[2,3,64,1]{1,3,0,2:T(1,128)S(1)}, u32[]{:S(2)}, u32[]{:S(2)}) async-start(f32[2,3,64,1]{1,3,0,2:T(1,128)} %copy.182), calls=%async_computation.2 | async-start | bytes 131072 | tf_op jit(solution)/shard_map/all_to_all | solution.py:199
  181.1 10.0 %all-to-all-done.2 = f32[2,3,64,1]{1,3,0,2:T(1,128)S(1)} async-done(((f32[2,3,64,1]{1,3,0,2:T(1,128)}), f32[2,3,64,1]{1,3,0,2:T(1,128)S(1)}, u32[]{:S(2)}, u32[]{:S(2)}) %all-to-all-start.2) | async-done | bytes 1568 | tf_op jit(solution)/shard_map/all_to_all | solution.py:199
  193.0 5.3 %all-to-all-start.3 = ((f32[2,3,1,16,4]{4,0,2,1,3:T(2,128)}), f32[2,3,1,16,4]{4,0,2,1,3:T(2,128)S(1)}, u32[]{:S(2)}, u32[]{:S(2)}) async-start(f32[2,3,1,16,4]{4,0,2,1,3:T(2,128)} %copy.187), calls=%async_computation.3 | async-start | bytes 98304 | tf_op jit(solution)/shard_map/all_to_all | solution.py:202
  198.3 2.3 %collective-permute-start.13 = (f32[19,1,8,128]{3,2,1,0:T(8,128)S(1)}, f32[19,1,8,128]{3,2,1,0:T(8,128)S(1)}, u32[]{:S(2)}, u32[]{:S(2)}) collective-permute-start(f32[19,1,8,128]{3,2,1,0:T(8,128)S(1)} %get-tuple-element.222), channel_id=1, source_target_pairs={{8,0},{16,8},{24,16},{32,24},{40,32},{48,40},{56,48},{64,56},{72,6... | collective-permute-start | bytes 233480 | tf_op jit(solution)/shard_map/ppermute | solution.py:49
  202.7 3.8 %all-to-all-done.3 = f32[2,3,1,16,4]{4,0,2,1,3:T(2,128)S(1)} async-done(((f32[2,3,1,16,4]{4,0,2,1,3:T(2,128)}), f32[2,3,1,16,4]{4,0,2,1,3:T(2,128)S(1)}, u32[]{:S(2)}, u32[]{:S(2)}) %all-to-all-start.3) | async-done | bytes 1568 | tf_op jit(solution)/shard_map/all_to_all | solution.py:202
  207.8 2.5 %collective-permute-done.12 = f32[19,1,8,128]{3,2,1,0:T(8,128)S(1)} collective-permute-done((f32[19,1,8,128]{3,2,1,0:T(8,128)S(1)}, f32[19,1,8,128]{3,2,1,0:T(8,128)S(1)}, u32[]{:S(2)}, u32[]{:S(2)}) %collective-permute-start.12) | collective-permute-done | bytes 77856 | tf_op jit(solution)/shard_map/ppermute | solution.py:47
  210.4 7.3 %collective-permute-start.14 = (f32[19,6,1,128]{3,2,1,0:T(1,128)S(1)}, f32[19,6,1,128]{3,2,1,0:T(1,128)S(1)}, u32[]{:S(2)}, u32[]{:S(2)}) collective-permute-start(f32[19,6,1,128]{3,2,1,0:T(1,128)S(1)} %get-tuple-element.196), channel_id=1, source_target_pairs={{0,1},{1,2},{2,3},{3,4},{4,5},{5,6},{6,7},{7,0},{8,9},{9,10},{10,1... | collective-permute-start | bytes 175112 | tf_op jit(solution)/shard_map/ppermute | solution.py:47
  219.6 10.1 %collective-permute-done.15 = f32[19,6,1,128]{3,2,1,0:T(1,128)S(1)} collective-permute-done((f32[19,6,1,128]{3,2,1,0:T(1,128)S(1)}, f32[19,6,1,128]{3,2,1,0:T(1,128)S(1)}, u32[]{:S(2)}, u32[]{:S(2)}) %collective-permute-start.15) | collective-permute-done | bytes 58400 | tf_op jit(solution)/shard_map/ppermute | solution.py:49
  (442 shorter events, 82.5 us)
Async XLA Ops:
  0.6 7.3 %copy-start = (f32[19,4,8,128]{3,2,1,0:T(8,128)S(1)}, f32[19,4,8,128]{3,2,1,0:T(8,128)}, u32[]{:S(2)}) copy-start(f32[19,4,8,128]{3,2,1,0:T(8,128)} %param.22) | copy-start | bytes 933892
  11.3 17.2 %collective-permute-start = (f32[19,1,8,128]{3,2,1,0:T(8,128)S(1)}, f32[19,1,8,128]{3,2,1,0:T(8,128)S(1)}, u32[]{:S(2)}, u32[]{:S(2)}) collective-permute-start(f32[19,1,8,128]{3,2,1,0:T(8,128)S(1)} %get-tuple-element.234), channel_id=1, source_target_pairs={{8,0},{16,8},{24,16},{32,24},{40,32},{48,40},{56,48},{64,56},{72,6... | collective-permute-start | bytes 233480 | tf_op jit(solution)/shard_map/ppermute | solution.py:49
  21.5 9.6 %collective-permute-start.1 = (f32[19,1,8,128]{3,2,1,0:T(8,128)S(1)}, f32[19,1,8,128]{3,2,1,0:T(8,128)S(1)}, u32[]{:S(2)}, u32[]{:S(2)}) collective-permute-start(f32[19,1,8,128]{3,2,1,0:T(8,128)S(1)} %get-tuple-element.235), channel_id=1, source_target_pairs={{0,8},{8,16},{16,24},{24,32},{32,40},{40,48},{48,56},{56,64},{64,7... | collective-permute-start | bytes 233480 | tf_op jit(solution)/shard_map/ppermute | solution.py:47
  31.2 10.1 %collective-permute-start.3 = (f32[19,6,1,128]{3,2,1,0:T(1,128)S(1)}, f32[19,6,1,128]{3,2,1,0:T(1,128)S(1)}, u32[]{:S(2)}, u32[]{:S(2)}) collective-permute-start(f32[19,6,1,128]{3,2,1,0:T(1,128)S(1)} %get-tuple-element.202), channel_id=1, source_target_pairs={{0,1},{1,2},{2,3},{3,4},{4,5},{5,6},{6,7},{7,0},{8,9},{9,10},{10,1... | collective-permute-start | bytes 175112 | tf_op jit(solution)/shard_map/ppermute | solution.py:47
  39.4 12.1 %collective-permute-start.2 = (f32[19,6,1,128]{3,2,1,0:T(1,128)S(1)}, f32[19,6,1,128]{3,2,1,0:T(1,128)S(1)}, u32[]{:S(2)}, u32[]{:S(2)}) collective-permute-start(f32[19,6,1,128]{3,2,1,0:T(1,128)S(1)} %get-tuple-element.201), channel_id=1, source_target_pairs={{1,0},{2,1},{3,2},{4,3},{5,4},{6,5},{7,6},{0,7},{9,8},{10,9},{11,1... | collective-permute-start | bytes 175112 | tf_op jit(solution)/shard_map/ppermute | solution.py:49
  53.8 6.3 %collective-permute-start.4 = (f32[19,1,8,128]{3,2,1,0:T(8,128)S(1)}, f32[19,1,8,128]{3,2,1,0:T(8,128)S(1)}, u32[]{:S(2)}, u32[]{:S(2)}) collective-permute-start(f32[19,1,8,128]{3,2,1,0:T(8,128)S(1)} %get-tuple-element.230), channel_id=1, source_target_pairs={{8,0},{16,8},{24,16},{32,24},{40,32},{48,40},{56,48},{64,56},{72,6... | collective-permute-start | bytes 233480 | tf_op jit(solution)/shard_map/ppermute | solution.py:49
  57.3 9.8 %collective-permute-start.5 = (f32[19,1,8,128]{3,2,1,0:T(8,128)S(1)}, f32[19,1,8,128]{3,2,1,0:T(8,128)S(1)}, u32[]{:S(2)}, u32[]{:S(2)}) collective-permute-start(f32[19,1,8,128]{3,2,1,0:T(8,128)S(1)} %get-tuple-element.231), channel_id=1, source_target_pairs={{0,8},{8,16},{16,24},{24,32},{32,40},{40,48},{48,56},{56,64},{64,7... | collective-permute-start | bytes 233480 | tf_op jit(solution)/shard_map/ppermute | solution.py:47
  67.1 6.1 %collective-permute-start.7 = (f32[19,6,1,128]{3,2,1,0:T(1,128)S(1)}, f32[19,6,1,128]{3,2,1,0:T(1,128)S(1)}, u32[]{:S(2)}, u32[]{:S(2)}) collective-permute-start(f32[19,6,1,128]{3,2,1,0:T(1,128)S(1)} %get-tuple-element.200), channel_id=1, source_target_pairs={{0,1},{1,2},{2,3},{3,4},{4,5},{5,6},{6,7},{7,0},{8,9},{9,10},{10,1... | collective-permute-start | bytes 175112 | tf_op jit(solution)/shard_map/ppermute | solution.py:47
  69.1 12.1 %collective-permute-start.6 = (f32[19,6,1,128]{3,2,1,0:T(1,128)S(1)}, f32[19,6,1,128]{3,2,1,0:T(1,128)S(1)}, u32[]{:S(2)}, u32[]{:S(2)}) collective-permute-start(f32[19,6,1,128]{3,2,1,0:T(1,128)S(1)} %get-tuple-element.199), channel_id=1, source_target_pairs={{1,0},{2,1},{3,2},{4,3},{5,4},{6,5},{7,6},{0,7},{9,8},{10,9},{11,1... | collective-permute-start | bytes 175112 | tf_op jit(solution)/shard_map/ppermute | solution.py:49
  83.4 5.2 %collective-permute-start.8 = (f32[19,1,8,128]{3,2,1,0:T(8,128)S(1)}, f32[19,1,8,128]{3,2,1,0:T(8,128)S(1)}, u32[]{:S(2)}, u32[]{:S(2)}) collective-permute-start(f32[19,1,8,128]{3,2,1,0:T(8,128)S(1)} %get-tuple-element.226), channel_id=1, source_target_pairs={{8,0},{16,8},{24,16},{32,24},{40,32},{48,40},{56,48},{64,56},{72,6... | collective-permute-start | bytes 233480 | tf_op jit(solution)/shard_map/ppermute | solution.py:49
  85.4 9.6 %collective-permute-start.9 = (f32[19,1,8,128]{3,2,1,0:T(8,128)S(1)}, f32[19,1,8,128]{3,2,1,0:T(8,128)S(1)}, u32[]{:S(2)}, u32[]{:S(2)}) collective-permute-start(f32[19,1,8,128]{3,2,1,0:T(8,128)S(1)} %get-tuple-element.227), channel_id=1, source_target_pairs={{0,8},{8,16},{16,24},{24,32},{32,40},{40,48},{48,56},{56,64},{64,7... | collective-permute-start | bytes 233480 | tf_op jit(solution)/shard_map/ppermute | solution.py:47
  95.1 6.1 %collective-permute-start.11 = (f32[19,6,1,128]{3,2,1,0:T(1,128)S(1)}, f32[19,6,1,128]{3,2,1,0:T(1,128)S(1)}, u32[]{:S(2)}, u32[]{:S(2)}) collective-permute-start(f32[19,6,1,128]{3,2,1,0:T(1,128)S(1)} %get-tuple-element.198), channel_id=1, source_target_pairs={{0,1},{1,2},{2,3},{3,4},{4,5},{5,6},{6,7},{7,0},{8,9},{9,10},{10,1... | collective-permute-start | bytes 175112 | tf_op jit(solution)/shard_map/ppermute | solution.py:47
  97.0 12.1 %collective-permute-start.10 = (f32[19,6,1,128]{3,2,1,0:T(1,128)S(1)}, f32[19,6,1,128]{3,2,1,0:T(1,128)S(1)}, u32[]{:S(2)}, u32[]{:S(2)}) collective-permute-start(f32[19,6,1,128]{3,2,1,0:T(1,128)S(1)} %get-tuple-element.197), channel_id=1, source_target_pairs={{1,0},{2,1},{3,2},{4,3},{5,4},{6,5},{7,6},{0,7},{9,8},{10,9},{11,1... | collective-permute-start | bytes 175112 | tf_op jit(solution)/shard_map/ppermute | solution.py:49
  101.2 9.5 %copy-start.21 = (f32[1,4,8,128]{3,2,1,0:T(8,128)}, f32[1,4,8,128]{3,2,1,0:T(8,128)S(1)}, u32[]{:S(2)}) copy-start(f32[1,4,8,128]{3,2,1,0:T(8,128)S(1)} %get-tuple-element.78) | copy-start | bytes 49156
  141.7 13.0 %all-to-all-start = ((f32[2,6,1,2,32]{1,3,2,0,4:T(2,128)}), f32[2,6,1,2,32]{1,3,2,0,4:T(2,128)S(1)}, u32[]{:S(2)}, u32[]{:S(2)}) async-start(f32[2,6,1,2,32]{1,3,2,0,4:T(2,128)} %copy.171), calls=%async_computation | async-start | bytes 131072 | tf_op jit(solution)/shard_map/all_to_all | solution.py:143
  155.6 7.8 %copy-start.38 = (f32[19]{0:T(128)S(1)}, f32[19]{0:T(128)}, u32[]{:S(2)}) copy-start(f32[19]{0:T(128)} %constant.177.clone) | copy-start | bytes 232
  157.8 5.7 %copy-start.20 = (f32[4,8,128]{2,1,0:T(8,128)S(1)}, f32[4,8,128]{2,1,0:T(8,128)}, u32[]{:S(2)}) copy-start(f32[4,8,128]{2,1,0:T(8,128)} %copy-done.19) | copy-start | bytes 49156
  157.8 15.5 %all-to-all-start.1 = ((f32[2,6,1,64]{1,0,2,3:T(2,128)}), f32[2,6,1,64]{1,0,2,3:T(2,128)S(1)}, u32[]{:S(2)}, u32[]{:S(2)}) async-start(f32[2,6,1,64]{1,0,2,3:T(2,128)} %copy.179), calls=%async_computation.1 | async-start | bytes 131072 | tf_op jit(solution)/shard_map/all_to_all | solution.py:148
  176.5 14.6 %all-to-all-start.2 = ((f32[2,3,64,1]{1,3,0,2:T(1,128)}), f32[2,3,64,1]{1,3,0,2:T(1,128)S(1)}, u32[]{:S(2)}, u32[]{:S(2)}) async-start(f32[2,3,64,1]{1,3,0,2:T(1,128)} %copy.182), calls=%async_computation.2 | async-start | bytes 131072 | tf_op jit(solution)/shard_map/all_to_all | solution.py:199
  193.0 13.5 %all-to-all-start.3 = ((f32[2,3,1,16,4]{4,0,2,1,3:T(2,128)}), f32[2,3,1,16,4]{4,0,2,1,3:T(2,128)S(1)}, u32[]{:S(2)}, u32[]{:S(2)}) async-start(f32[2,3,1,16,4]{4,0,2,1,3:T(2,128)} %copy.187), calls=%async_computation.3 | async-start | bytes 98304 | tf_op jit(solution)/shard_map/all_to_all | solution.py:202
  198.3 9.4 %collective-permute-start.13 = (f32[19,1,8,128]{3,2,1,0:T(8,128)S(1)}, f32[19,1,8,128]{3,2,1,0:T(8,128)S(1)}, u32[]{:S(2)}, u32[]{:S(2)}) collective-permute-start(f32[19,1,8,128]{3,2,1,0:T(8,128)S(1)} %get-tuple-element.222), channel_id=1, source_target_pairs={{8,0},{16,8},{24,16},{32,24},{40,32},{48,40},{56,48},{64,56},{72,6... | collective-permute-start | bytes 233480 | tf_op jit(solution)/shard_map/ppermute | solution.py:49
  200.7 9.6 %collective-permute-start.12 = (f32[19,1,8,128]{3,2,1,0:T(8,128)S(1)}, f32[19,1,8,128]{3,2,1,0:T(8,128)S(1)}, u32[]{:S(2)}, u32[]{:S(2)}) collective-permute-start(f32[19,1,8,128]{3,2,1,0:T(8,128)S(1)} %get-tuple-element.223), channel_id=1, source_target_pairs={{0,8},{8,16},{16,24},{24,32},{32,40},{40,48},{48,56},{56,64},{64,7... | collective-permute-start | bytes 233480 | tf_op jit(solution)/shard_map/ppermute | solution.py:47
  210.4 9.2 %collective-permute-start.14 = (f32[19,6,1,128]{3,2,1,0:T(1,128)S(1)}, f32[19,6,1,128]{3,2,1,0:T(1,128)S(1)}, u32[]{:S(2)}, u32[]{:S(2)}) collective-permute-start(f32[19,6,1,128]{3,2,1,0:T(1,128)S(1)} %get-tuple-element.196), channel_id=1, source_target_pairs={{0,1},{1,2},{2,3},{3,4},{4,5},{5,6},{6,7},{7,0},{8,9},{9,10},{10,1... | collective-permute-start | bytes 175112 | tf_op jit(solution)/shard_map/ppermute | solution.py:47
  217.7 12.1 %collective-permute-start.15 = (f32[19,6,1,128]{3,2,1,0:T(1,128)S(1)}, f32[19,6,1,128]{3,2,1,0:T(1,128)S(1)}, u32[]{:S(2)}, u32[]{:S(2)}) collective-permute-start(f32[19,6,1,128]{3,2,1,0:T(1,128)S(1)} %get-tuple-element.195), channel_id=1, source_target_pairs={{1,0},{2,1},{3,2},{4,3},{5,4},{6,5},{7,6},{0,7},{9,8},{10,9},{11,1... | collective-permute-start | bytes 175112 | tf_op jit(solution)/shard_map/ppermute | solution.py:49
  (35 other events, 27.3 us)
where the time goes:
time: 234 us; the launch traced here: 232 us
  waiting for transfers between devices  85.1 us (36%)
  starting transfers between devices  77.7 us (33%)
  local copies, waits for them, and re-layouts  53.3 us (23%)
  other arithmetic  8.57 us (4%)
  matrix products  4.96 us (2%)
  between operations  2.44 us (1%)
    ppermute x8, waiting for transfers between devices, with_halo(): lax.ppermute(head, axis, [((i + 1) % count, i) for i in range(count)])  35.6 us
    ppermute x8, starting transfers between devices, with_halo(): lax.ppermute(head, axis, [((i + 1) % count, i) for i in range(count)])  29.9 us
    ppermute x8, starting transfers between devices, with_halo(): lax.ppermute(tail, axis, [(i, (i + 1) % count) for i in range(count)])  27.5 us
    another operation x52, local copies, waits for them, and re-layouts, collide(): jnp.stack([moment[first] * moment[later] / density * fluid for first, lat...  26.4 us
    unnamed x172, local copies, waits for them, and re-layouts  19.1 us
    ppermute x8, waiting for transfers between devices, with_halo(): lax.ppermute(tail, axis, [(i, (i + 1) % count) for i in range(count)])  18.7 us
    all_to_all x1, waiting for transfers between devices, local(): lax.all_to_all(jnp.stack([real, imag]), 'gx', split_axis=2, concat_axis=3...  9.99 us
    all_to_all x1, waiting for transfers between devices, local(): lax.all_to_all(spectrum, 'gx', split_axis=3, concat_axis=2, tiled=True)  8.78 us
  transfers between devices with their start and end apart: 20, of which 13 were waited for; matrix products, arithmetic and copies ran while one was open for 4% of the time, Pallas kernels for 0%

commit v1 on v0

v1 whole, which is shorter than its diff:
```python
import functools
import math

import jax
import jax.numpy as jnp
import numpy as np
from jax import lax
from jax.experimental import pallas as pl
from jax.experimental.pallas import tpu as pltpu
from jax.sharding import PartitionSpec as P

NZ = 128
STEPS = 4
SZ = 32
LX = 4
LY = 8
VELOCITY = [
    [0, 0, 0],
    [1, 0, 0],
    [-1, 0, 0],
    [0, 1, 0],
    [0, -1, 0],
    [0, 0, 1],
    [0, 0, -1],
    [1, 1, 0],
    [-1, -1, 0],
    [1, -1, 0],
    [-1, 1, 0],
    [1, 0, 1],
    [-1, 0, -1],
    [1, 0, -1],
    [-1, 0, 1],
    [0, 1, 1],
    [0, -1, -1],
    [0, 1, -1],
    [0, -1, 1],
]
OPPOSITE = [0, 2, 1, 4, 3, 6, 5, 8, 7, 10, 9, 12, 11, 14, 13, 16, 15, 18, 17]
WEIGHTS = [1.0 / 3.0] + [1.0 / 18.0] * 6 + [1.0 / 36.0] * 12
PAIRS = [(0, 0), (1, 1), (2, 2), (0, 1), (0, 2), (1, 2)]
COMPONENT = [[0, 3, 4], [3, 1, 5], [4, 5, 2]]
SLOW_VISCOSITY = 0.0004
PHASES = [math.cos(2.0 * math.pi * (step + 0.5) / STEPS) for step in range(STEPS)]

CHANNELS = 23
CX = [v[0] for v in VELOCITY] + [0] * 4
CY = [v[1] for v in VELOCITY] + [0] * 4
HIGHEST = lax.Precision.HIGHEST


def pack_y(sign):
    out, at = [], 0
    for x in range(LX):
        for ch in range(CHANNELS):
            n = 3 if CY[ch] == sign else 2
            out.append((ch, x, LY - n if sign > 0 else 0, n, at))
            at += n
    return out, -(-at // 8) * 8


def pack_x(sign):
    out, at = [], 0
    layers = (3, 2, 1) if sign > 0 else (0, 1, 2)
    for depth, x in enumerate(layers):
        for ch in range(CHANNELS):
            if depth == 2 and CX[ch] != sign:
                continue
            low = 3 if CY[ch] == 1 else 2
            high = 3 if CY[ch] == -1 else 2
            out.append((ch, x, low, high, at))
            at += low + LY + high
    return out, -(-at // 8) * 8


Y_UP, Y_ROWS = pack_y(1)
Y_DOWN, _ = pack_y(-1)
X_RIGHT, X_ROWS = pack_x(1)
X_LEFT, _ = pack_x(-1)
Y_UP_AT = {(ch, x): (n, at) for ch, x, _, n, at in Y_UP}
Y_DOWN_AT = {(ch, x): (n, at) for ch, x, _, n, at in Y_DOWN}
UP = [i for i in range(19) if CY[i] == 1]
DOWN = [i for i in range(19) if CY[i] == -1]
RIGHT = [i for i in range(19) if CX[i] == 1]
LEFT = [i for i in range(19) if CX[i] == -1]
EDGE_Y_ROWS = 24
EDGE_X_ROWS = 40


def collide(f, label, drive, phase):
    rho = f[0]
    for i in range(1, 19):
        rho = rho + f[i]
    j = []
    for axis in range(3):
        total = None
        for i in range(1, 19, 2):
            c = VELOCITY[i][axis]
            if c == 0:
                continue
            term = f[i] - f[i + 1] if c > 0 else f[i + 1] - f[i]
            total = term if total is None else total + term
        j.append(total)
    second = label == 1.0
    solid = label == 2.0
    omega = jnp.where(second, 1.1, 1.6)
    keep = 1.0 - omega
    strength = jnp.where(second, 0.6 * phase, phase)
    inverse = 1.0 / rho
    mix = [omega * j[axis] + strength * drive[axis] for axis in range(3)]
    base = omega * (rho - 1.5 * (j[0] * j[0] + j[1] * j[1] + j[2] * j[2]) * inverse)
    curve = 4.5 * omega * inverse

    def along(vector, c):
        total = None
        for axis in range(3):
            if c[axis] == 0:
                continue
            if total is None:
                total = vector[axis] if c[axis] > 0 else -vector[axis]
            else:
                total = total + vector[axis] if c[axis] > 0 else total - vector[axis]
        return total

    post = [None] * 19
    post[0] = jnp.where(solid, f[0], keep * f[0] + WEIGHTS[0] * base)
    for i in range(1, 19, 2):
        w = WEIGHTS[i]
        cj = along(j, VELOCITY[i])
        even = w * (base + curve * (cj * cj))
        odd = (3.0 * w) * along(mix, VELOCITY[i])
        post[i] = jnp.where(solid, f[i + 1], keep * f[i] + (even + odd))
        post[i + 1] = jnp.where(solid, f[i], keep * f[i + 1] + (even - odd))
    fluid = jnp.where(solid, 0.0, inverse)
    stress = [j[a] * j[b] * fluid for a, b in PAIRS]
    return post, stress


def first_kernel(pops, label, drive, cells, total, send_a, send_b, box):
    up = lax.rem(lax.axis_index("gy"), 2)
    down = 1 - up
    sums = [jnp.zeros((LY, NZ), jnp.float32)] * 6
    for x in range(LX):
        f = [pops[i, x] for i in range(19)]
        lab = label[x].astype(jnp.float32)
        force = [drive[axis, x] for axis in range(3)]
        post, stress = collide(f, lab, force, PHASES[0])
        for i in range(19):
            cells[i, x] = post[i]
        cells[19, x] = lab
        for axis in range(3):
            cells[20 + axis, x] = force[axis]
        sums = [sums[k] + stress[k] for k in range(6)]
    for k in range(6):
        total[k] = sums[k]
    for ch, x, row, n, at in Y_UP:
        box[up, at : at + n, :] = cells[ch, x, row : row + n, :]
    for ch, x, row, n, at in Y_DOWN:
        box[down, at : at + n, :] = cells[ch, x, row : row + n, :]
    send_a[...] = box[0]
    send_b[...] = box[1]


def second_kernel(cells, got_a, got_b, send_a, send_b, rows, box):
    odd_y = lax.rem(lax.axis_index("gy"), 2)
    low_slot, high_slot = 1 - odd_y, odd_y
    right = lax.rem(lax.axis_index("gx"), 2)
    rows[0] = got_a[...]
    rows[1] = got_b[...]
    for slot, entries in ((right, X_RIGHT), (1 - right, X_LEFT)):
        for ch, x, low, high, at in entries:
            n, source = Y_UP_AT[ch, x]
            box[slot, at : at + n, :] = rows[low_slot, source : source + n, :]
            box[slot, at + low : at + low + LY, :] = cells[ch, x]
            n, source = Y_DOWN_AT[ch, x]
            box[slot, at + low + LY : at + low + LY + n, :] = rows[high_slot, source : source + n, :]
    send_a[...] = box[0]
    send_b[...] = box[1]


ROW0 = 12
COL0 = 3


def third_kernel(
    cells, total, ya, yb, xa, xb, post3, spread, edge_a, edge_b, rows, cols, one, two, aux, sums, box
):
    odd_y = lax.rem(lax.axis_index("gy"), 2)
    odd_x = lax.rem(lax.axis_index("gx"), 2)
    low_slot, high_slot = 1 - odd_y, odd_y
    left_slot, right_slot = 1 - odd_x, odd_x
    rows[0] = ya[...]
    rows[1] = yb[...]
    cols[0] = xa[...]
    cols[1] = xb[...]

    def place(ch, x, row, values):
        n = values.shape[0]
        if ch < 19:
            one[ch, x + COL0, row + ROW0 : row + ROW0 + n, :] = values
        else:
            aux[ch - 19, x + COL0, row + ROW0 : row + ROW0 + n, :] = values

    for ch in range(CHANNELS):
        for x in range(LX):
            place(ch, x, 0, cells[ch, x])
    for ch, x, row, n, at in Y_UP:
        place(ch, x, row - LY, rows[low_slot, at : at + n, :])
    for ch, x, row, n, at in Y_DOWN:
        place(ch, x, row + LY, rows[high_slot, at : at + n, :])
    for ch, x, low, high, at in X_RIGHT:
        place(ch, x - LX, -low, cols[left_slot, at : at + low + LY + high, :])
    for ch, x, low, high, at in X_LEFT:
        place(ch, x + LX, -low, cols[right_slot, at : at + low + LY + high, :])

    def arrive(source, x, row, n):
        f = []
        for i in range(19):
            cx, cy, cz = VELOCITY[i]
            value = source[i, x - cx, row - cy : row - cy + n, :]
            f.append(pltpu.roll(value, cz % NZ, 1) if cz else value)
        lab = aux[0, x, row : row + n, :]
        force = [aux[1 + axis, x, row : row + n, :] for axis in range(3)]
        return f, lab, force

    wide = 16
    start = ROW0 - 4
    sums[...] = jnp.zeros(sums.shape, jnp.float32)
    for step, source, target, least, most in ((1, one, two, 1, 9), (2, two, one, 2, 8)):

        def layer(x, carry, step=step, source=source, target=target):
            f, lab, force = arrive(source, x, start, wide)
            post, stress = collide(f, lab, force, PHASES[step])
            for i in range(19):
                target[i, x, start : start + wide, :] = post[i]
            own = jnp.logical_and(x >= COL0, x < COL0 + LX)
            for k in range(6):
                sums[k] += jnp.where(own, stress[k], 0.0)
            return carry

        lax.fori_loop(least, most, layer, 0)
    last = [total[k] + sums[k, 4:12, :] for k in range(6)]
    for x in range(LX):
        f, lab, force = arrive(one, x + COL0, ROW0, LY)
        post, stress = collide(f, lab, force, PHASES[3])
        for i in range(19):
            post3[i, x] = post[i]
        last = [last[k] + stress[k] for k in range(6)]
    stacked = jnp.concatenate(last, axis=0)
    r = lax.broadcasted_iota(jnp.int32, (16, 48), 0)
    c = lax.broadcasted_iota(jnp.int32, (16, 48), 1)
    chosen = jnp.logical_and((r & 7) == (c >> 3), (r >> 3) == ((c & 7) >> 2))
    left = jnp.where(chosen, 1.0, 0.0)
    halves = jnp.dot(left, stacked, precision=HIGHEST, preferred_element_type=jnp.float32)
    z = lax.broadcasted_iota(jnp.int32, (NZ, NZ), 0)
    lane = lax.broadcasted_iota(jnp.int32, (NZ, NZ), 1)
    mean = 1.0 / (STEPS * 64)
    slow = jnp.zeros((8, NZ), jnp.float32)
    for half in range(2):
        table = jnp.where(lane == (z >> 2) + half * SZ, mean, 0.0)
        slow = slow + jnp.dot(
            halves[half * 8 : half * 8 + 8],
            table,
            precision=HIGHEST,
            preferred_element_type=jnp.float32,
        )
    for d in range(spread.shape[0]):
        spread[d] = slow
    for k, i in enumerate(UP):
        for x in range(LX):
            box[odd_y, k * LX + x : k * LX + x + 1, :] = post3[i, x, LY - 1 : LY, :]
    for k, i in enumerate(DOWN):
        for x in range(LX):
            box[1 - odd_y, k * LX + x : k * LX + x + 1, :] = post3[i, x, 0:1, :]
    edge_a[...] = box[0]
    edge_b[...] = box[1]


def edge_kernel(post3, ya, yb, send_a, send_b, rows, box):
    odd_y = lax.rem(lax.axis_index("gy"), 2)
    low_slot, high_slot = 1 - odd_y, odd_y
    right = lax.rem(lax.axis_index("gx"), 2)
    rows[0] = ya[...]
    rows[1] = yb[...]
    for slot, comps, x in ((right, RIGHT, LX - 1), (1 - right, LEFT, 0)):
        for k, i in enumerate(comps):
            at = k * LY
            if CY[i] == 0:
                box[slot, at : at + LY, :] = post3[i, x]
            elif CY[i] == 1:
                source = UP.index(i) * LX + x
                box[slot, at : at + 1, :] = rows[low_slot, source : source + 1, :]
                box[slot, at + 1 : at + LY, :] = post3[i, x, 0 : LY - 1, :]
            else:
                source = DOWN.index(i) * LX + x
                box[slot, at : at + LY - 1, :] = post3[i, x, 1:LY, :]
                box[slot, at + LY - 1 : at + LY, :] = rows[high_slot, source : source + 1, :]
    send_a[...] = box[0]
    send_b[...] = box[1]


def momentum_kernel(post3, ya, yb, xa, xb, out, rows, cols, work):
    odd_y = lax.rem(lax.axis_index("gy"), 2)
    odd_x = lax.rem(lax.axis_index("gx"), 2)
    rows[0] = ya[...]
    rows[1] = yb[...]
    cols[0] = xa[...]
    cols[1] = xb[...]
    for i in range(1, 19):
        for x in range(LX):
            work[i, x + 1, 8:16, :] = post3[i, x]
    for k, i in enumerate(UP):
        for x in range(LX):
            at = k * LX + x
            work[i, x + 1, 7:8, :] = rows[1 - odd_y, at : at + 1, :]
    for k, i in enumerate(DOWN):
        for x in range(LX):
            at = k * LX + x
            work[i, x + 1, 16:17, :] = rows[odd_y, at : at + 1, :]
    for k, i in enumerate(RIGHT):
        work[i, 0, 8 - CY[i] : 16 - CY[i], :] = cols[1 - odd_x, k * LY : k * LY + LY, :]
    for k, i in enumerate(LEFT):
        work[i, LX + 1, 8 - CY[i] : 16 - CY[i], :] = cols[odd_x, k * LY : k * LY + LY, :]
    for x in range(LX):
        f = [None]
        for i in range(1, 19):
            cx, cy, cz = VELOCITY[i]
            value = work[i, x + 1 - cx, 8 - cy : 16 - cy, :]
            f.append(pltpu.roll(value, cz % NZ, 1) if cz else value)
        for axis in range(3):
            total = None
            for i in range(1, 19, 2):
                c = VELOCITY[i][axis]
                if c == 0:
                    continue
                term = f[i] - f[i + 1] if c > 0 else f[i + 1] - f[i]
                total = term if total is None else total + term
            out[axis, x] = total


LANES = 384


@functools.cache
def operator_tables(sx, sy):
    waves = [2.0 * math.pi * np.fft.fftfreq(n) for n in (sx, sy, SZ)]
    k = np.meshgrid(*waves, indexing="ij")
    square = k[0] ** 2 + k[1] ** 2 + k[2] ** 2
    positive = square > 0
    safe = np.where(positive, square, 1.0)
    half = SZ // 2 + 1
    modes = sy * half
    table = np.zeros((18, sx, LANES))
    twist = np.zeros((24, LANES))
    imaginary = []
    for a in range(3):
        for c in range(6):
            force = [
                -1j * sum(k[b] for b in range(3) if COMPONENT[first][b] == c) + 0.0 * k[0]
                for first in range(3)
            ]
            inner = k[0] * force[0] + k[1] * force[1] + k[2] * force[2]
            gain = np.where(positive, (force[a] - k[a] * inner / safe) / (SLOW_VISCOSITY * safe), 0.0)
            flipped = gain
            for axis in range(3):
                flipped = np.roll(np.flip(flipped, axis), 1, axis)
            gain = 0.5 * (gain + np.conj(flipped))
            line = np.fft.ifft(gain, axis=0)[:, :, :half].reshape(sx, modes)
            odd_x = (int(a == 0) + sum(int(d == 0) for d in PAIRS[c])) % 2
            imaginary.append(not odd_x)
            table[a * 6 + c, :, :modes] = line.real if odd_x else line.imag
            if odd_x:
                twist[a * 8 + c, :modes] = line.imag[0]
    ky = np.repeat(np.arange(sy), half)
    kz = np.tile(np.arange(half), sy)
    y = np.repeat(np.arange(2), SZ)
    z = np.tile(np.arange(SZ), 2)
    angle = 2.0 * math.pi * (np.outer(y, ky) / sy + np.outer(z, kz) / SZ)
    forward = np.zeros((128, 2 * LANES))
    forward[:64, :modes] = np.cos(angle)
    forward[:64, LANES : LANES + modes] = -np.sin(angle)
    weight = np.where((kz == 0) | (kz == SZ // 2), 1.0, 2.0) / (sy * SZ)
    backward = np.zeros((2 * LANES, 128))
    backward[:modes, :64] = (weight * np.cos(angle)).T
    backward[LANES : LANES + modes, :64] = (-weight * np.sin(angle)).T
    shift = 2.0 * math.pi * np.outer(2 * np.arange(sy // 2), ky) / sy
    turn = np.zeros((sy // 2, 2, LANES))
    turn[:, 0, :modes] = np.cos(shift)
    turn[:, 1, :modes] = np.sin(shift)
    return (
        forward.astype(np.float32),
        turn.astype(np.float32),
        table.astype(np.float32),
        twist.astype(np.float32),
        backward.astype(np.float32),
        tuple(imaginary),
    )


def solve_kernel(imaginary, blocks, forward, turn, table, twist, backward, out, part, hat, field, ring):
    devices = blocks.shape[0]
    sx = table.shape[1]
    me = lax.axis_index("gy")
    here = lax.axis_index("gx")
    part[...] = jnp.dot(
        blocks[...].reshape(devices * 8, NZ),
        forward[...],
        precision=HIGHEST,
        preferred_element_type=jnp.float32,
    ).reshape(devices, 8, 2 * LANES)
    real = jnp.zeros((8, LANES), jnp.float32)
    imag = jnp.zeros((8, LANES), jnp.float32)
    for d in range(devices):
        owner = lax.rem(me + d, devices)
        value = part[owner]
        re, im = value[:, :LANES], value[:, LANES:]
        cosine, sine = turn[d, 0:1, :], turn[d, 1:2, :]
        real = real + re * cosine + im * sine
        imag = imag + im * cosine - re * sine
    for c in range(6):
        hat[c] = jnp.broadcast_to(real[c : c + 1], (8, LANES))
        hat[6 + c] = jnp.broadcast_to(imag[c : c + 1], (8, LANES))
    alternate = jnp.where(lax.broadcasted_iota(jnp.int32, (8, LANES), 0) % 2 == 0, 1.0, -1.0)
    for a in range(3):
        wave = twist[a * 8 : a * 8 + 8, :]
        first_re = -alternate * jnp.sum(wave * imag, axis=0, keepdims=True)
        first_im = alternate * jnp.sum(wave * real, axis=0, keepdims=True)
        for at in range(0, sx, 8):
            re, im = first_re, first_im
            for c in range(6):
                gain = table[a * 6 + c, at : at + 8, :]
                if imaginary[a * 6 + c]:
                    re = re - gain * hat[6 + c]
                    im = im + gain * hat[c]
                else:
                    re = re + gain * hat[c]
                    im = im + gain * hat[6 + c]
            field[at : at + 8, :LANES] = re
            field[at : at + 8, LANES:] = im
        result = jnp.dot(
            field[...], backward[...], precision=HIGHEST, preferred_element_type=jnp.float32
        )[:, :64]
        lane = (a % 2) * 64
        ring[a // 2, 0:sx, lane : lane + 64] = result
        ring[a // 2, sx : 2 * sx, lane : lane + 64] = result
    ring[1, :, 64:128] = jnp.zeros((2 * sx, 64), jnp.float32)
    for t in range(sx):
        for half in range(2):
            out[t, half : half + 1, :] = ring[half, pl.ds(sx - here + t, 1), :]


def last_kernel(parts, out):
    total = jnp.sum(parts[...], axis=0)
    for a in range(3):
        row = total[a // 2 : a // 2 + 1, :]
        for y in range(2):
            lane = (a % 2) * 64 + y * SZ
            value = pltpu.roll(row, (NZ - lane) % NZ, 1) if lane else row
            out[a, 0, y : y + 1, :] = value[:, :SZ]


def call(body, outs, scratch, cost, limit=32):
    spec = pl.BlockSpec(memory_space=pltpu.VMEM)
    shapes = [jax.ShapeDtypeStruct(s, jnp.float32) for s in outs]
    def run(*args):
        return pl.pallas_call(
            body,
            out_shape=shapes,
            in_specs=[spec] * len(args),
            out_specs=[spec] * len(shapes),
            scratch_shapes=[pltpu.VMEM(s, jnp.float32) for s in scratch],
            compiler_params=pltpu.CompilerParams(vmem_limit_bytes=limit << 20),
            cost_estimate=pl.CostEstimate(flops=cost, bytes_accessed=cost, transcendentals=0),
        )(*args)

    return run


def swap(values, axis):
    count = lax.axis_size(axis)
    near = [(i, i ^ 1) for i in range(count)]
    far = [(i, (i + 1) % count if i % 2 else (i - 1) % count) for i in range(count)]
    second = lax.ppermute(values[1], axis, far)
    first = lax.ppermute(values[0], axis, near)
    return first, second


def local(pops, label, drive):
    nx = lax.axis_size("gx")
    ny = lax.axis_size("gy")
    cells, total, ya, yb = call(
        first_kernel,
        [(CHANNELS, LX, LY, NZ), (6, LY, NZ), (Y_ROWS, NZ), (Y_ROWS, NZ)],
        [(2, Y_ROWS, NZ)],
        2_000_000,
    )(pops, label, drive)
    ya, yb = swap((ya, yb), "gy")
    xa, xb = call(
        second_kernel,
        [(X_ROWS, NZ), (X_ROWS, NZ)],
        [(2, Y_ROWS, NZ), (2, X_ROWS, NZ)],
        2_000_000,
    )(cells, ya, yb)
    xa, xb = swap((xa, xb), "gx")
    post3, spread, ea, eb = call(
        third_kernel,
        [(19, LX, LY, NZ), (ny, 8, NZ), (EDGE_Y_ROWS, NZ), (EDGE_Y_ROWS, NZ)],
        [
            (2, Y_ROWS, NZ),
            (2, X_ROWS, NZ),
            (19, LX + 6, 32, NZ),
            (19, LX + 6, 32, NZ),
            (4, LX + 6, 32, NZ),
            (6, 16, NZ),
            (2, EDGE_Y_ROWS, NZ),
        ],
        20_000_000,
    )(cells, total, ya, yb, xa, xb)
    blocks = lax.all_to_all(spread, "gy", 0, 0, tiled=False)
    ea, eb = swap((ea, eb), "gy")
    fa, fb = call(
        edge_kernel,
        [(EDGE_X_ROWS, NZ), (EDGE_X_ROWS, NZ)],
        [(2, EDGE_Y_ROWS, NZ), (2, EDGE_X_ROWS, NZ)],
        200_000,
    )(post3, ea, eb)
    fa, fb = swap((fa, fb), "gx")
    (momentum,) = call(
        momentum_kernel,
        [(3, LX, LY, NZ)],
        [(2, EDGE_Y_ROWS, NZ), (2, EDGE_X_ROWS, NZ), (19, LX + 2, 24, NZ)],
        1_000_000,
    )(post3, ea, eb, fa, fb)
    forward, turn, table, twist, backward, imaginary = operator_tables(nx, 2 * ny)
    (parts,) = call(
        functools.partial(solve_kernel, imaginary),
        [(nx, 2, NZ)],
        [
            (ny, 8, 2 * LANES),
            (12, 8, LANES),
            (nx, 2 * LANES),
            (2, 2 * nx, NZ),
        ],
        10_000_000,
    )(blocks, forward, turn, table, twist, backward)
    parts = lax.all_to_all(parts, "gx", 0, 0, tiled=False)
    (running,) = call(last_kernel, [(3, 1, 2, SZ)], [], 100_000)(parts)
    return momentum, running


def solution(mesh):
    in_specs = (P(None, "gx", "gy", None), P("gx", "gy", None), P(None, "gx", "gy", None))
    out_specs = (P(None, "gx", "gy", None), P(None, "gx", "gy", None))
    return jax.shard_map(local, mesh=mesh, in_specs=in_specs, out_specs=out_specs, check_vma=False)
```

time: 234 us -> 99.6 us (0.43)
  the two profiles are of different devices: /device:TPU:6 before, /device:TPU:32 now
where the time goes in v1:
time: 99.6 us; the launch traced here: 99 us
  starting transfers between devices  42.9 us (43%)
  waiting for transfers between devices  24.9 us (25%)
  blocking collectives  19.9 us (20%)
  Pallas kernels  6.9 us (7%)
  local copies, waits for them, and re-layouts  3.64 us (4%)
    ppermute x4, waiting for transfers between devices, swap(): second = lax.ppermute(values[1], axis, far)  24.9 us
    ppermute x4, starting transfers between devices, swap(): second = lax.ppermute(values[1], axis, far)  24.8 us
    all_to_all x1, blocking collectives, local(): blocks = lax.all_to_all(spread, 'gy', 0, 0, tiled=False)  19.9 us
    ppermute x4, starting transfers between devices, swap(): first = lax.ppermute(values[0], axis, near)  9.71 us
    all_to_all x1, starting transfers between devices, local(): parts = lax.all_to_all(parts, 'gx', 0, 0, tiled=False)  8.44 us
    pallas_call x7, Pallas kernels, run(): pl.pallas_call(body, out_shape=shapes, in_specs=[spec] * len(args), out_s...  6.9 us
    unnamed x16, local copies, waits for them, and re-layouts  3.64 us
  transfers between devices with their start and end apart: 9, of which 4 were waited for; matrix products, arithmetic and copies ran while one was open for 0% of the time, Pallas kernels for 1%

profile of v1, /device:TPU:32, one launch (start us, length us, event | category | flops | bytes accessed | tf_op | source)
XLA Modules:
  0.0 99.0 jit_solution(2611594377384896473)
XLA Ops:
  0.7 1.1 %copy-done.3 = f32[19,4,8,128]{3,2,1,0:T(8,128)S(1)} copy-done((f32[19,4,8,128]{3,2,1,0:T(8,128)S(1)}, f32[19,4,8,128]{3,2,1,0:T(8,128)}, u32[]{:S(2)}) %copy-start.3) | copy-done | bytes 311320
  1.8 0.8 copy-done.4
  2.6 0.7 copy-done.7
  3.3 0.2 shard_map.95
  3.5 3.4 %collective-permute-start = (f32[208,128]{1,0:T(8,128)S(1)}, f32[208,128]{1,0:T(8,128)S(1)}, u32[]{:S(2)}, u32[]{:S(2)}) collective-permute-start(f32[208,128]{1,0:T(8,128)S(1)} %get-tuple-element.16), channel_id=1, source_target_pairs={{0,1},{1,0},{2,3},{3,2},{4,5},{5,4},{6,7},{7,6},{8,9},{9,8},{10,11... | collective-permute-start | bytes 319496 | tf_op jit(solution)/shard_map/ppermute | solution.py:483
  6.9 12.4 %collective-permute-start.1 = (f32[208,128]{1,0:T(8,128)S(1)}, f32[208,128]{1,0:T(8,128)S(1)}, u32[]{:S(2)}, u32[]{:S(2)}) collective-permute-start(f32[208,128]{1,0:T(8,128)S(1)} %get-tuple-element.17), channel_id=1, source_target_pairs={{0,7},{1,2},{2,1},{3,4},{4,3},{5,6},{6,5},{7,0},{8,15},{9,10},{10,... | collective-permute-start | bytes 319496 | tf_op jit(solution)/shard_map/ppermute | solution.py:482
  19.4 4.1 %collective-permute-done.1.got_b.yb = f32[208,128]{1,0:T(8,128)S(1)} collective-permute-done((f32[208,128]{1,0:T(8,128)S(1)}, f32[208,128]{1,0:T(8,128)S(1)}, u32[]{:S(2)}, u32[]{:S(2)}) %collective-permute-start.1) | collective-permute-done | bytes 106528 | tf_op jit(solution)/shard_map/ppermute | solution.py:482
  23.5 0.2 shard_map.96
  23.7 1.9 %collective-permute-start.2 = (f32[640,128]{1,0:T(8,128)S(1)}, f32[640,128]{1,0:T(8,128)S(1)}, u32[]{:S(2)}, u32[]{:S(2)}) collective-permute-start(f32[640,128]{1,0:T(8,128)S(1)} %get-tuple-element.18), channel_id=1, source_target_pairs={{0,8},{8,0},{16,24},{24,16},{32,40},{40,32},{48,56},{56,48},{64,72... | collective-permute-start | bytes 983048 | tf_op jit(solution)/shard_map/ppermute | solution.py:483
  25.6 3.9 %collective-permute-start.3 = (f32[640,128]{1,0:T(8,128)S(1)}, f32[640,128]{1,0:T(8,128)S(1)}, u32[]{:S(2)}, u32[]{:S(2)}) collective-permute-start(f32[640,128]{1,0:T(8,128)S(1)} %get-tuple-element.19), channel_id=1, source_target_pairs={{0,504},{8,16},{16,8},{24,32},{32,24},{40,48},{48,40},{56,64},{64,... | collective-permute-start | bytes 983048 | tf_op jit(solution)/shard_map/ppermute | solution.py:482
  29.5 8.6 %collective-permute-done.3.xb = f32[640,128]{1,0:T(8,128)S(1)} collective-permute-done((f32[640,128]{1,0:T(8,128)S(1)}, f32[640,128]{1,0:T(8,128)S(1)}, u32[]{:S(2)}, u32[]{:S(2)}) %collective-permute-start.3) | collective-permute-done | bytes 327712 | tf_op jit(solution)/shard_map/ppermute | solution.py:482
  38.1 2.8 %shard_map.97 = (f32[19,4,8,128]{3,2,1,0:T(8,128)S(1)}, f32[8,8,128]{2,1,0:T(8,128)S(1)}, f32[24,128]{1,0:T(8,128)S(1)}, f32[24,128]{1,0:T(8,128)S(1)}) custom-call(f32[23,4,8,128]{3,2,1,0:T(8,128)S(1)} %get-tuple-element.14.cells, f32[6,8,128]{2,1,0:T(8,128)S(1)} %get-tuple-element.15.total, f32[208,128]{1,0:T(8,128)S(1)} %collective-permute-done.got_a.ya, ...), custom_call_target="tpu_custom_call" | custom-call | flops 20000000 | bytes 20000000 | tf_op jit(solution)/shard_map/pallas_call | solution.py:465
  40.9 19.9 %all_to_all.10.blocks = f32[8,8,128]{2,1,0:T(8,128)S(1)} all-to-all(f32[8,8,128]{2,1,0:T(8,128)S(1)} %get-tuple-element.25), channel_id=1, replica_groups=mesh['gx'=64,'gy'=8] {'gy'}, dimensions={0} | all-to-all | bytes 65536 | tf_op jit(solution)/shard_map/all_to_all | solution.py:518
  60.8 1.0 copy-done.2
  61.7 2.3 %shard_map.100 = f32[64,2,128]{2,1,0:T(2,128)} custom-call(f32[8,8,128]{2,1,0:T(8,128)S(1)} %all_to_all.10.blocks, f32[128,768]{1,0:T(8,128)S(1)} %copy-done.2, f32[8,2,384]{2,1,0:T(2,128)S(1)} %copy-done.6, f32[18,64,384]{2,1,0:T(8,128)S(1)} %copy-done, f32[24,384]{1,0:T(8,128)S(1)} %copy-done.5, f32[768,128]{1,0:T(8,128)S(1)} %copy-done.1), custom_call_target="tpu_custom_call" | custom-call | flops 10000000 | bytes 10000000 | tf_op jit(solution)/shard_map/pallas_call | solution.py:465
  64.0 8.4 %all-to-all-start.1 = ((f32[64,2,128]{2,1,0:T(2,128)}), f32[64,2,128]{2,1,0:T(2,128)S(1)}, u32[]{:S(2)}, u32[]{:S(2)}) async-start(f32[64,2,128]{2,1,0:T(2,128)} %shard_map.100), calls=%async_computation.1 | async-start | bytes 131072 | tf_op jit(solution)/shard_map/all_to_all | solution.py:545
  72.5 2.5 %collective-permute-start.4 = (f32[24,128]{1,0:T(8,128)S(1)}, f32[24,128]{1,0:T(8,128)S(1)}, u32[]{:S(2)}, u32[]{:S(2)}) collective-permute-start(f32[24,128]{1,0:T(8,128)S(1)} %get-tuple-element.21), channel_id=1, source_target_pairs={{0,1},{1,0},{2,3},{3,2},{4,5},{5,4},{6,7},{7,6},{8,9},{9,8},{10,11... | collective-permute-start | bytes 36872 | tf_op jit(solution)/shard_map/ppermute | solution.py:483
  75.0 3.1 %collective-permute-start.5 = (f32[24,128]{1,0:T(8,128)S(1)}, f32[24,128]{1,0:T(8,128)S(1)}, u32[]{:S(2)}, u32[]{:S(2)}) collective-permute-start(f32[24,128]{1,0:T(8,128)S(1)} %get-tuple-element.22), channel_id=1, source_target_pairs={{0,7},{1,2},{2,1},{3,4},{4,3},{5,6},{6,5},{7,0},{8,15},{9,10},{10,... | collective-permute-start | bytes 36872 | tf_op jit(solution)/shard_map/ppermute | solution.py:482
  78.1 8.5 %collective-permute-done.5.yb = f32[24,128]{1,0:T(8,128)S(1)} collective-permute-done((f32[24,128]{1,0:T(8,128)S(1)}, f32[24,128]{1,0:T(8,128)S(1)}, u32[]{:S(2)}, u32[]{:S(2)}) %collective-permute-start.5) | collective-permute-done | bytes 12320 | tf_op jit(solution)/shard_map/ppermute | solution.py:482
  86.6 1.9 %collective-permute-start.6 = (f32[40,128]{1,0:T(8,128)S(1)}, f32[40,128]{1,0:T(8,128)S(1)}, u32[]{:S(2)}, u32[]{:S(2)}) collective-permute-start(f32[40,128]{1,0:T(8,128)S(1)} %get-tuple-element.23), channel_id=1, source_target_pairs={{0,8},{8,0},{16,24},{24,16},{32,40},{40,32},{48,56},{56,48},{64,72... | collective-permute-start | bytes 61448 | tf_op jit(solution)/shard_map/ppermute | solution.py:483
  88.5 5.3 %collective-permute-start.7 = (f32[40,128]{1,0:T(8,128)S(1)}, f32[40,128]{1,0:T(8,128)S(1)}, u32[]{:S(2)}, u32[]{:S(2)}) collective-permute-start(f32[40,128]{1,0:T(8,128)S(1)} %get-tuple-element.24), channel_id=1, source_target_pairs={{0,504},{8,16},{16,8},{24,32},{32,24},{40,48},{48,40},{56,64},{64,... | collective-permute-start | bytes 61448 | tf_op jit(solution)/shard_map/ppermute | solution.py:482
  93.8 3.7 %collective-permute-done.7.xb = f32[40,128]{1,0:T(8,128)S(1)} collective-permute-done((f32[40,128]{1,0:T(8,128)S(1)}, f32[40,128]{1,0:T(8,128)S(1)}, u32[]{:S(2)}, u32[]{:S(2)}) %collective-permute-start.7) | collective-permute-done | bytes 20512 | tf_op jit(solution)/shard_map/ppermute | solution.py:482
  97.5 0.7 shard_map.99
  98.3 0.7 shard_map.101
  (18 shorter events, 0.1 us)
Async XLA Ops:
  0.6 60.1 %copy-start.1 = (f32[768,128]{1,0:T(8,128)S(1)}, f32[768,128]{1,0:T(8,128)}, u32[]{:S(2)}) copy-start(f32[768,128]{1,0:T(8,128)} %constant.14.clone.backward) | copy-start | bytes 1179652
  0.6 60.1 %copy-start = (f32[18,64,384]{2,1,0:T(8,128)S(1)}, f32[18,64,384]{2,1,0:T(8,128)}, u32[]{:S(2)}) copy-start(f32[18,64,384]{2,1,0:T(8,128)} %constant.12.clone.table) | copy-start | bytes 5308420
  0.7 1.1 %copy-start.3 = (f32[19,4,8,128]{3,2,1,0:T(8,128)S(1)}, f32[19,4,8,128]{3,2,1,0:T(8,128)}, u32[]{:S(2)}) copy-start(f32[19,4,8,128]{3,2,1,0:T(8,128)} %pops.1) | copy-start | bytes 933892
  1.8 0.8 copy-start.4
  2.6 0.7 copy-start.7
  3.3 57.4 %copy-start.5 = (f32[24,384]{1,0:T(8,128)S(1)}, f32[24,384]{1,0:T(8,128)}, u32[]{:S(2)}) copy-start(f32[24,384]{1,0:T(8,128)} %constant.13.clone.twist) | copy-start | bytes 110596
  3.3 57.4 %copy-start.6 = (f32[8,2,384]{2,1,0:T(2,128)S(1)}, f32[8,2,384]{2,1,0:T(2,128)}, u32[]{:S(2)}) copy-start(f32[8,2,384]{2,1,0:T(2,128)} %constant.11.clone.turn) | copy-start | bytes 73732
  3.5 15.9 %collective-permute-start = (f32[208,128]{1,0:T(8,128)S(1)}, f32[208,128]{1,0:T(8,128)S(1)}, u32[]{:S(2)}, u32[]{:S(2)}) collective-permute-start(f32[208,128]{1,0:T(8,128)S(1)} %get-tuple-element.16), channel_id=1, source_target_pairs={{0,1},{1,0},{2,3},{3,2},{4,5},{5,4},{6,7},{7,6},{8,9},{9,8},{10,11... | collective-permute-start | bytes 319496 | tf_op jit(solution)/shard_map/ppermute | solution.py:483
  6.9 16.6 %collective-permute-start.1 = (f32[208,128]{1,0:T(8,128)S(1)}, f32[208,128]{1,0:T(8,128)S(1)}, u32[]{:S(2)}, u32[]{:S(2)}) collective-permute-start(f32[208,128]{1,0:T(8,128)S(1)} %get-tuple-element.17), channel_id=1, source_target_pairs={{0,7},{1,2},{2,1},{3,4},{4,3},{5,6},{6,5},{7,0},{8,15},{9,10},{10,... | collective-permute-start | bytes 319496 | tf_op jit(solution)/shard_map/ppermute | solution.py:482
  23.7 5.9 %collective-permute-start.2 = (f32[640,128]{1,0:T(8,128)S(1)}, f32[640,128]{1,0:T(8,128)S(1)}, u32[]{:S(2)}, u32[]{:S(2)}) collective-permute-start(f32[640,128]{1,0:T(8,128)S(1)} %get-tuple-element.18), channel_id=1, source_target_pairs={{0,8},{8,0},{16,24},{24,16},{32,40},{40,32},{48,56},{56,48},{64,72... | collective-permute-start | bytes 983048 | tf_op jit(solution)/shard_map/ppermute | solution.py:483
  25.6 12.5 %collective-permute-start.3 = (f32[640,128]{1,0:T(8,128)S(1)}, f32[640,128]{1,0:T(8,128)S(1)}, u32[]{:S(2)}, u32[]{:S(2)}) collective-permute-start(f32[640,128]{1,0:T(8,128)S(1)} %get-tuple-element.19), channel_id=1, source_target_pairs={{0,504},{8,16},{16,8},{24,32},{32,24},{40,48},{48,40},{56,64},{64,... | collective-permute-start | bytes 983048 | tf_op jit(solution)/shard_map/ppermute | solution.py:482
  60.7 1.0 %copy-start.2 = (f32[128,768]{1,0:T(8,128)S(1)}, f32[128,768]{1,0:T(8,128)}, u32[]{:S(2)}) copy-start(f32[128,768]{1,0:T(8,128)} %constant.10.clone.forward) | copy-start | bytes 1179652
  64.0 34.2 %all-to-all-start.1 = ((f32[64,2,128]{2,1,0:T(2,128)}), f32[64,2,128]{2,1,0:T(2,128)S(1)}, u32[]{:S(2)}, u32[]{:S(2)}) async-start(f32[64,2,128]{2,1,0:T(2,128)} %shard_map.100), calls=%async_computation.1 | async-start | bytes 131072 | tf_op jit(solution)/shard_map/all_to_all | solution.py:545
  72.5 5.6 %collective-permute-start.4 = (f32[24,128]{1,0:T(8,128)S(1)}, f32[24,128]{1,0:T(8,128)S(1)}, u32[]{:S(2)}, u32[]{:S(2)}) collective-permute-start(f32[24,128]{1,0:T(8,128)S(1)} %get-tuple-element.21), channel_id=1, source_target_pairs={{0,1},{1,0},{2,3},{3,2},{4,5},{5,4},{6,7},{7,6},{8,9},{9,8},{10,11... | collective-permute-start | bytes 36872 | tf_op jit(solution)/shard_map/ppermute | solution.py:483
  75.0 11.6 %collective-permute-start.5 = (f32[24,128]{1,0:T(8,128)S(1)}, f32[24,128]{1,0:T(8,128)S(1)}, u32[]{:S(2)}, u32[]{:S(2)}) collective-permute-start(f32[24,128]{1,0:T(8,128)S(1)} %get-tuple-element.22), channel_id=1, source_target_pairs={{0,7},{1,2},{2,1},{3,4},{4,3},{5,6},{6,5},{7,0},{8,15},{9,10},{10,... | collective-permute-start | bytes 36872 | tf_op jit(solution)/shard_map/ppermute | solution.py:482
  86.6 7.2 %collective-permute-start.6 = (f32[40,128]{1,0:T(8,128)S(1)}, f32[40,128]{1,0:T(8,128)S(1)}, u32[]{:S(2)}, u32[]{:S(2)}) collective-permute-start(f32[40,128]{1,0:T(8,128)S(1)} %get-tuple-element.23), channel_id=1, source_target_pairs={{0,8},{8,0},{16,24},{24,16},{32,40},{40,32},{48,56},{56,48},{64,72... | collective-permute-start | bytes 61448 | tf_op jit(solution)/shard_map/ppermute | solution.py:483
  88.5 9.0 %collective-permute-start.7 = (f32[40,128]{1,0:T(8,128)S(1)}, f32[40,128]{1,0:T(8,128)S(1)}, u32[]{:S(2)}, u32[]{:S(2)}) collective-permute-start(f32[40,128]{1,0:T(8,128)S(1)} %get-tuple-element.24), channel_id=1, source_target_pairs={{0,504},{8,16},{16,8},{24,32},{32,24},{40,48},{48,40},{56,64},{64,... | collective-permute-start | bytes 61448 | tf_op jit(solution)/shard_map/ppermute | solution.py:482

commit v2 on v1

v2 whole, which is shorter than its diff:
```python
import functools
import math

import jax
import jax.numpy as jnp
import numpy as np
from jax import lax
from jax.experimental import pallas as pl
from jax.experimental.pallas import tpu as pltpu
from jax.sharding import PartitionSpec as P

NZ = 128
STEPS = 4
SZ = 32
LX = 4
LY = 8
VELOCITY = [
    [0, 0, 0],
    [1, 0, 0],
    [-1, 0, 0],
    [0, 1, 0],
    [0, -1, 0],
    [0, 0, 1],
    [0, 0, -1],
    [1, 1, 0],
    [-1, -1, 0],
    [1, -1, 0],
    [-1, 1, 0],
    [1, 0, 1],
    [-1, 0, -1],
    [1, 0, -1],
    [-1, 0, 1],
    [0, 1, 1],
    [0, -1, -1],
    [0, 1, -1],
    [0, -1, 1],
]
OPPOSITE = [0, 2, 1, 4, 3, 6, 5, 8, 7, 10, 9, 12, 11, 14, 13, 16, 15, 18, 17]
WEIGHTS = [1.0 / 3.0] + [1.0 / 18.0] * 6 + [1.0 / 36.0] * 12
PAIRS = [(0, 0), (1, 1), (2, 2), (0, 1), (0, 2), (1, 2)]
COMPONENT = [[0, 3, 4], [3, 1, 5], [4, 5, 2]]
SLOW_VISCOSITY = 0.0004
PHASES = [math.cos(2.0 * math.pi * (step + 0.5) / STEPS) for step in range(STEPS)]

CHANNELS = 23
CX = [v[0] for v in VELOCITY] + [0] * 4
CY = [v[1] for v in VELOCITY] + [0] * 4
HIGHEST = lax.Precision.HIGHEST
GX = ("cy", "zl", "core")
GY = ("zh", "cx")
GROUP = 8


REACH = STEPS - 1


def pack_y(sign):
    out, at = [], 0
    for x in range(LX):
        for ch in range(CHANNELS):
            n = REACH + sign * CY[ch]
            out.append((ch, x, LY - n if sign > 0 else 0, n, at))
            at += n
    return out, -(-at // 8) * 8


def pack_x(sign):
    out, at = [], 0
    for ch in range(CHANNELS):
        n = REACH + sign * CX[ch]
        for x in range(LX - n, LX) if sign > 0 else range(n):
            out.append((ch, x, REACH + CY[ch], REACH - CY[ch], at))
            at += 2 * REACH + LY
    return out, -(-at // 8) * 8


Y_UP, Y_ROWS = pack_y(1)
Y_DOWN, _ = pack_y(-1)
X_RIGHT, X_ROWS = pack_x(1)
X_LEFT, _ = pack_x(-1)
Y_UP_AT = {(ch, x): (n, at) for ch, x, _, n, at in Y_UP}
Y_DOWN_AT = {(ch, x): (n, at) for ch, x, _, n, at in Y_DOWN}


def collide(f, label, drive, phase):
    rho = f[0]
    for i in range(1, 19):
        rho = rho + f[i]
    j = []
    for axis in range(3):
        total = None
        for i in range(1, 19, 2):
            c = VELOCITY[i][axis]
            if c == 0:
                continue
            term = f[i] - f[i + 1] if c > 0 else f[i + 1] - f[i]
            total = term if total is None else total + term
        j.append(total)
    second = label == 1.0
    solid = label == 2.0
    omega = jnp.where(second, 1.1, 1.6)
    keep = 1.0 - omega
    strength = jnp.where(second, 0.6 * phase, phase)
    inverse = 1.0 / rho
    mix = [omega * j[axis] + strength * drive[axis] for axis in range(3)]
    base = omega * (rho - 1.5 * (j[0] * j[0] + j[1] * j[1] + j[2] * j[2]) * inverse)
    curve = 4.5 * omega * inverse

    def along(vector, c):
        total = None
        for axis in range(3):
            if c[axis] == 0:
                continue
            if total is None:
                total = vector[axis] if c[axis] > 0 else -vector[axis]
            else:
                total = total + vector[axis] if c[axis] > 0 else total - vector[axis]
        return total

    post = [None] * 19
    post[0] = jnp.where(solid, f[0], keep * f[0] + WEIGHTS[0] * base)
    for i in range(1, 19, 2):
        w = WEIGHTS[i]
        cj = along(j, VELOCITY[i])
        even = w * (base + curve * (cj * cj))
        odd = (3.0 * w) * along(mix, VELOCITY[i])
        post[i] = jnp.where(solid, f[i + 1], keep * f[i] + (even + odd))
        post[i + 1] = jnp.where(solid, f[i], keep * f[i + 1] + (even - odd))
    fluid = jnp.where(solid, 0.0, inverse)
    stress = [j[a] * j[b] * fluid for a, b in PAIRS]
    return post, stress


def first_kernel(pops_in, label_in, drive_in, cells, total, far, near, box, pops, label, drive, sems):
    copies = [
        pltpu.make_async_copy(source, target, sems.at[k])
        for k, (source, target) in enumerate(((pops_in, pops), (label_in, label), (drive_in, drive)))
    ]
    for copy in copies:
        copy.start()
    for copy in copies:
        copy.wait()
    up = lax.rem(lax.axis_index(GY), 2)
    down = 1 - up
    sums = [jnp.zeros((LY, NZ), jnp.float32)] * 6
    for x in range(LX):
        f = [pops[i, x] for i in range(19)]
        lab = label[x].astype(jnp.float32)
        force = [drive[axis, x] for axis in range(3)]
        post, stress = collide(f, lab, force, PHASES[0])
        for i in range(19):
            cells[i, x] = post[i]
        cells[19, x] = lab
        for axis in range(3):
            cells[20 + axis, x] = force[axis]
        sums = [sums[k] + stress[k] for k in range(6)]
    for k in range(6):
        total[k] = sums[k]
    for ch, x, row, n, at in Y_UP:
        box[up, at : at + n, :] = cells[ch, x, row : row + n, :]
    for ch, x, row, n, at in Y_DOWN:
        box[down, at : at + n, :] = cells[ch, x, row : row + n, :]
    near[...] = box[0]
    far[...] = box[1]


def second_kernel(cells, got_far, got_near, far, near, rows, box):
    odd_y = lax.rem(lax.axis_index(GY), 2)
    low_slot, high_slot = 1 - odd_y, odd_y
    right = lax.rem(lax.axis_index(GX), 2)
    rows[0] = got_near[...]
    rows[1] = got_far[...]
    for slot, entries in ((right, X_RIGHT), (1 - right, X_LEFT)):
        for ch, x, low, high, at in entries:
            n, source = Y_UP_AT[ch, x]
            box[slot, at : at + n, :] = rows[low_slot, source : source + n, :]
            box[slot, at + low : at + low + LY, :] = cells[ch, x]
            n, source = Y_DOWN_AT[ch, x]
            box[slot, at + low + LY : at + low + LY + n, :] = rows[high_slot, source : source + n, :]
    near[...] = box[0]
    far[...] = box[1]


ROW0 = 12
COL0 = 4
WORK_ROWS = 32
WORK_COLS = LX + 8
STATE_ROW0 = 8
STATE_COL0 = 2
STATE_ROWS = 24
STATE_COLS = LX + 4


def arrive(source, x, row, n):
    f = []
    for i in range(19):
        cx, cy, cz = VELOCITY[i]
        value = source[i, x - cx, row - cy : row - cy + n, :]
        f.append(pltpu.roll(value, cz % NZ, 1) if cz else value)
    return f


def around(aux, x, row, n):
    return aux[0, x, row : row + n, :], [aux[1 + axis, x, row : row + n, :] for axis in range(3)]


def third_kernel(
    cells, total, y_far, y_near, x_far, x_near, state, aux, spread, rows, cols, one, mid, sums, two, sem
):
    odd_y = lax.rem(lax.axis_index(GY), 2)
    odd_x = lax.rem(lax.axis_index(GX), 2)
    low_slot, high_slot = 1 - odd_y, odd_y
    left_slot, right_slot = 1 - odd_x, odd_x
    rows[0] = y_near[...]
    rows[1] = y_far[...]
    cols[0] = x_near[...]
    cols[1] = x_far[...]

    def place(ch, x, row, values):
        n = values.shape[0]
        if ch < 19:
            one[ch, x + COL0, row + ROW0 : row + ROW0 + n, :] = values
        else:
            aux[ch - 19, x + COL0, row + ROW0 : row + ROW0 + n, :] = values

    for ch in range(CHANNELS):
        for x in range(LX):
            place(ch, x, 0, cells[ch, x])
    for ch, x, row, n, at in Y_UP:
        place(ch, x, row - LY, rows[low_slot, at : at + n, :])
    for ch, x, row, n, at in Y_DOWN:
        place(ch, x, row + LY, rows[high_slot, at : at + n, :])
    for ch, x, low, high, at in X_RIGHT:
        place(ch, x - LX, -low, cols[left_slot, at : at + low + LY + high, :])
    for ch, x, low, high, at in X_LEFT:
        place(ch, x + LX, -low, cols[right_slot, at : at + low + LY + high, :])

    wide = 16
    start = ROW0 - 4
    sums[...] = jnp.zeros(sums.shape, jnp.float32)
    for step, source, target, back, to in ((1, one, mid, 0, start), (2, mid, two, 2, STATE_ROW0 - 4)):

        def layer(x, carry, step=step, source=source, target=target, back=back, to=to):
            f = arrive(source, x, start, wide)
            lab, force = around(aux, x, start, wide)
            post, stress = collide(f, lab, force, PHASES[step])
            for i in range(19):
                target[i, x - back, to : to + wide, :] = post[i]
            own = jnp.logical_and(x >= COL0, x < COL0 + LX)
            for k in range(6):
                sums[k] += jnp.where(own, stress[k], 0.0)
            return carry

        lax.fori_loop(COL0 + step - STEPS, COL0 + LX + STEPS - step, layer, 0)
    save = pltpu.make_async_copy(two, state, sem)
    save.start()
    last = [total[k] + sums[k, 4:12, :] for k in range(6)]
    for x in range(LX):
        f = arrive(two, x + STATE_COL0, STATE_ROW0, LY)
        lab, force = around(aux, x + COL0, ROW0, LY)
        _, stress = collide(f, lab, force, PHASES[3])
        last = [last[k] + stress[k] for k in range(6)]
    stacked = jnp.concatenate(last, axis=0)
    r = lax.broadcasted_iota(jnp.int32, (16, 48), 0)
    c = lax.broadcasted_iota(jnp.int32, (16, 48), 1)
    chosen = jnp.logical_and((r & 7) == (c >> 3), (r >> 3) == ((c & 7) >> 2))
    left = jnp.where(chosen, 1.0, 0.0)
    halves = jnp.dot(left, stacked, precision=HIGHEST, preferred_element_type=jnp.float32)
    z = lax.broadcasted_iota(jnp.int32, (NZ, NZ), 0)
    lane = lax.broadcasted_iota(jnp.int32, (NZ, NZ), 1)
    mean = 1.0 / (STEPS * 64)
    slow = jnp.zeros((8, NZ), jnp.float32)
    for half in range(2):
        table = jnp.where(lane == (z >> 2) + half * SZ, mean, 0.0)
        slow = slow + jnp.dot(
            halves[half * 8 : half * 8 + 8],
            table,
            precision=HIGHEST,
            preferred_element_type=jnp.float32,
        )
    for d in range(spread.shape[0]):
        spread[d] = slow
    save.wait()


def momentum_kernel(state, aux, out, work):
    wide = 16

    def layer(x, carry):
        f = arrive(state, x, STATE_ROW0 - 4, wide)
        lab, force = around(aux, x + (COL0 - STATE_COL0), ROW0 - 4, wide)
        post, _ = collide(f, lab, force, PHASES[3])
        for i in range(1, 19):
            work[i, x, STATE_ROW0 - 4 : STATE_ROW0 - 4 + wide, :] = post[i]
        return carry

    lax.fori_loop(STATE_COL0 - 1, STATE_COL0 + LX + 1, layer, 0)
    for x in range(LX):
        f = arrive(work, x + STATE_COL0, STATE_ROW0, LY)
        for axis in range(3):
            total = None
            for i in range(1, 19, 2):
                c = VELOCITY[i][axis]
                if c == 0:
                    continue
                term = f[i] - f[i + 1] if c > 0 else f[i + 1] - f[i]
                total = term if total is None else total + term
            out[axis, x] = total


TILES = 3


@functools.cache
def operator_table(sx, sy):
    waves = [2.0 * math.pi * np.fft.fftfreq(n) for n in (sx, sy, SZ)]
    k = np.meshgrid(*waves, indexing="ij")
    square = k[0] ** 2 + k[1] ** 2 + k[2] ** 2
    positive = square > 0
    safe = np.where(positive, square, 1.0)
    half = SZ // 2 + 1
    modes = sy * half
    lanes = TILES * NZ
    ky = np.repeat(np.arange(sy), half)
    kz = np.tile(np.arange(half), sy)
    weight = np.where((kz == 0) | (kz == SZ // 2), 1.0, 2.0) / (sy * SZ)
    gains = np.zeros((3, 6, sx, lanes))
    twists = np.zeros((3, 8, lanes))
    imaginary = []
    for a in range(3):
        for c in range(6):
            force = [
                -1j * sum(k[b] for b in range(3) if COMPONENT[first][b] == c) + 0.0 * k[0]
                for first in range(3)
            ]
            inner = k[0] * force[0] + k[1] * force[1] + k[2] * force[2]
            gain = np.where(positive, (force[a] - k[a] * inner / safe) / (SLOW_VISCOSITY * safe), 0.0)
            flipped = gain
            for axis in range(3):
                flipped = np.roll(np.flip(flipped, axis), 1, axis)
            gain = 0.5 * (gain + np.conj(flipped))
            line = weight * np.fft.ifft(gain, axis=0)[:, :, :half].reshape(sx, modes)
            odd_x = (int(a == 0) + sum(int(d == 0) for d in PAIRS[c])) % 2
            imaginary.append(not odd_x)
            gains[a, c, :, :modes] = line.real if odd_x else line.imag
            if odd_x:
                twists[a, c, :modes] = line.imag[0]
    gains = np.concatenate([gains, gains[:, :, :GROUP]], axis=2)
    gains = gains.reshape(3, 6, sx + GROUP, TILES, NZ).transpose(0, 1, 3, 2, 4)
    twists = twists.reshape(3, 8, TILES, NZ).transpose(0, 2, 1, 3)
    y = np.repeat(np.arange(2), SZ)
    z = np.tile(np.arange(SZ), 2)
    angle = 2.0 * math.pi * (np.outer(y, ky) / sy + np.outer(z, kz) / SZ)
    forward = np.zeros((2, NZ, lanes))
    forward[0, :64, :modes] = np.cos(angle)
    forward[1, :64, :modes] = -np.sin(angle)
    forward = forward.reshape(2, NZ, TILES, NZ).transpose(0, 2, 1, 3)
    shift = 2.0 * math.pi * np.outer(2 * np.arange(sy // 2), ky) / sy
    turns = np.zeros((sy // 2, 2, lanes))
    turns[:, 0, :modes] = np.cos(shift)
    turns[:, 1, :modes] = np.sin(shift)
    turns = np.concatenate([turns.reshape(-1, NZ), np.zeros((-turns.size // NZ % 8, NZ))])
    sections = [gains.reshape(-1, NZ), twists.reshape(-1, NZ), turns, forward.reshape(-1, NZ)]
    starts = np.cumsum([0] + [len(section) for section in sections])
    table = np.concatenate(sections).astype(np.float32)
    return table, tuple(int(start) for start in starts[:4]), tuple(imaginary)


def solve_kernel(starts, imaginary, pairs, blocks, table, out, part, field):
    groups = blocks.shape[0]
    sx = groups * GROUP
    at_gain, at_twist, at_turn, at_forward = starts
    me = lax.axis_index("cy")
    mine = lax.rem(lax.axis_index(GX), GROUP)
    pair = lax.axis_index(GY)
    forward = jnp.concatenate(
        [table[at_forward + k * NZ : at_forward + (k + 1) * NZ, :] for k in range(2 * TILES)], axis=1
    )
    part[...] = jnp.dot(
        blocks[...].reshape(groups * 8, NZ),
        forward,
        precision=HIGHEST,
        preferred_element_type=jnp.float32,
    ).reshape(groups, 8, 2 * TILES * NZ)

    row = lax.broadcasted_iota(jnp.int32, (GROUP, NZ), 0)
    alternate = jnp.where(lax.rem(row + mine, 2) == 0, 1.0, -1.0)
    starts_x = [lax.rem(GROUP * (me + groups - g) + sx - mine, sx) for g in range(groups)]
    for k in range(TILES):
        re_lanes = slice(k * NZ, (k + 1) * NZ)
        im_lanes = slice((TILES + k) * NZ, (TILES + k + 1) * NZ)
        all_re = part[0, :, re_lanes]
        all_im = part[0, :, im_lanes]
        for g in range(1, groups):
            all_re = all_re + part[g, :, re_lanes]
            all_im = all_im + part[g, :, im_lanes]
        re, im = [], []
        for a in range(3):
            at = at_twist + (a * TILES + k) * 8
            wave = table[at : at + 8, :]
            re.append(-alternate * jnp.sum(wave * all_im, axis=0, keepdims=True))
            im.append(alternate * jnp.sum(wave * all_re, axis=0, keepdims=True))
        for g in range(groups):
            for c in range(6):
                hat_re = jnp.broadcast_to(part[g, c : c + 1, re_lanes], (GROUP, NZ))
                hat_im = jnp.broadcast_to(part[g, c : c + 1, im_lanes], (GROUP, NZ))
                for a in range(3):
                    at = at_gain + ((a * 6 + c) * TILES + k) * (sx + GROUP)
                    gain = table[pl.ds(at + starts_x[g], GROUP), :]
                    if imaginary[a * 6 + c]:
                        re[a] = re[a] - gain * hat_im
                        im[a] = im[a] + gain * hat_re
                    else:
                        re[a] = re[a] + gain * hat_re
                        im[a] = im[a] + gain * hat_im
        for j in range(pairs):
            d = lax.rem(pairs + j - pair, pairs)
            cosine = table[pl.ds(at_turn + k + d * (2 * TILES), 1), :]
            sine = table[pl.ds(at_turn + TILES + k + d * (2 * TILES), 1), :]
            for a in range(3):
                at = (a * pairs + j) * GROUP
                field[at : at + GROUP, re_lanes] = re[a] * cosine - im[a] * sine
                field[at : at + GROUP, im_lanes] = re[a] * sine + im[a] * cosine
    result = lax.dot_general(
        field[...],
        forward,
        (((1,), (1,)), ((), ())),
        precision=HIGHEST,
        preferred_element_type=jnp.float32,
    )
    for j in range(pairs):
        first, second, third = [
            result[(a * pairs + j) * GROUP : (a * pairs + j + 1) * GROUP] for a in range(3)
        ]
        both = first + pltpu.roll(second, 64, 1)
        for r in range(GROUP):
            out[r * pairs + j, 0:1, :] = both[r : r + 1]
            out[r * pairs + j, 1:2, :] = third[r : r + 1]


def last_kernel(parts, out):
    total = jnp.sum(parts[...], axis=0)
    for a in range(3):
        row = total[a // 2 : a // 2 + 1, :]
        for y in range(2):
            lane = (a % 2) * 64 + y * SZ
            value = pltpu.roll(row, (NZ - lane) % NZ, 1) if lane else row
            out[a, 0, y : y + 1, :] = value[:, :SZ]


def call(body, outs, scratch, cost, limit=16, place=pltpu.VMEM, more=(), far=0):
    shapes = [
        pltpu.HBM(s, jnp.float32) if k < far else jax.ShapeDtypeStruct(s, jnp.float32) for k, s in enumerate(outs)
    ]

    def run(*args):
        return pl.pallas_call(
            body,
            out_shape=shapes,
            in_specs=[pl.BlockSpec(memory_space=place)] * len(args),
            out_specs=[
                pl.BlockSpec(memory_space=pltpu.HBM if k < far else pltpu.VMEM) for k in range(len(shapes))
            ],
            scratch_shapes=[pltpu.VMEM(s, jnp.float32) for s in scratch] + list(more),
            compiler_params=pltpu.CompilerParams(vmem_limit_bytes=limit << 20),
            cost_estimate=pl.CostEstimate(flops=cost, bytes_accessed=cost, transcendentals=0),
        )(*args)

    return run


def swap(far, near, axis):
    count = lax.axis_size(axis)
    near_pairs = [(i, i ^ 1) for i in range(count)]
    far_pairs = [(i, (i + 1) % count if i % 2 else (i - 1) % count) for i in range(count)]
    return lax.ppermute(far, axis, far_pairs), lax.ppermute(near, axis, near_pairs)


def local(pops, label, drive):
    nx = lax.axis_size(GX)
    ny = lax.axis_size(GY)
    groups = lax.axis_size("cy")
    cells, total, far, near = call(
        first_kernel,
        [(CHANNELS, LX, LY, NZ), (6, LY, NZ), (Y_ROWS, NZ), (Y_ROWS, NZ)],
        [(2, Y_ROWS, NZ), pops.shape],
        2_000_000,
        place=pltpu.HBM,
        more=[
            pltpu.VMEM(label.shape, jnp.int32),
            pltpu.VMEM(drive.shape, jnp.float32),
            pltpu.SemaphoreType.DMA((3,)),
        ],
    )(*[pltpu.with_memory_space_constraint(value, pltpu.HBM) for value in (pops, label, drive)])
    y_far, y_near = swap(far, near, GY)
    far, near = call(
        second_kernel,
        [(X_ROWS, NZ), (X_ROWS, NZ)],
        [(2, Y_ROWS, NZ), (2, X_ROWS, NZ)],
        2_000_000,
    )(cells, y_far, y_near)
    x_far, x_near = swap(far, near, GX)
    state, aux, spread = call(
        third_kernel,
        [(19, STATE_COLS, STATE_ROWS, NZ), (4, WORK_COLS, WORK_ROWS, NZ), (groups, 8, NZ)],
        [
            (2, Y_ROWS, NZ),
            (2, X_ROWS, NZ),
            (19, WORK_COLS, WORK_ROWS, NZ),
            (19, WORK_COLS, WORK_ROWS, NZ),
            (6, 16, NZ),
            (19, STATE_COLS, STATE_ROWS, NZ),
        ],
        20_000_000,
        more=[pltpu.SemaphoreType.DMA(())],
        far=1,
    )(cells, total, y_far, y_near, x_far, x_near)
    blocks = lax.all_to_all(spread, "cy", 0, 0, tiled=False)
    (momentum,) = call(
        momentum_kernel,
        [(3, LX, LY, NZ)],
        [(19, STATE_COLS, STATE_ROWS, NZ)],
        10_000_000,
    )(state, aux)
    blocks, momentum = lax.optimization_barrier((blocks, momentum))
    table, starts, imaginary = operator_table(nx, 2 * ny)
    (parts,) = call(
        functools.partial(solve_kernel, starts, imaginary, ny),
        [(GROUP * ny, 2, NZ)],
        [(groups, 8, 2 * TILES * NZ), (3 * ny * GROUP, 2 * TILES * NZ)],
        10_000_000,
    )(blocks, table)
    parts = lax.all_to_all(parts, ("zl", "core", "zh", "cx"), 0, 0, tiled=False)
    (running,) = call(last_kernel, [(3, 1, 2, SZ)], [], 100_000)(parts)
    return momentum, running


def solution(mesh):
    nx, ny = mesh.devices.shape
    devices = mesh.devices.reshape(nx // GROUP, 4, 2, 2, ny // 2)
    mesh = jax.sharding.Mesh(devices, GX + GY)
    in_specs = (P(None, GX, GY, None), P(GX, GY, None), P(None, GX, GY, None))
    out_specs = (P(None, GX, GY, None), P(None, GX, GY, None))
    return jax.shard_map(local, mesh=mesh, in_specs=in_specs, out_specs=out_specs, check_vma=False)
```

time: 99.6 us -> 79.6 us (0.80)
  the two profiles are of different devices: /device:TPU:32 before, /device:TPU:1 now
where the time goes in v2:
time: 79.6 us; the launch traced here: 79.3 us
  starting transfers between devices  32.7 us (41%)
  blocking collectives  19.6 us (25%)
  waiting for transfers between devices  14.8 us (19%)
  Pallas kernels  9.97 us (13%)
  local copies, waits for them, and re-layouts  1.51 us (2%)
    all_to_all x1, blocking collectives, local(): parts = lax.all_to_all(parts, ('zl', 'core', 'zh', 'cx'), 0, 0, tiled=False)  19.6 us
    ppermute x2, starting transfers between devices, swap(): lax.ppermute(far, axis, far_pairs)  18.6 us
    ppermute x2, waiting for transfers between devices, swap(): lax.ppermute(far, axis, far_pairs)  10.3 us
    pallas_call x6, Pallas kernels, run(): pl.pallas_call(body, out_shape=shapes, in_specs=[pl.BlockSpec(memory_spac...  9.97 us
    ppermute x2, starting transfers between devices, swap(): lax.ppermute(near, axis, near_pairs)  7.2 us
    all_to_all x1, starting transfers between devices, local(): blocks = lax.all_to_all(spread, 'cy', 0, 0, tiled=False)  6.83 us
    all_to_all x1, waiting for transfers between devices, local(): blocks = lax.all_to_all(spread, 'cy', 0, 0, tiled=False)  3.96 us
  transfers between devices with their start and end apart: 5, of which 4 were waited for; matrix products, arithmetic and copies ran while one was open for 0% of the time, Pallas kernels for 2%

profile of v2, /device:TPU:1, one launch (start us, length us, event | category | flops | bytes accessed | tf_op | source)
XLA Modules:
  0.0 79.3 jit_solution(6749481985631335530)
XLA Ops:
  0.6 1.2 %shard_map.59 = (f32[23,4,8,128]{3,2,1,0:T(8,128)S(1)}, f32[6,8,128]{2,1,0:T(8,128)S(1)}, f32[280,128]{1,0:T(8,128)S(1)}, f32[280,128]{1,0:T(8,128)S(1)}) custom-call(f32[19,4,8,128]{3,2,1,0:T(8,128)} %pops_in.1, s32[4,8,128]{2,1,0:T(8,128)} %label_in.1, f32[3,4,8,128]{3,2,1,0:T(8,128)} %drive_in.1), custom_call_target="tpu_custom_call" | custom-call | flops 2000000 | bytes 2000000 | tf_op jit(solution)/shard_map/pallas_call | solution.py:457
  1.9 13.7 %collective-permute-start = (f32[280,128]{1,0:T(8,128)S(1)}, f32[280,128]{1,0:T(8,128)S(1)}, u32[]{:S(2)}, u32[]{:S(2)}) collective-permute-start(f32[280,128]{1,0:T(8,128)S(1)} %get-tuple-element.15), channel_id=1, source_target_pairs={{0,7},{1,2},{2,1},{3,4},{4,3},{5,6},{6,5},{7,0},{8,15},{9,10},{10,... | collective-permute-start | bytes 430088 | tf_op jit(solution)/shard_map/ppermute | solution.py:476
  15.5 1.9 %collective-permute-start.1 = (f32[280,128]{1,0:T(8,128)S(1)}, f32[280,128]{1,0:T(8,128)S(1)}, u32[]{:S(2)}, u32[]{:S(2)}) collective-permute-start(f32[280,128]{1,0:T(8,128)S(1)} %get-tuple-element.16), channel_id=1, source_target_pairs={{0,1},{1,0},{2,3},{3,2},{4,5},{5,4},{6,7},{7,6},{8,9},{9,8},{10,11... | collective-permute-start | bytes 430088 | tf_op jit(solution)/shard_map/ppermute | solution.py:476
  17.5 3.8 %collective-permute-done.got_far.y_far = f32[280,128]{1,0:T(8,128)S(1)} collective-permute-done((f32[280,128]{1,0:T(8,128)S(1)}, f32[280,128]{1,0:T(8,128)S(1)}, u32[]{:S(2)}, u32[]{:S(2)}) %collective-permute-start) | collective-permute-done | bytes 143392 | tf_op jit(solution)/shard_map/ppermute | solution.py:476
  21.3 0.5 collective-permute-done.1.got_near.y_near
  21.7 0.0 copy-start
  21.8 0.2 shard_map.60
  22.0 5.0 %collective-permute-start.2 = (f32[968,128]{1,0:T(8,128)S(1)}, f32[968,128]{1,0:T(8,128)S(1)}, u32[]{:S(2)}, u32[]{:S(2)}) collective-permute-start(f32[968,128]{1,0:T(8,128)S(1)} %get-tuple-element.17), channel_id=1, source_target_pairs={{0,504},{8,16},{16,8},{24,32},{32,24},{40,48},{48,40},{56,64},{64,... | collective-permute-start | bytes 1486856 | tf_op jit(solution)/shard_map/ppermute | solution.py:476
  27.0 5.3 %collective-permute-start.3 = (f32[968,128]{1,0:T(8,128)S(1)}, f32[968,128]{1,0:T(8,128)S(1)}, u32[]{:S(2)}, u32[]{:S(2)}) collective-permute-start(f32[968,128]{1,0:T(8,128)S(1)} %get-tuple-element.18), channel_id=1, source_target_pairs={{0,8},{8,0},{16,24},{24,16},{32,40},{40,32},{48,56},{56,48},{64,72... | collective-permute-start | bytes 1486856 | tf_op jit(solution)/shard_map/ppermute | solution.py:476
  32.3 6.6 %collective-permute-done.2.x_far = f32[968,128]{1,0:T(8,128)S(1)} collective-permute-done((f32[968,128]{1,0:T(8,128)S(1)}, f32[968,128]{1,0:T(8,128)S(1)}, u32[]{:S(2)}, u32[]{:S(2)}) %collective-permute-start.2) | collective-permute-done | bytes 495648 | tf_op jit(solution)/shard_map/ppermute | solution.py:476
  38.8 0.0 collective-permute-done.3.x_near
  38.8 4.8 %shard_map.61 = (f32[19,8,24,128]{3,2,1,0:T(8,128)}, f32[4,12,32,128]{3,2,1,0:T(8,128)S(1)}, f32[8,8,128]{2,1,0:T(8,128)}) custom-call(f32[23,4,8,128]{3,2,1,0:T(8,128)S(1)} %get-tuple-element.13.cells, f32[6,8,128]{2,1,0:T(8,128)S(1)} %get-tuple-element.14.total, f32[280,128]{1,0:T(8,128)S(1)} %collective-permute-done.got_far.y_far, ...), custom_call_target="tpu_custom_call" | custom-call | flops 20000000 | bytes 20000000 | tf_op jit(solution)/shard_map/pallas_call | solution.py:457
  43.6 6.8 %all-to-all-start = ((f32[8,8,128]{2,1,0:T(8,128)}), f32[8,8,128]{2,1,0:T(8,128)S(1)}, u32[]{:S(2)}, u32[]{:S(2)}) async-start(f32[8,8,128]{2,1,0:T(8,128)} %get-tuple-element.19), calls=%async_computation | async-start | bytes 65536 | tf_op jit(solution)/shard_map/all_to_all | solution.py:518
  50.5 0.0 copy-start.1
  50.5 1.5 %copy-done.1 = f32[19,8,24,128]{3,2,1,0:T(8,128)S(1)} copy-done((f32[19,8,24,128]{3,2,1,0:T(8,128)S(1)}, f32[19,8,24,128]{3,2,1,0:T(8,128)}, u32[]{:S(2)}) %copy-start.1) | copy-done | bytes 1867800
  52.0 1.5 %shard_map.62 = f32[3,4,8,128]{3,2,1,0:T(8,128)} custom-call(f32[19,8,24,128]{3,2,1,0:T(8,128)S(1)} %copy-done.1, f32[4,12,32,128]{3,2,1,0:T(8,128)S(1)} %get-tuple-element.21.aux), custom_call_target="tpu_custom_call" | custom-call | flops 10000000 | bytes 10000000 | tf_op jit(solution)/shard_map/pallas_call | solution.py:457
  53.5 4.0 %all-to-all-done.blocks = f32[8,8,128]{2,1,0:T(8,128)S(1)} async-done(((f32[8,8,128]{2,1,0:T(8,128)}), f32[8,8,128]{2,1,0:T(8,128)S(1)}, u32[]{:S(2)}, u32[]{:S(2)}) %all-to-all-start) | async-done | bytes 32800 | tf_op jit(solution)/shard_map/all_to_all | solution.py:518
  57.5 0.0 copy-done
  57.5 1.5 %shard_map.63 = f32[64,2,128]{2,1,0:T(2,128)S(1)} custom-call(f32[8,8,128]{2,1,0:T(8,128)S(1)} %all-to-all-done.blocks, f32[4776,128]{1,0:T(8,128)S(1)} %copy-done), custom_call_target="tpu_custom_call" | custom-call | flops 10000000 | bytes 10000000 | tf_op jit(solution)/shard_map/pallas_call | solution.py:457
  58.9 19.6 %all_to_all.10.parts = f32[64,2,128]{2,1,0:T(2,128)S(1)} all-to-all(f32[64,2,128]{2,1,0:T(2,128)S(1)} %shard_map.63), channel_id=1, replica_groups=mesh['cy'=8,'zl'=4,'core'=2,'zh'=2,'cx'=4] {'zl','core','zh','cx'}, dimensions={0} | all-to-all | bytes 131072 | tf_op jit(solution)/shard_map/all_to_all | solution.py:533
  78.6 0.7 shard_map.64
Async XLA Ops:
  1.9 19.4 %collective-permute-start = (f32[280,128]{1,0:T(8,128)S(1)}, f32[280,128]{1,0:T(8,128)S(1)}, u32[]{:S(2)}, u32[]{:S(2)}) collective-permute-start(f32[280,128]{1,0:T(8,128)S(1)} %get-tuple-element.15), channel_id=1, source_target_pairs={{0,7},{1,2},{2,1},{3,4},{4,3},{5,6},{6,5},{7,0},{8,15},{9,10},{10,... | collective-permute-start | bytes 430088 | tf_op jit(solution)/shard_map/ppermute | solution.py:476
  15.5 6.2 %collective-permute-start.1 = (f32[280,128]{1,0:T(8,128)S(1)}, f32[280,128]{1,0:T(8,128)S(1)}, u32[]{:S(2)}, u32[]{:S(2)}) collective-permute-start(f32[280,128]{1,0:T(8,128)S(1)} %get-tuple-element.16), channel_id=1, source_target_pairs={{0,1},{1,0},{2,3},{3,2},{4,5},{5,4},{6,7},{7,6},{8,9},{9,8},{10,11... | collective-permute-start | bytes 430088 | tf_op jit(solution)/shard_map/ppermute | solution.py:476
  21.7 35.7 %copy-start = (f32[4776,128]{1,0:T(8,128)S(1)}, f32[4776,128]{1,0:T(8,128)}, u32[]{:S(2)}) copy-start(f32[4776,128]{1,0:T(8,128)} %constant.2.clone.table) | copy-start | bytes 7335940
  22.0 16.8 %collective-permute-start.2 = (f32[968,128]{1,0:T(8,128)S(1)}, f32[968,128]{1,0:T(8,128)S(1)}, u32[]{:S(2)}, u32[]{:S(2)}) collective-permute-start(f32[968,128]{1,0:T(8,128)S(1)} %get-tuple-element.17), channel_id=1, source_target_pairs={{0,504},{8,16},{16,8},{24,32},{32,24},{40,48},{48,40},{56,64},{64,... | collective-permute-start | bytes 1486856 | tf_op jit(solution)/shard_map/ppermute | solution.py:476
  27.0 11.9 %collective-permute-start.3 = (f32[968,128]{1,0:T(8,128)S(1)}, f32[968,128]{1,0:T(8,128)S(1)}, u32[]{:S(2)}, u32[]{:S(2)}) collective-permute-start(f32[968,128]{1,0:T(8,128)S(1)} %get-tuple-element.18), channel_id=1, source_target_pairs={{0,8},{8,0},{16,24},{24,16},{32,40},{40,32},{48,56},{56,48},{64,72... | collective-permute-start | bytes 1486856 | tf_op jit(solution)/shard_map/ppermute | solution.py:476
  43.6 13.8 %all-to-all-start = ((f32[8,8,128]{2,1,0:T(8,128)}), f32[8,8,128]{2,1,0:T(8,128)S(1)}, u32[]{:S(2)}, u32[]{:S(2)}) async-start(f32[8,8,128]{2,1,0:T(8,128)} %get-tuple-element.19), calls=%async_computation | async-start | bytes 65536 | tf_op jit(solution)/shard_map/all_to_all | solution.py:518
  50.5 1.5 %copy-start.1 = (f32[19,8,24,128]{3,2,1,0:T(8,128)S(1)}, f32[19,8,24,128]{3,2,1,0:T(8,128)}, u32[]{:S(2)}) copy-start(f32[19,8,24,128]{3,2,1,0:T(8,128)} %get-tuple-element.20.state) | copy-start | bytes 5603332

commit v3 on v2

--- a/solution.py
+++ b/solution.py
@@ -51,7 +51,7 @@
 GROUP = 8
 
 
-REACH = STEPS - 1
+REACH = STEPS - 2
 
 
 def pack_y(sign):
@@ -74,12 +74,21 @@
     return out, -(-at // 8) * 8
 
 
+SPAN = 2 * REACH + LY
 Y_UP, Y_ROWS = pack_y(1)
 Y_DOWN, _ = pack_y(-1)
 X_RIGHT, X_ROWS = pack_x(1)
 X_LEFT, _ = pack_x(-1)
 Y_UP_AT = {(ch, x): (n, at) for ch, x, _, n, at in Y_UP}
 Y_DOWN_AT = {(ch, x): (n, at) for ch, x, _, n, at in Y_DOWN}
+X_RIGHT_AT = {(ch, x): at for ch, x, _, _, at in X_RIGHT}
+X_LEFT_AT = {(ch, x): at for ch, x, _, _, at in X_LEFT}
+UP = [i for i in range(19) if CY[i] == 1]
+DOWN = [i for i in range(19) if CY[i] == -1]
+RIGHT = [i for i in range(19) if CX[i] == 1]
+LEFT = [i for i in range(19) if CX[i] == -1]
+EDGE_Y_ROWS = 24
+EDGE_X_ROWS = 40
 
 
 def collide(f, label, drive, phase):
@@ -181,85 +190,88 @@
     far[...] = box[1]
 
 
-ROW0 = 12
-COL0 = 4
-WORK_ROWS = 32
-WORK_COLS = LX + 8
-STATE_ROW0 = 8
-STATE_COL0 = 2
-STATE_ROWS = 24
-STATE_COLS = LX + 4
+PACK = 16
+ROW0 = 8
+WORK_ROWS = 24
+
+
+def own_kernel(cells, got_far, got_near, packs, rows):
+    odd_y = lax.rem(lax.axis_index(GY), 2)
+    rows[0] = got_near[...]
+    rows[1] = got_far[...]
+    for ch in range(CHANNELS):
+        for x in range(LX):
+            low, source = Y_UP_AT[ch, x]
+            packs[ch, x, 0:low, :] = rows[1 - odd_y, source : source + low, :]
+            packs[ch, x, low : low + LY, :] = cells[ch, x]
+            high, source = Y_DOWN_AT[ch, x]
+            packs[ch, x, low + LY : low + LY + high, :] = rows[odd_y, source : source + high, :]
+
+
+def spin(value, i):
+    cz = VELOCITY[i][2]
+    return pltpu.roll(value, cz % NZ, 1) if cz else value
 
 
 def arrive(source, x, row, n):
-    f = []
-    for i in range(19):
-        cx, cy, cz = VELOCITY[i]
-        value = source[i, x - cx, row - cy : row - cy + n, :]
-        f.append(pltpu.roll(value, cz % NZ, 1) if cz else value)
-    return f
-
-
-def around(aux, x, row, n):
-    return aux[0, x, row : row + n, :], [aux[1 + axis, x, row : row + n, :] for axis in range(3)]
+    return [
+        spin(source[i, x - CX[i], row - CY[i] : row - CY[i] + n, :], i) for i in range(19)
+    ]
 
 
 def third_kernel(
-    cells, total, y_far, y_near, x_far, x_near, state, aux, spread, rows, cols, one, mid, sums, two, sem
+    cells, total, packs, x_far, x_near, post3, spread, edge_far, edge_near, cols, one, two, sums, box
 ):
     odd_y = lax.rem(lax.axis_index(GY), 2)
     odd_x = lax.rem(lax.axis_index(GX), 2)
-    low_slot, high_slot = 1 - odd_y, odd_y
     left_slot, right_slot = 1 - odd_x, odd_x
-    rows[0] = y_near[...]
-    rows[1] = y_far[...]
     cols[0] = x_near[...]
     cols[1] = x_far[...]
 
-    def place(ch, x, row, values):
-        n = values.shape[0]
-        if ch < 19:
-            one[ch, x + COL0, row + ROW0 : row + ROW0 + n, :] = values
-        else:
-            aux[ch - 19, x + COL0, row + ROW0 : row + ROW0 + n, :] = values
-
-    for ch in range(CHANNELS):
-        for x in range(LX):
-            place(ch, x, 0, cells[ch, x])
-    for ch, x, row, n, at in Y_UP:
-        place(ch, x, row - LY, rows[low_slot, at : at + n, :])
-    for ch, x, row, n, at in Y_DOWN:
-        place(ch, x, row + LY, rows[high_slot, at : at + n, :])
-    for ch, x, low, high, at in X_RIGHT:
-        place(ch, x - LX, -low, cols[left_slot, at : at + low + LY + high, :])
-    for ch, x, low, high, at in X_LEFT:
-        place(ch, x + LX, -low, cols[right_slot, at : at + low + LY + high, :])
-
-    wide = 16
-    start = ROW0 - 4
-    sums[...] = jnp.zeros(sums.shape, jnp.float32)
-    for step, source, target, back, to in ((1, one, mid, 0, start), (2, mid, two, 2, STATE_ROW0 - 4)):
-
-        def layer(x, carry, step=step, source=source, target=target, back=back, to=to):
-            f = arrive(source, x, start, wide)
-            lab, force = around(aux, x, start, wide)
-            post, stress = collide(f, lab, force, PHASES[step])
-            for i in range(19):
-                target[i, x - back, to : to + wide, :] = post[i]
-            own = jnp.logical_and(x >= COL0, x < COL0 + LX)
-            for k in range(6):
-                sums[k] += jnp.where(own, stress[k], 0.0)
-            return carry
-
-        lax.fori_loop(COL0 + step - STEPS, COL0 + LX + STEPS - step, layer, 0)
-    save = pltpu.make_async_copy(two, state, sem)
-    save.start()
-    last = [total[k] + sums[k, 4:12, :] for k in range(6)]
+    def packed(ch, x):
+        if x < 0:
+            at = X_RIGHT_AT[ch, x + LX]
+            return cols[left_slot, at : at + SPAN, :]
+        if x >= LX:
+            at = X_LEFT_AT[ch, x - LX]
+            return cols[right_slot, at : at + SPAN, :]
+        return packs[ch, x, 0:SPAN, :]
+
+    def add(first, second):
+        return second if first is None else [a + b for a, b in zip(first, second)]
+
+    low = ROW0 - REACH
+    kept = None
+    for x in range(-REACH, LX + REACH):
+        f = [spin(packed(i, x - CX[i]), i) for i in range(19)]
+        post, stress = collide(f, packed(19, x), [packed(20 + axis, x) for axis in range(3)], PHASES[1])
+        for i in range(19):
+            one[i, x + REACH, low : low + SPAN, :] = post[i]
+        if 0 <= x < LX:
+            kept = add(kept, stress)
+    for k in range(6):
+        sums[k, 0:SPAN, :] = kept[k]
+    low, n = ROW0 - 1, LY + 2
+    kept = None
+    for x in range(-1, LX + 1):
+        f = arrive(one, x + REACH, low, n)
+        lab, *force = [packed(ch, x)[REACH - 1 : REACH - 1 + n] for ch in range(19, CHANNELS)]
+        post, stress = collide(f, lab, force, PHASES[2])
+        for i in range(19):
+            two[i, x + 1, low : low + n, :] = post[i]
+        if 0 <= x < LX:
+            kept = add(kept, stress)
+    for k in range(6):
+        sums[6 + k, 0:n, :] = kept[k]
+    last = [
+        total[k] + sums[k, REACH : REACH + LY, :] + sums[6 + k, 1 : 1 + LY, :] for k in range(6)
+    ]
     for x in range(LX):
-        f = arrive(two, x + STATE_COL0, STATE_ROW0, LY)
-        lab, force = around(aux, x + COL0, ROW0, LY)
-        _, stress = collide(f, lab, force, PHASES[3])
-        last = [last[k] + stress[k] for k in range(6)]
+        f = arrive(two, x + 1, ROW0, LY)
+        post, stress = collide(f, cells[19, x], [cells[20 + axis, x] for axis in range(3)], PHASES[3])
+        for i in range(19):
+            post3[i, x] = post[i]
+        last = add(last, stress)
     stacked = jnp.concatenate(last, axis=0)
     r = lax.broadcasted_iota(jnp.int32, (16, 48), 0)
     c = lax.broadcasted_iota(jnp.int32, (16, 48), 1)
@@ -280,23 +292,64 @@
         )
     for d in range(spread.shape[0]):
         spread[d] = slow
-    save.wait()
-
-
-def momentum_kernel(state, aux, out, work):
-    wide = 16
-
-    def layer(x, carry):
-        f = arrive(state, x, STATE_ROW0 - 4, wide)
-        lab, force = around(aux, x + (COL0 - STATE_COL0), ROW0 - 4, wide)
-        post, _ = collide(f, lab, force, PHASES[3])
-        for i in range(1, 19):
-            work[i, x, STATE_ROW0 - 4 : STATE_ROW0 - 4 + wide, :] = post[i]
-        return carry
-
-    lax.fori_loop(STATE_COL0 - 1, STATE_COL0 + LX + 1, layer, 0)
+    for slot, comps, row in ((odd_y, UP, LY - 1), (1 - odd_y, DOWN, 0)):
+        for k, i in enumerate(comps):
+            for x in range(LX):
+                at = k * LX + x
+                box[slot, at : at + 1, :] = post3[i, x, row : row + 1, :]
+    edge_near[...] = box[0]
+    edge_far[...] = box[1]
+
+
+def edge_kernel(post3, y_far, y_near, far, near, rows, box):
+    odd_y = lax.rem(lax.axis_index(GY), 2)
+    low_slot, high_slot = 1 - odd_y, odd_y
+    right = lax.rem(lax.axis_index(GX), 2)
+    rows[0] = y_near[...]
+    rows[1] = y_far[...]
+    for slot, comps, x in ((right, RIGHT, LX - 1), (1 - right, LEFT, 0)):
+        for k, i in enumerate(comps):
+            at = k * LY
+            if CY[i] == 0:
+                box[slot, at : at + LY, :] = post3[i, x]
+            elif CY[i] == 1:
+                source = UP.index(i) * LX + x
+                box[slot, at : at + 1, :] = rows[low_slot, source : source + 1, :]
+                box[slot, at + 1 : at + LY, :] = post3[i, x, 0 : LY - 1, :]
+            else:
+                source = DOWN.index(i) * LX + x
+                box[slot, at : at + LY - 1, :] = post3[i, x, 1:LY, :]
+                box[slot, at + LY - 1 : at + LY, :] = rows[high_slot, source : source + 1, :]
+    near[...] = box[0]
+    far[...] = box[1]
+
+
+def momentum_kernel(post3, y_far, y_near, x_far, x_near, out, rows, cols, work):
+    odd_y = lax.rem(lax.axis_index(GY), 2)
+    odd_x = lax.rem(lax.axis_index(GX), 2)
+    rows[0] = y_near[...]
+    rows[1] = y_far[...]
+    cols[0] = x_near[...]
+    cols[1] = x_far[...]
+    for i in range(1, 19):
+        for x in range(LX):
+            work[i, x + 1, ROW0 : ROW0 + LY, :] = post3[i, x]
+    for k, i in enumerate(UP):
+        for x in range(LX):
+            at = k * LX + x
+            work[i, x + 1, ROW0 - 1 : ROW0, :] = rows[1 - odd_y, at : at + 1, :]
+    for k, i in enumerate(DOWN):
+        for x in range(LX):
+            at = k * LX + x
+            work[i, x + 1, ROW0 + LY : ROW0 + LY + 1, :] = rows[odd_y, at : at + 1, :]
+    for k, i in enumerate(RIGHT):
+        work[i, 0, ROW0 - CY[i] : ROW0 - CY[i] + LY, :] = cols[1 - odd_x, k * LY : k * LY + LY, :]
+    for k, i in enumerate(LEFT):
+        work[i, LX + 1, ROW0 - CY[i] : ROW0 - CY[i] + LY, :] = cols[odd_x, k * LY : k * LY + LY, :]
     for x in range(LX):
-        f = arrive(work, x + STATE_COL0, STATE_ROW0, LY)
+        f = [None] + [
+            spin(work[i, x + 1 - CX[i], ROW0 - CY[i] : ROW0 - CY[i] + LY, :], i) for i in range(1, 19)
+        ]
         for axis in range(3):
             total = None
             for i in range(1, 19, 2):
@@ -448,19 +501,16 @@
             out[a, 0, y : y + 1, :] = value[:, :SZ]
 
 
-def call(body, outs, scratch, cost, limit=16, place=pltpu.VMEM, more=(), far=0):
-    shapes = [
-        pltpu.HBM(s, jnp.float32) if k < far else jax.ShapeDtypeStruct(s, jnp.float32) for k, s in enumerate(outs)
-    ]
+def call(body, outs, scratch, cost, limit=16, place=pltpu.VMEM, more=()):
+    shapes = [jax.ShapeDtypeStruct(s, jnp.float32) for s in outs]
+    spec = pl.BlockSpec(memory_space=pltpu.VMEM)
 
     def run(*args):
         return pl.pallas_call(
             body,
             out_shape=shapes,
             in_specs=[pl.BlockSpec(memory_space=place)] * len(args),
-            out_specs=[
-                pl.BlockSpec(memory_space=pltpu.HBM if k < far else pltpu.VMEM) for k in range(len(shapes))
-            ],
+            out_specs=[spec] * len(shapes),
             scratch_shapes=[pltpu.VMEM(s, jnp.float32) for s in scratch] + list(more),
             compiler_params=pltpu.CompilerParams(vmem_limit_bytes=limit << 20),
             cost_estimate=pl.CostEstimate(flops=cost, bytes_accessed=cost, transcendentals=0),
@@ -500,29 +550,24 @@
         2_000_000,
     )(cells, y_far, y_near)
     x_far, x_near = swap(far, near, GX)
-    state, aux, spread = call(
+    (packs,) = call(
+        own_kernel, [(CHANNELS, LX, PACK, NZ)], [(2, Y_ROWS, NZ)], 2_000_000
+    )(cells, y_far, y_near)
+    post3, spread, far, near = call(
         third_kernel,
-        [(19, STATE_COLS, STATE_ROWS, NZ), (4, WORK_COLS, WORK_ROWS, NZ), (groups, 8, NZ)],
+        [(19, LX, LY, NZ), (groups, 8, NZ), (EDGE_Y_ROWS, NZ), (EDGE_Y_ROWS, NZ)],
         [
-            (2, Y_ROWS, NZ),
             (2, X_ROWS, NZ),
-            (19, WORK_COLS, WORK_ROWS, NZ),
-            (19, WORK_COLS, WORK_ROWS, NZ),
-            (6, 16, NZ),
-            (19, STATE_COLS, STATE_ROWS, NZ),
+            (19, LX + 2 * REACH, WORK_ROWS, NZ),
+            (19, LX + 2, WORK_ROWS, NZ),
+            (12, 16, NZ),
+            (2, EDGE_Y_ROWS, NZ),
         ],
         20_000_000,
-        more=[pltpu.SemaphoreType.DMA(())],
-        far=1,
-    )(cells, total, y_far, y_near, x_far, x_near)
+    )(cells, total, packs, x_far, x_near)
     blocks = lax.all_to_all(spread, "cy", 0, 0, tiled=False)
-    (momentum,) = call(
-        momentum_kernel,
-        [(3, LX, LY, NZ)],
-        [(19, STATE_COLS, STATE_ROWS, NZ)],
-        10_000_000,
-    )(state, aux)
-    blocks, momentum = lax.optimization_barrier((blocks, momentum))
+    ey_far, ey_near = swap(far, near, GY)
+    blocks, ey_far, ey_near = lax.optimization_barrier((blocks, ey_far, ey_near))
     table, starts, imaginary = operator_table(nx, 2 * ny)
     (parts,) = call(
         functools.partial(solve_kernel, starts, imaginary, ny),
@@ -531,6 +576,19 @@
         10_000_000,
     )(blocks, table)
     parts = lax.all_to_all(parts, ("zl", "core", "zh", "cx"), 0, 0, tiled=False)
+    far, near = call(
+        edge_kernel,
+        [(EDGE_X_ROWS, NZ), (EDGE_X_ROWS, NZ)],
+        [(2, EDGE_Y_ROWS, NZ), (2, EDGE_X_ROWS, NZ)],
+        200_000,
+    )(post3, ey_far, ey_near)
+    ex_far, ex_near = swap(far, near, GX)
+    (momentum,) = call(
+        momentum_kernel,
+        [(3, LX, LY, NZ)],
+        [(2, EDGE_Y_ROWS, NZ), (2, EDGE_X_ROWS, NZ), (19, LX + 2, WORK_ROWS, NZ)],
+        1_000_000,
+    )(post3, ey_far, ey_near, ex_far, ex_near)
     (running,) = call(last_kernel, [(3, 1, 2, SZ)], [], 100_000)(parts)
     return momentum, running
 

time: 79.6 us -> 78.8 us (0.990)
  starting transfers between devices: 32.7 us -> 61.7 us
  blocking collectives: 19.6 us -> 0 us
  waiting for transfers between devices: 14.8 us -> 8.4 us
  Pallas kernels: 9.97 us -> 7.48 us
  local copies, waits for them, and re-layouts: 1.51 us -> 0.01 us
    all_to_all x1 -> x0, blocking collectives: 19.6 us -> none  [local(): parts = lax.all_to_all(parts, ('zl', 'core', 'zh', 'cx'), 0, 0, tiled=False)]
    ppermute x2 -> x4, starting transfers between devices: 18.6 us -> 30 us  [swap(): lax.ppermute(far, axis, far_pairs)]
    all_to_all x0 -> x1, starting transfers between devices: none -> 9.29 us  [local(): parts = lax.all_to_all(parts, ('zl', 'core', 'zh', 'cx'), 0, 0, tiled=False)]
    ppermute x2 -> x4, starting transfers between devices: 7.2 us -> 15.6 us  [swap(): lax.ppermute(near, axis, near_pairs)]
    ppermute x2 -> x4, waiting for transfers between devices: 10.3 us -> 4.23 us  [swap(): lax.ppermute(far, axis, far_pairs)]
    all_to_all x1, waiting for transfers between devices: 3.96 us -> 0.01 us  [local(): blocks = lax.all_to_all(spread, 'cy', 0, 0, tiled=False)]
    ppermute x2 -> x4, waiting for transfers between devices: 0.5 us -> 4.17 us  [swap(): lax.ppermute(near, axis, near_pairs)]
    pallas_call x6 -> x8, Pallas kernels: 9.97 us -> 7.48 us  [run(): pl.pallas_call(body, out_shape=shapes, in_specs=[pl.BlockSpec(memory_spac...]
  transfers between devices with their start and end apart: 5 -> 10, of which waited for: 4 -> 6; matrix products, arithmetic and copies ran while one was open for 0% -> 0% of each run, Pallas kernels for 2% -> 1%
where the time goes in v3:
time: 78.8 us; the launch traced here: 78.4 us
  starting transfers between devices  61.7 us (78%)
  waiting for transfers between devices  8.4 us (11%)
  Pallas kernels  7.48 us (9%)
    ppermute x4, starting transfers between devices, swap(): lax.ppermute(far, axis, far_pairs)  30 us
    ppermute x4, starting transfers between devices, swap(): lax.ppermute(near, axis, near_pairs)  15.6 us
    all_to_all x1, starting transfers between devices, local(): parts = lax.all_to_all(parts, ('zl', 'core', 'zh', 'cx'), 0, 0, tiled=False)  9.29 us
    pallas_call x8, Pallas kernels, run(): pl.pallas_call(body, out_shape=shapes, in_specs=[pl.BlockSpec(memory_spac...  7.48 us
    all_to_all x1, starting transfers between devices, local(): blocks = lax.all_to_all(spread, 'cy', 0, 0, tiled=False)  6.82 us
    ppermute x4, waiting for transfers between devices, swap(): lax.ppermute(far, axis, far_pairs)  4.23 us
    ppermute x4, waiting for transfers between devices, swap(): lax.ppermute(near, axis, near_pairs)  4.17 us
  transfers between devices with their start and end apart: 10, of which 6 were waited for; matrix products, arithmetic and copies ran while one was open for 0% of the time, Pallas kernels for 1%

profile of v3, /device:TPU:1, one launch (start us, length us, event | category | flops | bytes accessed | tf_op | source)
XLA Modules:
  0.0 78.4 jit_solution(3821334264407669138)
XLA Ops:
  0.6 0.0 copy-start
  0.6 1.4 %shard_map.59 = (f32[23,4,8,128]{3,2,1,0:T(8,128)S(1)}, f32[6,8,128]{2,1,0:T(8,128)S(1)}, f32[184,128]{1,0:T(8,128)S(1)}, f32[184,128]{1,0:T(8,128)S(1)}) custom-call(f32[19,4,8,128]{3,2,1,0:T(8,128)} %pops_in.1, s32[4,8,128]{2,1,0:T(8,128)} %label_in.1, f32[3,4,8,128]{3,2,1,0:T(8,128)} %drive_in.1), custom_call_target="tpu_custom_call" | custom-call | flops 2000000 | bytes 2000000 | tf_op jit(solution)/shard_map/pallas_call | solution.py:509
  2.0 13.7 %collective-permute-start = (f32[184,128]{1,0:T(8,128)S(1)}, f32[184,128]{1,0:T(8,128)S(1)}, u32[]{:S(2)}, u32[]{:S(2)}) collective-permute-start(f32[184,128]{1,0:T(8,128)S(1)} %get-tuple-element.19), channel_id=1, source_target_pairs={{0,7},{1,2},{2,1},{3,4},{4,3},{5,6},{6,5},{7,0},{8,15},{9,10},{10,... | collective-permute-start | bytes 282632 | tf_op jit(solution)/shard_map/ppermute | solution.py:526
  15.7 1.9 %collective-permute-start.1 = (f32[184,128]{1,0:T(8,128)S(1)}, f32[184,128]{1,0:T(8,128)S(1)}, u32[]{:S(2)}, u32[]{:S(2)}) collective-permute-start(f32[184,128]{1,0:T(8,128)S(1)} %get-tuple-element.20), channel_id=1, source_target_pairs={{0,1},{1,0},{2,3},{3,2},{4,5},{5,4},{6,7},{7,6},{8,9},{9,8},{10,11... | collective-permute-start | bytes 282632 | tf_op jit(solution)/shard_map/ppermute | solution.py:526
  17.6 2.0 %collective-permute-done.got_far = f32[184,128]{1,0:T(8,128)S(1)} collective-permute-done((f32[184,128]{1,0:T(8,128)S(1)}, f32[184,128]{1,0:T(8,128)S(1)}, u32[]{:S(2)}, u32[]{:S(2)}) %collective-permute-start) | collective-permute-done | bytes 94240 | tf_op jit(solution)/shard_map/ppermute | solution.py:526
  19.7 1.3 %collective-permute-done.1.got_near = f32[184,128]{1,0:T(8,128)S(1)} collective-permute-done((f32[184,128]{1,0:T(8,128)S(1)}, f32[184,128]{1,0:T(8,128)S(1)}, u32[]{:S(2)}, u32[]{:S(2)}) %collective-permute-start.1) | collective-permute-done | bytes 94240 | tf_op jit(solution)/shard_map/ppermute | solution.py:526
  21.0 0.1 shard_map.61
  21.2 5.1 %collective-permute-start.2 = (f32[552,128]{1,0:T(8,128)S(1)}, f32[552,128]{1,0:T(8,128)S(1)}, u32[]{:S(2)}, u32[]{:S(2)}) collective-permute-start(f32[552,128]{1,0:T(8,128)S(1)} %get-tuple-element.21), channel_id=1, source_target_pairs={{0,504},{8,16},{16,8},{24,32},{32,24},{40,48},{48,40},{56,64},{64,... | collective-permute-start | bytes 847880 | tf_op jit(solution)/shard_map/ppermute | solution.py:526
  26.3 5.0 %collective-permute-start.3 = (f32[552,128]{1,0:T(8,128)S(1)}, f32[552,128]{1,0:T(8,128)S(1)}, u32[]{:S(2)}, u32[]{:S(2)}) collective-permute-start(f32[552,128]{1,0:T(8,128)S(1)} %get-tuple-element.22), channel_id=1, source_target_pairs={{0,8},{8,0},{16,24},{24,16},{32,40},{40,32},{48,56},{56,48},{64,72... | collective-permute-start | bytes 847880 | tf_op jit(solution)/shard_map/ppermute | solution.py:526
  31.3 0.1 shard_map.60.packs
  31.4 1.4 %collective-permute-done.2.x_far = f32[552,128]{1,0:T(8,128)S(1)} collective-permute-done((f32[552,128]{1,0:T(8,128)S(1)}, f32[552,128]{1,0:T(8,128)S(1)}, u32[]{:S(2)}, u32[]{:S(2)}) %collective-permute-start.2) | collective-permute-done | bytes 282656 | tf_op jit(solution)/shard_map/ppermute | solution.py:526
  32.8 2.3 %shard_map.62 = (f32[19,4,8,128]{3,2,1,0:T(8,128)S(1)}, f32[8,8,128]{2,1,0:T(8,128)}, f32[24,128]{1,0:T(8,128)S(1)}, f32[24,128]{1,0:T(8,128)S(1)}) custom-call(f32[23,4,8,128]{3,2,1,0:T(8,128)S(1)} %get-tuple-element.17.cells, f32[6,8,128]{2,1,0:T(8,128)S(1)} %get-tuple-element.18.total, f32[23,4,16,128]{3,2,1,0:T(8,128)S(1)} %shard_map.60.packs, ...), custom_call_target="tpu_custom_call" | custom-call | flops 20000000 | bytes 20000000 | tf_op jit(solution)/shard_map/pallas_call | solution.py:509
  35.1 6.8 %all-to-all-start = ((f32[8,8,128]{2,1,0:T(8,128)}), f32[8,8,128]{2,1,0:T(8,128)S(1)}, u32[]{:S(2)}, u32[]{:S(2)}) async-start(f32[8,8,128]{2,1,0:T(8,128)} %get-tuple-element.24), calls=%async_computation | async-start | bytes 65536 | tf_op jit(solution)/shard_map/all_to_all | solution.py:568
  41.9 7.7 %collective-permute-start.4 = (f32[24,128]{1,0:T(8,128)S(1)}, f32[24,128]{1,0:T(8,128)S(1)}, u32[]{:S(2)}, u32[]{:S(2)}) collective-permute-start(f32[24,128]{1,0:T(8,128)S(1)} %get-tuple-element.25), channel_id=1, source_target_pairs={{0,7},{1,2},{2,1},{3,4},{4,3},{5,6},{6,5},{7,0},{8,15},{9,10},{10,... | collective-permute-start | bytes 36872 | tf_op jit(solution)/shard_map/ppermute | solution.py:526
  49.6 1.9 %collective-permute-start.5 = (f32[24,128]{1,0:T(8,128)S(1)}, f32[24,128]{1,0:T(8,128)S(1)}, u32[]{:S(2)}, u32[]{:S(2)}) collective-permute-start(f32[24,128]{1,0:T(8,128)S(1)} %get-tuple-element.26), channel_id=1, source_target_pairs={{0,1},{1,0},{2,3},{3,2},{4,5},{5,4},{6,7},{7,6},{8,9},{9,8},{10,11... | collective-permute-start | bytes 36872 | tf_op jit(solution)/shard_map/ppermute | solution.py:526
  51.5 0.8 %collective-permute-done.4.y_far = f32[24,128]{1,0:T(8,128)S(1)} collective-permute-done((f32[24,128]{1,0:T(8,128)S(1)}, f32[24,128]{1,0:T(8,128)S(1)}, u32[]{:S(2)}, u32[]{:S(2)}) %collective-permute-start.4) | collective-permute-done | bytes 12320 | tf_op jit(solution)/shard_map/ppermute | solution.py:526
  52.3 2.0 %collective-permute-done.5.y_near = f32[24,128]{1,0:T(8,128)S(1)} collective-permute-done((f32[24,128]{1,0:T(8,128)S(1)}, f32[24,128]{1,0:T(8,128)S(1)}, u32[]{:S(2)}, u32[]{:S(2)}) %collective-permute-start.5) | collective-permute-done | bytes 12320 | tf_op jit(solution)/shard_map/ppermute | solution.py:526
  54.4 2.1 %shard_map.65 = f32[64,2,128]{2,1,0:T(2,128)} custom-call(f32[8,8,128]{2,1,0:T(8,128)S(1)} %all-to-all-done.blocks, f32[4776,128]{1,0:T(8,128)S(1)} %copy-done), custom_call_target="tpu_custom_call" | custom-call | flops 10000000 | bytes 10000000 | tf_op jit(solution)/shard_map/pallas_call | solution.py:509
  56.5 9.3 %all-to-all-start.1 = ((f32[64,2,128]{2,1,0:T(2,128)}), f32[64,2,128]{2,1,0:T(2,128)S(1)}, u32[]{:S(2)}, u32[]{:S(2)}) async-start(f32[64,2,128]{2,1,0:T(2,128)} %shard_map.65), calls=%async_computation.1 | async-start | bytes 131072 | tf_op jit(solution)/shard_map/all_to_all | solution.py:578
  65.8 3.5 %collective-permute-start.6 = (f32[40,128]{1,0:T(8,128)S(1)}, f32[40,128]{1,0:T(8,128)S(1)}, u32[]{:S(2)}, u32[]{:S(2)}) collective-permute-start(f32[40,128]{1,0:T(8,128)S(1)} %get-tuple-element.29), channel_id=1, source_target_pairs={{0,504},{8,16},{16,8},{24,32},{32,24},{40,48},{48,40},{56,64},{64,... | collective-permute-start | bytes 61448 | tf_op jit(solution)/shard_map/ppermute | solution.py:526
  69.3 6.7 %collective-permute-start.7 = (f32[40,128]{1,0:T(8,128)S(1)}, f32[40,128]{1,0:T(8,128)S(1)}, u32[]{:S(2)}, u32[]{:S(2)}) collective-permute-start(f32[40,128]{1,0:T(8,128)S(1)} %get-tuple-element.30), channel_id=1, source_target_pairs={{0,8},{8,0},{16,24},{24,16},{32,40},{40,32},{48,56},{56,48},{64,72... | collective-permute-start | bytes 61448 | tf_op jit(solution)/shard_map/ppermute | solution.py:526
  76.1 0.8 %collective-permute-done.7.x_near = f32[40,128]{1,0:T(8,128)S(1)} collective-permute-done((f32[40,128]{1,0:T(8,128)S(1)}, f32[40,128]{1,0:T(8,128)S(1)}, u32[]{:S(2)}, u32[]{:S(2)}) %collective-permute-start.7) | collective-permute-done | bytes 20512 | tf_op jit(solution)/shard_map/ppermute | solution.py:526
  76.9 0.7 shard_map.64
  77.7 0.7 shard_map.66
  (6 shorter events, 0.1 us)
Async XLA Ops:
  0.6 53.7 %copy-start = (f32[4776,128]{1,0:T(8,128)S(1)}, f32[4776,128]{1,0:T(8,128)}, u32[]{:S(2)}) copy-start(f32[4776,128]{1,0:T(8,128)} %constant.2.clone.table) | copy-start | bytes 7335940
  2.0 17.6 %collective-permute-start = (f32[184,128]{1,0:T(8,128)S(1)}, f32[184,128]{1,0:T(8,128)S(1)}, u32[]{:S(2)}, u32[]{:S(2)}) collective-permute-start(f32[184,128]{1,0:T(8,128)S(1)} %get-tuple-element.19), channel_id=1, source_target_pairs={{0,7},{1,2},{2,1},{3,4},{4,3},{5,6},{6,5},{7,0},{8,15},{9,10},{10,... | collective-permute-start | bytes 282632 | tf_op jit(solution)/shard_map/ppermute | solution.py:526
  15.7 5.3 %collective-permute-start.1 = (f32[184,128]{1,0:T(8,128)S(1)}, f32[184,128]{1,0:T(8,128)S(1)}, u32[]{:S(2)}, u32[]{:S(2)}) collective-permute-start(f32[184,128]{1,0:T(8,128)S(1)} %get-tuple-element.20), channel_id=1, source_target_pairs={{0,1},{1,0},{2,3},{3,2},{4,5},{5,4},{6,7},{7,6},{8,9},{9,8},{10,11... | collective-permute-start | bytes 282632 | tf_op jit(solution)/shard_map/ppermute | solution.py:526
  21.2 11.6 %collective-permute-start.2 = (f32[552,128]{1,0:T(8,128)S(1)}, f32[552,128]{1,0:T(8,128)S(1)}, u32[]{:S(2)}, u32[]{:S(2)}) collective-permute-start(f32[552,128]{1,0:T(8,128)S(1)} %get-tuple-element.21), channel_id=1, source_target_pairs={{0,504},{8,16},{16,8},{24,32},{32,24},{40,48},{48,40},{56,64},{64,... | collective-permute-start | bytes 847880 | tf_op jit(solution)/shard_map/ppermute | solution.py:526
  26.3 6.5 %collective-permute-start.3 = (f32[552,128]{1,0:T(8,128)S(1)}, f32[552,128]{1,0:T(8,128)S(1)}, u32[]{:S(2)}, u32[]{:S(2)}) collective-permute-start(f32[552,128]{1,0:T(8,128)S(1)} %get-tuple-element.22), channel_id=1, source_target_pairs={{0,8},{8,0},{16,24},{24,16},{32,40},{40,32},{48,56},{56,48},{64,72... | collective-permute-start | bytes 847880 | tf_op jit(solution)/shard_map/ppermute | solution.py:526
  35.1 19.3 %all-to-all-start = ((f32[8,8,128]{2,1,0:T(8,128)}), f32[8,8,128]{2,1,0:T(8,128)S(1)}, u32[]{:S(2)}, u32[]{:S(2)}) async-start(f32[8,8,128]{2,1,0:T(8,128)} %get-tuple-element.24), calls=%async_computation | async-start | bytes 65536 | tf_op jit(solution)/shard_map/all_to_all | solution.py:568
  41.9 10.4 %collective-permute-start.4 = (f32[24,128]{1,0:T(8,128)S(1)}, f32[24,128]{1,0:T(8,128)S(1)}, u32[]{:S(2)}, u32[]{:S(2)}) collective-permute-start(f32[24,128]{1,0:T(8,128)S(1)} %get-tuple-element.25), channel_id=1, source_target_pairs={{0,7},{1,2},{2,1},{3,4},{4,3},{5,6},{6,5},{7,0},{8,15},{9,10},{10,... | collective-permute-start | bytes 36872 | tf_op jit(solution)/shard_map/ppermute | solution.py:526
  49.6 4.7 %collective-permute-start.5 = (f32[24,128]{1,0:T(8,128)S(1)}, f32[24,128]{1,0:T(8,128)S(1)}, u32[]{:S(2)}, u32[]{:S(2)}) collective-permute-start(f32[24,128]{1,0:T(8,128)S(1)} %get-tuple-element.26), channel_id=1, source_target_pairs={{0,1},{1,0},{2,3},{3,2},{4,5},{5,4},{6,7},{7,6},{8,9},{9,8},{10,11... | collective-permute-start | bytes 36872 | tf_op jit(solution)/shard_map/ppermute | solution.py:526
  56.5 21.2 %all-to-all-start.1 = ((f32[64,2,128]{2,1,0:T(2,128)}), f32[64,2,128]{2,1,0:T(2,128)S(1)}, u32[]{:S(2)}, u32[]{:S(2)}) async-start(f32[64,2,128]{2,1,0:T(2,128)} %shard_map.65), calls=%async_computation.1 | async-start | bytes 131072 | tf_op jit(solution)/shard_map/all_to_all | solution.py:578
  65.8 10.3 %collective-permute-start.6 = (f32[40,128]{1,0:T(8,128)S(1)}, f32[40,128]{1,0:T(8,128)S(1)}, u32[]{:S(2)}, u32[]{:S(2)}) collective-permute-start(f32[40,128]{1,0:T(8,128)S(1)} %get-tuple-element.29), channel_id=1, source_target_pairs={{0,504},{8,16},{16,8},{24,32},{32,24},{40,48},{48,40},{56,64},{64,... | collective-permute-start | bytes 61448 | tf_op jit(solution)/shard_map/ppermute | solution.py:526
  69.3 7.6 %collective-permute-start.7 = (f32[40,128]{1,0:T(8,128)S(1)}, f32[40,128]{1,0:T(8,128)S(1)}, u32[]{:S(2)}, u32[]{:S(2)}) collective-permute-start(f32[40,128]{1,0:T(8,128)S(1)} %get-tuple-element.30), channel_id=1, source_target_pairs={{0,8},{8,0},{16,24},{24,16},{32,40},{40,32},{48,56},{56,48},{64,72... | collective-permute-start | bytes 61448 | tf_op jit(solution)/shard_map/ppermute | solution.py:526

commit v4 on v3

--- a/solution.py
+++ b/solution.py
@@ -51,7 +51,7 @@
 GROUP = 8
 
 
-REACH = STEPS - 2
+REACH = STEPS - 1
 
 
 def pack_y(sign):
@@ -83,12 +83,6 @@
 Y_DOWN_AT = {(ch, x): (n, at) for ch, x, _, n, at in Y_DOWN}
 X_RIGHT_AT = {(ch, x): at for ch, x, _, _, at in X_RIGHT}
 X_LEFT_AT = {(ch, x): at for ch, x, _, _, at in X_LEFT}
-UP = [i for i in range(19) if CY[i] == 1]
-DOWN = [i for i in range(19) if CY[i] == -1]
-RIGHT = [i for i in range(19) if CX[i] == 1]
-LEFT = [i for i in range(19) if CX[i] == -1]
-EDGE_Y_ROWS = 24
-EDGE_X_ROWS = 40
 
 
 def collide(f, label, drive, phase):
@@ -193,6 +187,8 @@
 PACK = 16
 ROW0 = 8
 WORK_ROWS = 24
+STATE_ROW0 = 4
+STATE_ROWS = 16
 
 
 def own_kernel(cells, got_far, got_near, packs, rows):
@@ -220,9 +216,8 @@
 
 
 def third_kernel(
-    cells, total, packs, x_far, x_near, post3, spread, edge_far, edge_near, cols, one, two, sums, box
+    cells, total, packs, x_far, x_near, state, near_aux, spread, cols, one, two, sums, sem
 ):
-    odd_y = lax.rem(lax.axis_index(GY), 2)
     odd_x = lax.rem(lax.axis_index(GX), 2)
     left_slot, right_slot = 1 - odd_x, odd_x
     cols[0] = x_near[...]
@@ -251,26 +246,28 @@
             kept = add(kept, stress)
     for k in range(6):
         sums[k, 0:SPAN, :] = kept[k]
-    low, n = ROW0 - 1, LY + 2
+    low, n = ROW0 - (REACH - 1), LY + 2 * (REACH - 1)
+    to = STATE_ROW0 - (REACH - 1)
     kept = None
-    for x in range(-1, LX + 1):
+    for x in range(1 - REACH, LX + REACH - 1):
         f = arrive(one, x + REACH, low, n)
-        lab, *force = [packed(ch, x)[REACH - 1 : REACH - 1 + n] for ch in range(19, CHANNELS)]
+        lab, *force = [packed(ch, x)[1 : 1 + n] for ch in range(19, CHANNELS)]
         post, stress = collide(f, lab, force, PHASES[2])
         for i in range(19):
-            two[i, x + 1, low : low + n, :] = post[i]
+            two[i, x + REACH - 1, to : to + n, :] = post[i]
         if 0 <= x < LX:
             kept = add(kept, stress)
+    save = pltpu.make_async_copy(two, state, sem)
+    save.start()
     for k in range(6):
         sums[6 + k, 0:n, :] = kept[k]
     last = [
-        total[k] + sums[k, REACH : REACH + LY, :] + sums[6 + k, 1 : 1 + LY, :] for k in range(6)
+        total[k] + sums[k, REACH : REACH + LY, :] + sums[6 + k, REACH - 1 : REACH - 1 + LY, :]
+        for k in range(6)
     ]
     for x in range(LX):
-        f = arrive(two, x + 1, ROW0, LY)
-        post, stress = collide(f, cells[19, x], [cells[20 + axis, x] for axis in range(3)], PHASES[3])
-        for i in range(19):
-            post3[i, x] = post[i]
+        f = arrive(two, x + REACH - 1, STATE_ROW0, LY)
+        _, stress = collide(f, cells[19, x], [cells[20 + axis, x] for axis in range(3)], PHASES[3])
         last = add(last, stress)
     stacked = jnp.concatenate(last, axis=0)
     r = lax.broadcasted_iota(jnp.int32, (16, 48), 0)
@@ -292,64 +289,22 @@
         )
     for d in range(spread.shape[0]):
         spread[d] = slow
-    for slot, comps, row in ((odd_y, UP, LY - 1), (1 - odd_y, DOWN, 0)):
-        for k, i in enumerate(comps):
-            for x in range(LX):
-                at = k * LX + x
-                box[slot, at : at + 1, :] = post3[i, x, row : row + 1, :]
-    edge_near[...] = box[0]
-    edge_far[...] = box[1]
-
-
-def edge_kernel(post3, y_far, y_near, far, near, rows, box):
-    odd_y = lax.rem(lax.axis_index(GY), 2)
-    low_slot, high_slot = 1 - odd_y, odd_y
-    right = lax.rem(lax.axis_index(GX), 2)
-    rows[0] = y_near[...]
-    rows[1] = y_far[...]
-    for slot, comps, x in ((right, RIGHT, LX - 1), (1 - right, LEFT, 0)):
-        for k, i in enumerate(comps):
-            at = k * LY
-            if CY[i] == 0:
-                box[slot, at : at + LY, :] = post3[i, x]
-            elif CY[i] == 1:
-                source = UP.index(i) * LX + x
-                box[slot, at : at + 1, :] = rows[low_slot, source : source + 1, :]
-                box[slot, at + 1 : at + LY, :] = post3[i, x, 0 : LY - 1, :]
-            else:
-                source = DOWN.index(i) * LX + x
-                box[slot, at : at + LY - 1, :] = post3[i, x, 1:LY, :]
-                box[slot, at + LY - 1 : at + LY, :] = rows[high_slot, source : source + 1, :]
-    near[...] = box[0]
-    far[...] = box[1]
-
-
-def momentum_kernel(post3, y_far, y_near, x_far, x_near, out, rows, cols, work):
-    odd_y = lax.rem(lax.axis_index(GY), 2)
-    odd_x = lax.rem(lax.axis_index(GX), 2)
-    rows[0] = y_near[...]
-    rows[1] = y_far[...]
-    cols[0] = x_near[...]
-    cols[1] = x_far[...]
-    for i in range(1, 19):
-        for x in range(LX):
-            work[i, x + 1, ROW0 : ROW0 + LY, :] = post3[i, x]
-    for k, i in enumerate(UP):
-        for x in range(LX):
-            at = k * LX + x
-            work[i, x + 1, ROW0 - 1 : ROW0, :] = rows[1 - odd_y, at : at + 1, :]
-    for k, i in enumerate(DOWN):
-        for x in range(LX):
-            at = k * LX + x
-            work[i, x + 1, ROW0 + LY : ROW0 + LY + 1, :] = rows[odd_y, at : at + 1, :]
-    for k, i in enumerate(RIGHT):
-        work[i, 0, ROW0 - CY[i] : ROW0 - CY[i] + LY, :] = cols[1 - odd_x, k * LY : k * LY + LY, :]
-    for k, i in enumerate(LEFT):
-        work[i, LX + 1, ROW0 - CY[i] : ROW0 - CY[i] + LY, :] = cols[odd_x, k * LY : k * LY + LY, :]
+    for ch in range(19, CHANNELS):
+        for x in range(-1, LX + 1):
+            near_aux[ch - 19, x + 1, 0 : LY + 2, :] = packed(ch, x)[REACH - 1 : REACH + 1 + LY]
+    save.wait()
+
+
+def momentum_kernel(state, aux, out, work):
+    n = LY + 2
+    for x in range(-1, LX + 1):
+        f = arrive(state, x + REACH - 1, STATE_ROW0 - 1, n)
+        lab, *force = [aux[ch, x + 1, 0:n, :] for ch in range(4)]
+        post, _ = collide(f, lab, force, PHASES[3])
+        for i in range(1, 19):
+            work[i, x + 1, 0:n, :] = post[i]
     for x in range(LX):
-        f = [None] + [
-            spin(work[i, x + 1 - CX[i], ROW0 - CY[i] : ROW0 - CY[i] + LY, :], i) for i in range(1, 19)
-        ]
+        f = [None] + [spin(work[i, x + 1 - CX[i], 1 - CY[i] : 1 - CY[i] + LY, :], i) for i in range(1, 19)]
         for axis in range(3):
             total = None
             for i in range(1, 19, 2):
@@ -501,16 +456,21 @@
             out[a, 0, y : y + 1, :] = value[:, :SZ]
 
 
-def call(body, outs, scratch, cost, limit=16, place=pltpu.VMEM, more=()):
-    shapes = [jax.ShapeDtypeStruct(s, jnp.float32) for s in outs]
-    spec = pl.BlockSpec(memory_space=pltpu.VMEM)
+def call(body, outs, scratch, cost, limit=16, place=pltpu.VMEM, more=(), outside=0):
+    shapes = [
+        pltpu.HBM(s, jnp.float32) if k < outside else jax.ShapeDtypeStruct(s, jnp.float32)
+        for k, s in enumerate(outs)
+    ]
+    specs = [
+        pl.BlockSpec(memory_space=pltpu.HBM if k < outside else pltpu.VMEM) for k in range(len(outs))
+    ]
 
     def run(*args):
         return pl.pallas_call(
             body,
             out_shape=shapes,
             in_specs=[pl.BlockSpec(memory_space=place)] * len(args),
-            out_specs=[spec] * len(shapes),
+            out_specs=specs,
             scratch_shapes=[pltpu.VMEM(s, jnp.float32) for s in scratch] + list(more),
             compiler_params=pltpu.CompilerParams(vmem_limit_bytes=limit << 20),
             cost_estimate=pl.CostEstimate(flops=cost, bytes_accessed=cost, transcendentals=0),
@@ -553,21 +513,25 @@
     (packs,) = call(
         own_kernel, [(CHANNELS, LX, PACK, NZ)], [(2, Y_ROWS, NZ)], 2_000_000
     )(cells, y_far, y_near)
-    post3, spread, far, near = call(
+    state_shape = (19, LX + 2 * REACH - 2, STATE_ROWS, NZ)
+    state, aux, spread = call(
         third_kernel,
-        [(19, LX, LY, NZ), (groups, 8, NZ), (EDGE_Y_ROWS, NZ), (EDGE_Y_ROWS, NZ)],
+        [state_shape, (4, LX + 2, STATE_ROWS, NZ), (groups, 8, NZ)],
         [
             (2, X_ROWS, NZ),
             (19, LX + 2 * REACH, WORK_ROWS, NZ),
-            (19, LX + 2, WORK_ROWS, NZ),
+            state_shape,
             (12, 16, NZ),
-            (2, EDGE_Y_ROWS, NZ),
         ],
         20_000_000,
+        more=[pltpu.SemaphoreType.DMA(())],
+        outside=1,
     )(cells, total, packs, x_far, x_near)
     blocks = lax.all_to_all(spread, "cy", 0, 0, tiled=False)
-    ey_far, ey_near = swap(far, near, GY)
-    blocks, ey_far, ey_near = lax.optimization_barrier((blocks, ey_far, ey_near))
+    (momentum,) = call(
+        momentum_kernel, [(3, LX, LY, NZ)], [(19, LX + 2, STATE_ROWS, NZ)], 10_000_000
+    )(state, aux)
+    blocks, momentum = lax.optimization_barrier((blocks, momentum))
     table, starts, imaginary = operator_table(nx, 2 * ny)
     (parts,) = call(
         functools.partial(solve_kernel, starts, imaginary, ny),
@@ -576,19 +540,6 @@
         10_000_000,
     )(blocks, table)
     parts = lax.all_to_all(parts, ("zl", "core", "zh", "cx"), 0, 0, tiled=False)
-    far, near = call(
-        edge_kernel,
-        [(EDGE_X_ROWS, NZ), (EDGE_X_ROWS, NZ)],
-        [(2, EDGE_Y_ROWS, NZ), (2, EDGE_X_ROWS, NZ)],
-        200_000,
-    )(post3, ey_far, ey_near)
-    ex_far, ex_near = swap(far, near, GX)
-    (momentum,) = call(
-        momentum_kernel,
-        [(3, LX, LY, NZ)],
-        [(2, EDGE_Y_ROWS, NZ), (2, EDGE_X_ROWS, NZ), (19, LX + 2, WORK_ROWS, NZ)],
-        1_000_000,
-    )(post3, ey_far, ey_near, ex_far, ex_near)
     (running,) = call(last_kernel, [(3, 1, 2, SZ)], [], 100_000)(parts)
     return momentum, running
 

time: 78.8 us -> 78 us (0.990)
  starting transfers between devices: 61.7 us -> 32.7 us
  blocking collectives: 0 us -> 19.7 us
  waiting for transfers between devices: 8.4 us -> 15.2 us
  local copies, waits for them, and re-layouts: 0.01 us -> 1.3 us
    all_to_all x0 -> x1, blocking collectives: none -> 19.7 us  [local(): parts = lax.all_to_all(parts, ('zl', 'core', 'zh', 'cx'), 0, 0, tiled=False)]
    ppermute x4 -> x2, starting transfers between devices: 30 us -> 18.5 us  [swap(): lax.ppermute(far, axis, far_pairs)]
    all_to_all x1 -> x0, starting transfers between devices: 9.29 us -> none  [local(): parts = lax.all_to_all(parts, ('zl', 'core', 'zh', 'cx'), 0, 0, tiled=False)]
    ppermute x4 -> x2, starting transfers between devices: 15.6 us -> 7.33 us  [swap(): lax.ppermute(near, axis, near_pairs)]
    ppermute x4 -> x2, waiting for transfers between devices: 4.23 us -> 10.1 us  [swap(): lax.ppermute(far, axis, far_pairs)]
    all_to_all x1, waiting for transfers between devices: 0.01 us -> 4.58 us  [local(): blocks = lax.all_to_all(spread, 'cy', 0, 0, tiled=False)]
    ppermute x4 -> x2, waiting for transfers between devices: 4.17 us -> 0.5 us  [swap(): lax.ppermute(near, axis, near_pairs)]
    unnamed x2 -> x4, local copies, waits for them, and re-layouts: 0.01 us -> 1.3 us
  transfers between devices with their start and end apart: 10 -> 5, of which waited for: 6 -> 4; matrix products, arithmetic and copies ran while one was open for 0% -> 0% of each run, Pallas kernels for 1% -> 2%
where the time goes in v4:
time: 78 us; the launch traced here: 77.6 us
  starting transfers between devices  32.7 us (42%)
  blocking collectives  19.7 us (25%)
  waiting for transfers between devices  15.2 us (19%)
  Pallas kernels  8.08 us (10%)
  local copies, waits for them, and re-layouts  1.3 us (2%)
    all_to_all x1, blocking collectives, local(): parts = lax.all_to_all(parts, ('zl', 'core', 'zh', 'cx'), 0, 0, tiled=False)  19.7 us
    ppermute x2, starting transfers between devices, swap(): lax.ppermute(far, axis, far_pairs)  18.5 us
    ppermute x2, waiting for transfers between devices, swap(): lax.ppermute(far, axis, far_pairs)  10.1 us
    pallas_call x7, Pallas kernels, run(): pl.pallas_call(body, out_shape=shapes, in_specs=[pl.BlockSpec(memory_spac...  8.08 us
    ppermute x2, starting transfers between devices, swap(): lax.ppermute(near, axis, near_pairs)  7.33 us
    all_to_all x1, starting transfers between devices, local(): blocks = lax.all_to_all(spread, 'cy', 0, 0, tiled=False)  6.83 us
    all_to_all x1, waiting for transfers between devices, local(): blocks = lax.all_to_all(spread, 'cy', 0, 0, tiled=False)  4.58 us
  transfers between devices with their start and end apart: 5, of which 4 were waited for; matrix products, arithmetic and copies ran while one was open for 0% of the time, Pallas kernels for 2%

profile of v4, /device:TPU:1, one launch (start us, length us, event | category | flops | bytes accessed | tf_op | source)
XLA Modules:
  0.0 77.6 jit_solution(15938871998236579949)
XLA Ops:
  0.6 1.2 %shard_map.59 = (f32[23,4,8,128]{3,2,1,0:T(8,128)S(1)}, f32[6,8,128]{2,1,0:T(8,128)S(1)}, f32[280,128]{1,0:T(8,128)S(1)}, f32[280,128]{1,0:T(8,128)S(1)}) custom-call(f32[19,4,8,128]{3,2,1,0:T(8,128)} %pops_in.1, s32[4,8,128]{2,1,0:T(8,128)} %label_in.1, f32[3,4,8,128]{3,2,1,0:T(8,128)} %drive_in.1), custom_call_target="tpu_custom_call" | custom-call | flops 2000000 | bytes 2000000 | tf_op jit(solution)/shard_map/pallas_call | solution.py:469
  1.9 13.7 %collective-permute-start = (f32[280,128]{1,0:T(8,128)S(1)}, f32[280,128]{1,0:T(8,128)S(1)}, u32[]{:S(2)}, u32[]{:S(2)}) collective-permute-start(f32[280,128]{1,0:T(8,128)S(1)} %get-tuple-element.15), channel_id=1, source_target_pairs={{0,7},{1,2},{2,1},{3,4},{4,3},{5,6},{6,5},{7,0},{8,15},{9,10},{10,... | collective-permute-start | bytes 430088 | tf_op jit(solution)/shard_map/ppermute | solution.py:486
  15.5 1.9 %collective-permute-start.1 = (f32[280,128]{1,0:T(8,128)S(1)}, f32[280,128]{1,0:T(8,128)S(1)}, u32[]{:S(2)}, u32[]{:S(2)}) collective-permute-start(f32[280,128]{1,0:T(8,128)S(1)} %get-tuple-element.16), channel_id=1, source_target_pairs={{0,1},{1,0},{2,3},{3,2},{4,5},{5,4},{6,7},{7,6},{8,9},{9,8},{10,11... | collective-permute-start | bytes 430088 | tf_op jit(solution)/shard_map/ppermute | solution.py:486
  17.5 3.8 %collective-permute-done.got_far = f32[280,128]{1,0:T(8,128)S(1)} collective-permute-done((f32[280,128]{1,0:T(8,128)S(1)}, f32[280,128]{1,0:T(8,128)S(1)}, u32[]{:S(2)}, u32[]{:S(2)}) %collective-permute-start) | collective-permute-done | bytes 143392 | tf_op jit(solution)/shard_map/ppermute | solution.py:486
  21.2 0.5 collective-permute-done.1.got_near
  21.7 0.2 shard_map.61
  22.0 4.9 %collective-permute-start.2 = (f32[968,128]{1,0:T(8,128)S(1)}, f32[968,128]{1,0:T(8,128)S(1)}, u32[]{:S(2)}, u32[]{:S(2)}) collective-permute-start(f32[968,128]{1,0:T(8,128)S(1)} %get-tuple-element.17), channel_id=1, source_target_pairs={{0,504},{8,16},{16,8},{24,32},{32,24},{40,48},{48,40},{56,64},{64,... | collective-permute-start | bytes 1486856 | tf_op jit(solution)/shard_map/ppermute | solution.py:486
  26.8 0.0 copy-start
  26.8 5.4 %collective-permute-start.3 = (f32[968,128]{1,0:T(8,128)S(1)}, f32[968,128]{1,0:T(8,128)S(1)}, u32[]{:S(2)}, u32[]{:S(2)}) collective-permute-start(f32[968,128]{1,0:T(8,128)S(1)} %get-tuple-element.18), channel_id=1, source_target_pairs={{0,8},{8,0},{16,24},{24,16},{32,40},{40,32},{48,56},{56,48},{64,72... | collective-permute-start | bytes 1486856 | tf_op jit(solution)/shard_map/ppermute | solution.py:486
  32.3 0.1 shard_map.60.packs
  32.4 6.3 %collective-permute-done.2.x_far = f32[968,128]{1,0:T(8,128)S(1)} collective-permute-done((f32[968,128]{1,0:T(8,128)S(1)}, f32[968,128]{1,0:T(8,128)S(1)}, u32[]{:S(2)}, u32[]{:S(2)}) %collective-permute-start.2) | collective-permute-done | bytes 495648 | tf_op jit(solution)/shard_map/ppermute | solution.py:486
  38.7 0.0 collective-permute-done.3.x_near
  38.7 3.2 %shard_map.62 = (f32[19,8,16,128]{3,2,1,0:T(8,128)}, f32[4,6,16,128]{3,2,1,0:T(8,128)S(1)}, f32[8,8,128]{2,1,0:T(8,128)}) custom-call(f32[23,4,8,128]{3,2,1,0:T(8,128)S(1)} %get-tuple-element.13.cells, f32[6,8,128]{2,1,0:T(8,128)S(1)} %get-tuple-element.14.total, f32[23,4,16,128]{3,2,1,0:T(8,128)S(1)} %shard_map.60.packs, ...), custom_call_target="tpu_custom_call" | custom-call | flops 20000000 | bytes 20000000 | tf_op jit(solution)/shard_map/pallas_call | solution.py:469
  41.9 6.8 %all-to-all-start = ((f32[8,8,128]{2,1,0:T(8,128)}), f32[8,8,128]{2,1,0:T(8,128)S(1)}, u32[]{:S(2)}, u32[]{:S(2)}) async-start(f32[8,8,128]{2,1,0:T(8,128)} %get-tuple-element.19), calls=%async_computation | async-start | bytes 65536 | tf_op jit(solution)/shard_map/all_to_all | solution.py:530
  48.8 0.0 copy-start.1
  48.8 1.3 %copy-done.1 = f32[19,8,16,128]{3,2,1,0:T(8,128)S(1)} copy-done((f32[19,8,16,128]{3,2,1,0:T(8,128)S(1)}, f32[19,8,16,128]{3,2,1,0:T(8,128)}, u32[]{:S(2)}) %copy-start.1) | copy-done | bytes 1245208
  50.1 1.1 %shard_map.63 = f32[3,4,8,128]{3,2,1,0:T(8,128)} custom-call(f32[19,8,16,128]{3,2,1,0:T(8,128)S(1)} %copy-done.1, f32[4,6,16,128]{3,2,1,0:T(8,128)S(1)} %get-tuple-element.21.aux), custom_call_target="tpu_custom_call" | custom-call | flops 10000000 | bytes 10000000 | tf_op jit(solution)/shard_map/pallas_call | solution.py:469
  51.1 4.6 %all-to-all-done.blocks = f32[8,8,128]{2,1,0:T(8,128)S(1)} async-done(((f32[8,8,128]{2,1,0:T(8,128)}), f32[8,8,128]{2,1,0:T(8,128)S(1)}, u32[]{:S(2)}, u32[]{:S(2)}) %all-to-all-start) | async-done | bytes 32800 | tf_op jit(solution)/shard_map/all_to_all | solution.py:530
  55.7 0.0 copy-done
  55.7 1.5 %shard_map.64 = f32[64,2,128]{2,1,0:T(2,128)S(1)} custom-call(f32[8,8,128]{2,1,0:T(8,128)S(1)} %all-to-all-done.blocks, f32[4776,128]{1,0:T(8,128)S(1)} %copy-done), custom_call_target="tpu_custom_call" | custom-call | flops 10000000 | bytes 10000000 | tf_op jit(solution)/shard_map/pallas_call | solution.py:469
  57.2 19.7 %all_to_all.10.parts = f32[64,2,128]{2,1,0:T(2,128)S(1)} all-to-all(f32[64,2,128]{2,1,0:T(2,128)S(1)} %shard_map.64), channel_id=1, replica_groups=mesh['cy'=8,'zl'=4,'core'=2,'zh'=2,'cx'=4] {'zl','core','zh','cx'}, dimensions={0} | all-to-all | bytes 131072 | tf_op jit(solution)/shard_map/all_to_all | solution.py:542
  76.9 0.7 shard_map.65
Async XLA Ops:
  1.9 19.4 %collective-permute-start = (f32[280,128]{1,0:T(8,128)S(1)}, f32[280,128]{1,0:T(8,128)S(1)}, u32[]{:S(2)}, u32[]{:S(2)}) collective-permute-start(f32[280,128]{1,0:T(8,128)S(1)} %get-tuple-element.15), channel_id=1, source_target_pairs={{0,7},{1,2},{2,1},{3,4},{4,3},{5,6},{6,5},{7,0},{8,15},{9,10},{10,... | collective-permute-start | bytes 430088 | tf_op jit(solution)/shard_map/ppermute | solution.py:486
  15.5 6.2 %collective-permute-start.1 = (f32[280,128]{1,0:T(8,128)S(1)}, f32[280,128]{1,0:T(8,128)S(1)}, u32[]{:S(2)}, u32[]{:S(2)}) collective-permute-start(f32[280,128]{1,0:T(8,128)S(1)} %get-tuple-element.16), channel_id=1, source_target_pairs={{0,1},{1,0},{2,3},{3,2},{4,5},{5,4},{6,7},{7,6},{8,9},{9,8},{10,11... | collective-permute-start | bytes 430088 | tf_op jit(solution)/shard_map/ppermute | solution.py:486
  22.0 16.7 %collective-permute-start.2 = (f32[968,128]{1,0:T(8,128)S(1)}, f32[968,128]{1,0:T(8,128)S(1)}, u32[]{:S(2)}, u32[]{:S(2)}) collective-permute-start(f32[968,128]{1,0:T(8,128)S(1)} %get-tuple-element.17), channel_id=1, source_target_pairs={{0,504},{8,16},{16,8},{24,32},{32,24},{40,48},{48,40},{56,64},{64,... | collective-permute-start | bytes 1486856 | tf_op jit(solution)/shard_map/ppermute | solution.py:486
  26.8 28.9 %copy-start = (f32[4776,128]{1,0:T(8,128)S(1)}, f32[4776,128]{1,0:T(8,128)}, u32[]{:S(2)}) copy-start(f32[4776,128]{1,0:T(8,128)} %constant.2.clone.table) | copy-start | bytes 7335940
  26.8 11.8 %collective-permute-start.3 = (f32[968,128]{1,0:T(8,128)S(1)}, f32[968,128]{1,0:T(8,128)S(1)}, u32[]{:S(2)}, u32[]{:S(2)}) collective-permute-start(f32[968,128]{1,0:T(8,128)S(1)} %get-tuple-element.18), channel_id=1, source_target_pairs={{0,8},{8,0},{16,24},{24,16},{32,40},{40,32},{48,56},{56,48},{64,72... | collective-permute-start | bytes 1486856 | tf_op jit(solution)/shard_map/ppermute | solution.py:486
  41.9 13.8 %all-to-all-start = ((f32[8,8,128]{2,1,0:T(8,128)}), f32[8,8,128]{2,1,0:T(8,128)S(1)}, u32[]{:S(2)}, u32[]{:S(2)}) async-start(f32[8,8,128]{2,1,0:T(8,128)} %get-tuple-element.19), calls=%async_computation | async-start | bytes 65536 | tf_op jit(solution)/shard_map/all_to_all | solution.py:530
  48.8 1.3 %copy-start.1 = (f32[19,8,16,128]{3,2,1,0:T(8,128)S(1)}, f32[19,8,16,128]{3,2,1,0:T(8,128)}, u32[]{:S(2)}) copy-start(f32[19,8,16,128]{3,2,1,0:T(8,128)} %get-tuple-element.20.state) | copy-start | bytes 3735556

commit v5 on v4

--- a/solution.py
+++ b/solution.py
@@ -51,14 +51,15 @@
 GROUP = 8
 
 
-REACH = STEPS - 1
+REACH_X = STEPS - 2
+REACH_Y = STEPS - 1
 
 
 def pack_y(sign):
     out, at = [], 0
     for x in range(LX):
         for ch in range(CHANNELS):
-            n = REACH + sign * CY[ch]
+            n = REACH_Y + sign * CY[ch]
             out.append((ch, x, LY - n if sign > 0 else 0, n, at))
             at += n
     return out, -(-at // 8) * 8
@@ -67,14 +68,14 @@
 def pack_x(sign):
     out, at = [], 0
     for ch in range(CHANNELS):
-        n = REACH + sign * CX[ch]
+        n = REACH_X + sign * CX[ch]
         for x in range(LX - n, LX) if sign > 0 else range(n):
-            out.append((ch, x, REACH + CY[ch], REACH - CY[ch], at))
-            at += 2 * REACH + LY
+            out.append((ch, x, REACH_Y + CY[ch], REACH_Y - CY[ch], at))
+            at += 2 * REACH_Y + LY
     return out, -(-at // 8) * 8
 
 
-SPAN = 2 * REACH + LY
+SPAN = 2 * REACH_Y + LY
 Y_UP, Y_ROWS = pack_y(1)
 Y_DOWN, _ = pack_y(-1)
 X_RIGHT, X_ROWS = pack_x(1)
@@ -83,6 +84,9 @@
 Y_DOWN_AT = {(ch, x): (n, at) for ch, x, _, n, at in Y_DOWN}
 X_RIGHT_AT = {(ch, x): at for ch, x, _, _, at in X_RIGHT}
 X_LEFT_AT = {(ch, x): at for ch, x, _, _, at in X_LEFT}
+RIGHT = [i for i in range(19) if CX[i] == 1]
+LEFT = [i for i in range(19) if CX[i] == -1]
+EDGE_ROWS = len(RIGHT) * LY
 
 
 def collide(f, label, drive, phase):
@@ -187,8 +191,6 @@
 PACK = 16
 ROW0 = 8
 WORK_ROWS = 24
-STATE_ROW0 = 4
-STATE_ROWS = 16
 
 
 def own_kernel(cells, got_far, got_near, packs, rows):
@@ -216,7 +218,7 @@
 
 
 def third_kernel(
-    cells, total, packs, x_far, x_near, state, near_aux, spread, cols, one, two, sums, sem
+    cells, total, packs, x_far, x_near, post3, spread, edge_far, edge_near, cols, one, two, sums, box
 ):
     odd_x = lax.rem(lax.axis_index(GX), 2)
     left_slot, right_slot = 1 - odd_x, odd_x
@@ -235,40 +237,27 @@
     def add(first, second):
         return second if first is None else [a + b for a, b in zip(first, second)]
 
-    low = ROW0 - REACH
-    kept = None
-    for x in range(-REACH, LX + REACH):
-        f = [spin(packed(i, x - CX[i]), i) for i in range(19)]
-        post, stress = collide(f, packed(19, x), [packed(20 + axis, x) for axis in range(3)], PHASES[1])
-        for i in range(19):
-            one[i, x + REACH, low : low + SPAN, :] = post[i]
-        if 0 <= x < LX:
-            kept = add(kept, stress)
-    for k in range(6):
-        sums[k, 0:SPAN, :] = kept[k]
-    low, n = ROW0 - (REACH - 1), LY + 2 * (REACH - 1)
-    to = STATE_ROW0 - (REACH - 1)
-    kept = None
-    for x in range(1 - REACH, LX + REACH - 1):
-        f = arrive(one, x + REACH, low, n)
-        lab, *force = [packed(ch, x)[1 : 1 + n] for ch in range(19, CHANNELS)]
-        post, stress = collide(f, lab, force, PHASES[2])
-        for i in range(19):
-            two[i, x + REACH - 1, to : to + n, :] = post[i]
-        if 0 <= x < LX:
-            kept = add(kept, stress)
-    save = pltpu.make_async_copy(two, state, sem)
-    save.start()
-    for k in range(6):
-        sums[6 + k, 0:n, :] = kept[k]
-    last = [
-        total[k] + sums[k, REACH : REACH + LY, :] + sums[6 + k, REACH - 1 : REACH - 1 + LY, :]
-        for k in range(6)
-    ]
-    for x in range(LX):
-        f = arrive(two, x + REACH - 1, STATE_ROW0, LY)
-        _, stress = collide(f, cells[19, x], [cells[20 + axis, x] for axis in range(3)], PHASES[3])
-        last = add(last, stress)
+    last = [total[k] for k in range(6)]
+    for step, source, target in ((1, None, one), (2, one, two), (3, two, post3)):
+        near, wide = REACH_X + 1 - step, REACH_Y + 1 - step
+        n = LY + 2 * wide
+        to = 0 if step == 3 else ROW0 - wide
+        kept = None
+        for x in range(-near, LX + near):
+            if step == 1:
+                f = [spin(packed(i, x - CX[i]), i) for i in range(19)]
+            else:
+                f = arrive(source, x + near + 1, ROW0 - wide, n)
+            at = REACH_Y - wide
+            lab, *force = [packed(ch, x)[at : at + n] for ch in range(19, CHANNELS)]
+            post, stress = collide(f, lab, force, PHASES[step])
+            for i in range(19):
+                target[i, x + near, to : to + n, :] = post[i]
+            if 0 <= x < LX:
+                kept = add(kept, stress)
+        for k in range(6):
+            sums[6 * step - 6 + k, 0:n, :] = kept[k]
+        last = [last[k] + sums[6 * step - 6 + k, wide : wide + LY, :] for k in range(6)]
     stacked = jnp.concatenate(last, axis=0)
     r = lax.broadcasted_iota(jnp.int32, (16, 48), 0)
     c = lax.broadcasted_iota(jnp.int32, (16, 48), 1)
@@ -289,22 +278,30 @@
         )
     for d in range(spread.shape[0]):
         spread[d] = slow
-    for ch in range(19, CHANNELS):
-        for x in range(-1, LX + 1):
-            near_aux[ch - 19, x + 1, 0 : LY + 2, :] = packed(ch, x)[REACH - 1 : REACH + 1 + LY]
-    save.wait()
-
-
-def momentum_kernel(state, aux, out, work):
-    n = LY + 2
-    for x in range(-1, LX + 1):
-        f = arrive(state, x + REACH - 1, STATE_ROW0 - 1, n)
-        lab, *force = [aux[ch, x + 1, 0:n, :] for ch in range(4)]
-        post, _ = collide(f, lab, force, PHASES[3])
+    for slot, comps, x in ((odd_x, RIGHT, LX - 1), (1 - odd_x, LEFT, 0)):
+        for k, i in enumerate(comps):
+            box[slot, k * LY : k * LY + LY, :] = post3[i, x, 1 - CY[i] : 1 - CY[i] + LY, :]
+    edge_near[...] = box[0]
+    edge_far[...] = box[1]
+
+
+def momentum_kernel(post3, x_far, x_near, out, cols):
+    odd_x = lax.rem(lax.axis_index(GX), 2)
+    cols[0] = x_near[...]
+    cols[1] = x_far[...]
+    for x in range(LX):
+        f = [None]
         for i in range(1, 19):
-            work[i, x + 1, 0:n, :] = post[i]
-    for x in range(LX):
-        f = [None] + [spin(work[i, x + 1 - CX[i], 1 - CY[i] : 1 - CY[i] + LY, :], i) for i in range(1, 19)]
+            source = x - CX[i]
+            if source < 0:
+                at = RIGHT.index(i) * LY
+                value = cols[1 - odd_x, at : at + LY, :]
+            elif source >= LX:
+                at = LEFT.index(i) * LY
+                value = cols[odd_x, at : at + LY, :]
+            else:
+                value = post3[i, source, 1 - CY[i] : 1 - CY[i] + LY, :]
+            f.append(spin(value, i))
         for axis in range(3):
             total = None
             for i in range(1, 19, 2):
@@ -456,21 +453,16 @@
             out[a, 0, y : y + 1, :] = value[:, :SZ]
 
 
-def call(body, outs, scratch, cost, limit=16, place=pltpu.VMEM, more=(), outside=0):
-    shapes = [
-        pltpu.HBM(s, jnp.float32) if k < outside else jax.ShapeDtypeStruct(s, jnp.float32)
-        for k, s in enumerate(outs)
-    ]
-    specs = [
-        pl.BlockSpec(memory_space=pltpu.HBM if k < outside else pltpu.VMEM) for k in range(len(outs))
-    ]
+def call(body, outs, scratch, cost, limit=16, place=pltpu.VMEM, more=()):
+    shapes = [jax.ShapeDtypeStruct(s, jnp.float32) for s in outs]
+    spec = pl.BlockSpec(memory_space=pltpu.VMEM)
 
     def run(*args):
         return pl.pallas_call(
             body,
             out_shape=shapes,
             in_specs=[pl.BlockSpec(memory_space=place)] * len(args),
-            out_specs=specs,
+            out_specs=[spec] * len(shapes),
             scratch_shapes=[pltpu.VMEM(s, jnp.float32) for s in scratch] + list(more),
             compiler_params=pltpu.CompilerParams(vmem_limit_bytes=limit << 20),
             cost_estimate=pl.CostEstimate(flops=cost, bytes_accessed=cost, transcendentals=0),
@@ -513,25 +505,24 @@
     (packs,) = call(
         own_kernel, [(CHANNELS, LX, PACK, NZ)], [(2, Y_ROWS, NZ)], 2_000_000
     )(cells, y_far, y_near)
-    state_shape = (19, LX + 2 * REACH - 2, STATE_ROWS, NZ)
-    state, aux, spread = call(
+    post3, spread, far, near = call(
         third_kernel,
-        [state_shape, (4, LX + 2, STATE_ROWS, NZ), (groups, 8, NZ)],
+        [(19, LX, PACK, NZ), (groups, 8, NZ), (EDGE_ROWS, NZ), (EDGE_ROWS, NZ)],
         [
             (2, X_ROWS, NZ),
-            (19, LX + 2 * REACH, WORK_ROWS, NZ),
-            state_shape,
-            (12, 16, NZ),
+            (19, LX + 2 * REACH_X, WORK_ROWS, NZ),
+            (19, LX + 2 * REACH_X - 2, WORK_ROWS, NZ),
+            (18, 16, NZ),
+            (2, EDGE_ROWS, NZ),
         ],
         20_000_000,
-        more=[pltpu.SemaphoreType.DMA(())],
-        outside=1,
     )(cells, total, packs, x_far, x_near)
     blocks = lax.all_to_all(spread, "cy", 0, 0, tiled=False)
+    edge_far, edge_near = swap(far, near, GX)
+    blocks, edge_far, edge_near = lax.optimization_barrier((blocks, edge_far, edge_near))
     (momentum,) = call(
-        momentum_kernel, [(3, LX, LY, NZ)], [(19, LX + 2, STATE_ROWS, NZ)], 10_000_000
-    )(state, aux)
-    blocks, momentum = lax.optimization_barrier((blocks, momentum))
+        momentum_kernel, [(3, LX, LY, NZ)], [(2, EDGE_ROWS, NZ)], 1_000_000
+    )(post3, edge_far, edge_near)
     table, starts, imaginary = operator_table(nx, 2 * ny)
     (parts,) = call(
         functools.partial(solve_kernel, starts, imaginary, ny),
@@ -540,6 +531,7 @@
         10_000_000,
     )(blocks, table)
     parts = lax.all_to_all(parts, ("zl", "core", "zh", "cx"), 0, 0, tiled=False)
+    parts, momentum = lax.optimization_barrier((parts, momentum))
     (running,) = call(last_kernel, [(3, 1, 2, SZ)], [], 100_000)(parts)
     return momentum, running
 

time: 78 us -> 76.6 us (0.982)
  blocking collectives: 19.7 us -> 0 us
  starting transfers between devices: 32.7 us -> 52 us
  local copies, waits for them, and re-layouts: 1.3 us -> 0.01 us
    all_to_all x1 -> x0, blocking collectives: 19.7 us -> none  [local(): parts = lax.all_to_all(parts, ('zl', 'core', 'zh', 'cx'), 0, 0, tiled=False)]
    all_to_all x0 -> x1, starting transfers between devices: none -> 11 us  [local(): parts = lax.all_to_all(parts, ('zl', 'core', 'zh', 'cx'), 0, 0, tiled=False)]
    all_to_all x0 -> x1, waiting for transfers between devices: none -> 8.59 us  [local(): parts = lax.all_to_all(parts, ('zl', 'core', 'zh', 'cx'), 0, 0, tiled=False)]
    ppermute x2 -> x3, starting transfers between devices: 18.5 us -> 23.2 us  [swap(): lax.ppermute(far, axis, far_pairs)]
    all_to_all x1, waiting for transfers between devices: 4.58 us -> 0.01 us  [local(): blocks = lax.all_to_all(spread, 'cy', 0, 0, tiled=False)]
    ppermute x2 -> x3, waiting for transfers between devices: 10.1 us -> 5.97 us  [swap(): lax.ppermute(far, axis, far_pairs)]
    ppermute x2 -> x3, starting transfers between devices: 7.33 us -> 11 us  [swap(): lax.ppermute(near, axis, near_pairs)]
    unnamed x4 -> x2, local copies, waits for them, and re-layouts: 1.3 us -> 0.01 us
  transfers between devices with their start and end apart: 5 -> 8, of which waited for: 4 -> 5; matrix products, arithmetic and copies ran while one was open for 0% -> 0% of each run, Pallas kernels for 2% -> 1%
where the time goes in v5:
time: 76.6 us; the launch traced here: 76.2 us
  starting transfers between devices  52 us (68%)
  waiting for transfers between devices  15.9 us (21%)
  Pallas kernels  7.63 us (10%)
    ppermute x3, starting transfers between devices, swap(): lax.ppermute(far, axis, far_pairs)  23.2 us
    ppermute x3, starting transfers between devices, swap(): lax.ppermute(near, axis, near_pairs)  11 us
    all_to_all x1, starting transfers between devices, local(): parts = lax.all_to_all(parts, ('zl', 'core', 'zh', 'cx'), 0, 0, tiled=False)  11 us
    all_to_all x1, waiting for transfers between devices, local(): parts = lax.all_to_all(parts, ('zl', 'core', 'zh', 'cx'), 0, 0, tiled=False)  8.59 us
    pallas_call x7, Pallas kernels, run(): pl.pallas_call(body, out_shape=shapes, in_specs=[pl.BlockSpec(memory_spac...  7.63 us
    all_to_all x1, starting transfers between devices, local(): blocks = lax.all_to_all(spread, 'cy', 0, 0, tiled=False)  6.82 us
    ppermute x3, waiting for transfers between devices, swap(): lax.ppermute(far, axis, far_pairs)  5.97 us
  transfers between devices with their start and end apart: 8, of which 5 were waited for; matrix products, arithmetic and copies ran while one was open for 0% of the time, Pallas kernels for 1%

profile of v5, /device:TPU:1, one launch (start us, length us, event | category | flops | bytes accessed | tf_op | source)
XLA Modules:
  0.0 76.2 jit_solution(3378201986355556437)
XLA Ops:
  0.6 0.0 copy-start
  0.6 1.4 %shard_map.59 = (f32[23,4,8,128]{3,2,1,0:T(8,128)S(1)}, f32[6,8,128]{2,1,0:T(8,128)S(1)}, f32[280,128]{1,0:T(8,128)S(1)}, f32[280,128]{1,0:T(8,128)S(1)}) custom-call(f32[19,4,8,128]{3,2,1,0:T(8,128)} %pops_in.1, s32[4,8,128]{2,1,0:T(8,128)} %label_in.1, f32[3,4,8,128]{3,2,1,0:T(8,128)} %drive_in.1), custom_call_target="tpu_custom_call" | custom-call | flops 2000000 | bytes 2000000 | tf_op jit(solution)/shard_map/pallas_call | solution.py:461
  2.0 13.7 %collective-permute-start = (f32[280,128]{1,0:T(8,128)S(1)}, f32[280,128]{1,0:T(8,128)S(1)}, u32[]{:S(2)}, u32[]{:S(2)}) collective-permute-start(f32[280,128]{1,0:T(8,128)S(1)} %get-tuple-element.19), channel_id=1, source_target_pairs={{0,7},{1,2},{2,1},{3,4},{4,3},{5,6},{6,5},{7,0},{8,15},{9,10},{10,... | collective-permute-start | bytes 430088 | tf_op jit(solution)/shard_map/ppermute | solution.py:478
  15.7 1.9 %collective-permute-start.1 = (f32[280,128]{1,0:T(8,128)S(1)}, f32[280,128]{1,0:T(8,128)S(1)}, u32[]{:S(2)}, u32[]{:S(2)}) collective-permute-start(f32[280,128]{1,0:T(8,128)S(1)} %get-tuple-element.20), channel_id=1, source_target_pairs={{0,1},{1,0},{2,3},{3,2},{4,5},{5,4},{6,7},{7,6},{8,9},{9,8},{10,11... | collective-permute-start | bytes 430088 | tf_op jit(solution)/shard_map/ppermute | solution.py:478
  17.6 3.8 %collective-permute-done.got_far = f32[280,128]{1,0:T(8,128)S(1)} collective-permute-done((f32[280,128]{1,0:T(8,128)S(1)}, f32[280,128]{1,0:T(8,128)S(1)}, u32[]{:S(2)}, u32[]{:S(2)}) %collective-permute-start) | collective-permute-done | bytes 143392 | tf_op jit(solution)/shard_map/ppermute | solution.py:478
  21.4 0.5 collective-permute-done.1.got_near
  21.9 0.2 shard_map.61
  22.1 4.9 %collective-permute-start.2 = (f32[648,128]{1,0:T(8,128)S(1)}, f32[648,128]{1,0:T(8,128)S(1)}, u32[]{:S(2)}, u32[]{:S(2)}) collective-permute-start(f32[648,128]{1,0:T(8,128)S(1)} %get-tuple-element.21), channel_id=1, source_target_pairs={{0,504},{8,16},{16,8},{24,32},{32,24},{40,48},{48,40},{56,64},{64,... | collective-permute-start | bytes 995336 | tf_op jit(solution)/shard_map/ppermute | solution.py:478
  26.9 5.3 %collective-permute-start.3 = (f32[648,128]{1,0:T(8,128)S(1)}, f32[648,128]{1,0:T(8,128)S(1)}, u32[]{:S(2)}, u32[]{:S(2)}) collective-permute-start(f32[648,128]{1,0:T(8,128)S(1)} %get-tuple-element.22), channel_id=1, source_target_pairs={{0,8},{8,0},{16,24},{24,16},{32,40},{40,32},{48,56},{56,48},{64,72... | collective-permute-start | bytes 995336 | tf_op jit(solution)/shard_map/ppermute | solution.py:478
  32.2 0.1 shard_map.60.packs
  32.3 2.2 %collective-permute-done.2.x_far = f32[648,128]{1,0:T(8,128)S(1)} collective-permute-done((f32[648,128]{1,0:T(8,128)S(1)}, f32[648,128]{1,0:T(8,128)S(1)}, u32[]{:S(2)}, u32[]{:S(2)}) %collective-permute-start.2) | collective-permute-done | bytes 331808 | tf_op jit(solution)/shard_map/ppermute | solution.py:478
  34.5 0.0 collective-permute-done.3.x_near
  34.5 2.4 %shard_map.62 = (f32[19,4,16,128]{3,2,1,0:T(8,128)S(1)}, f32[8,8,128]{2,1,0:T(8,128)}, f32[40,128]{1,0:T(8,128)S(1)}, f32[40,128]{1,0:T(8,128)S(1)}) custom-call(f32[23,4,8,128]{3,2,1,0:T(8,128)S(1)} %get-tuple-element.17.cells, f32[6,8,128]{2,1,0:T(8,128)S(1)} %get-tuple-element.18.total, f32[23,4,16,128]{3,2,1,0:T(8,128)S(1)} %shard_map.60.packs, ...), custom_call_target="tpu_custom_call" | custom-call | flops 20000000 | bytes 20000000 | tf_op jit(solution)/shard_map/pallas_call | solution.py:461
  37.0 6.8 %all-to-all-start = ((f32[8,8,128]{2,1,0:T(8,128)}), f32[8,8,128]{2,1,0:T(8,128)S(1)}, u32[]{:S(2)}, u32[]{:S(2)}) async-start(f32[8,8,128]{2,1,0:T(8,128)} %get-tuple-element.23), calls=%async_computation | async-start | bytes 65536 | tf_op jit(solution)/shard_map/all_to_all | solution.py:520
  43.8 4.7 %collective-permute-start.4 = (f32[40,128]{1,0:T(8,128)S(1)}, f32[40,128]{1,0:T(8,128)S(1)}, u32[]{:S(2)}, u32[]{:S(2)}) collective-permute-start(f32[40,128]{1,0:T(8,128)S(1)} %get-tuple-element.24), channel_id=1, source_target_pairs={{0,504},{8,16},{16,8},{24,32},{32,24},{40,48},{48,40},{56,64},{64,... | collective-permute-start | bytes 61448 | tf_op jit(solution)/shard_map/ppermute | solution.py:478
  48.4 3.8 %collective-permute-start.5 = (f32[40,128]{1,0:T(8,128)S(1)}, f32[40,128]{1,0:T(8,128)S(1)}, u32[]{:S(2)}, u32[]{:S(2)}) collective-permute-start(f32[40,128]{1,0:T(8,128)S(1)} %get-tuple-element.25), channel_id=1, source_target_pairs={{0,8},{8,0},{16,24},{24,16},{32,40},{40,32},{48,56},{56,48},{64,72... | collective-permute-start | bytes 61448 | tf_op jit(solution)/shard_map/ppermute | solution.py:478
  52.3 0.0 collective-permute-done.4.x_far
  52.3 0.8 %collective-permute-done.5.x_near = f32[40,128]{1,0:T(8,128)S(1)} collective-permute-done((f32[40,128]{1,0:T(8,128)S(1)}, f32[40,128]{1,0:T(8,128)S(1)}, u32[]{:S(2)}, u32[]{:S(2)}) %collective-permute-start.5) | collective-permute-done | bytes 20512 | tf_op jit(solution)/shard_map/ppermute | solution.py:478
  53.1 0.0 all-to-all-done.blocks
  53.1 2.1 %shard_map.63 = f32[64,2,128]{2,1,0:T(2,128)} custom-call(f32[8,8,128]{2,1,0:T(8,128)S(1)} %all-to-all-done.blocks, f32[4776,128]{1,0:T(8,128)S(1)} %copy-done), custom_call_target="tpu_custom_call" | custom-call | flops 10000000 | bytes 10000000 | tf_op jit(solution)/shard_map/pallas_call | solution.py:461
  55.2 11.0 %all-to-all-start.1 = ((f32[64,2,128]{2,1,0:T(2,128)}), f32[64,2,128]{2,1,0:T(2,128)S(1)}, u32[]{:S(2)}, u32[]{:S(2)}) async-start(f32[64,2,128]{2,1,0:T(2,128)} %shard_map.63), calls=%async_computation.1 | async-start | bytes 131072 | tf_op jit(solution)/shard_map/all_to_all | solution.py:533
  66.2 0.7 shard_map.64
  66.9 8.6 %all-to-all-done.1.parts = f32[64,2,128]{2,1,0:T(2,128)S(1)} async-done(((f32[64,2,128]{2,1,0:T(2,128)}), f32[64,2,128]{2,1,0:T(2,128)S(1)}, u32[]{:S(2)}, u32[]{:S(2)}) %all-to-all-start.1) | async-done | bytes 65568 | tf_op jit(solution)/shard_map/all_to_all | solution.py:533
  75.5 0.7 shard_map.65
  (1 shorter events, 0.0 us)
Async XLA Ops:
  0.6 52.5 %copy-start = (f32[4776,128]{1,0:T(8,128)S(1)}, f32[4776,128]{1,0:T(8,128)}, u32[]{:S(2)}) copy-start(f32[4776,128]{1,0:T(8,128)} %constant.2.clone.table) | copy-start | bytes 7335940
  2.0 19.4 %collective-permute-start = (f32[280,128]{1,0:T(8,128)S(1)}, f32[280,128]{1,0:T(8,128)S(1)}, u32[]{:S(2)}, u32[]{:S(2)}) collective-permute-start(f32[280,128]{1,0:T(8,128)S(1)} %get-tuple-element.19), channel_id=1, source_target_pairs={{0,7},{1,2},{2,1},{3,4},{4,3},{5,6},{6,5},{7,0},{8,15},{9,10},{10,... | collective-permute-start | bytes 430088 | tf_op jit(solution)/shard_map/ppermute | solution.py:478
  15.7 6.2 %collective-permute-start.1 = (f32[280,128]{1,0:T(8,128)S(1)}, f32[280,128]{1,0:T(8,128)S(1)}, u32[]{:S(2)}, u32[]{:S(2)}) collective-permute-start(f32[280,128]{1,0:T(8,128)S(1)} %get-tuple-element.20), channel_id=1, source_target_pairs={{0,1},{1,0},{2,3},{3,2},{4,5},{5,4},{6,7},{7,6},{8,9},{9,8},{10,11... | collective-permute-start | bytes 430088 | tf_op jit(solution)/shard_map/ppermute | solution.py:478
  22.1 12.5 %collective-permute-start.2 = (f32[648,128]{1,0:T(8,128)S(1)}, f32[648,128]{1,0:T(8,128)S(1)}, u32[]{:S(2)}, u32[]{:S(2)}) collective-permute-start(f32[648,128]{1,0:T(8,128)S(1)} %get-tuple-element.21), channel_id=1, source_target_pairs={{0,504},{8,16},{16,8},{24,32},{32,24},{40,48},{48,40},{56,64},{64,... | collective-permute-start | bytes 995336 | tf_op jit(solution)/shard_map/ppermute | solution.py:478
  26.9 7.6 %collective-permute-start.3 = (f32[648,128]{1,0:T(8,128)S(1)}, f32[648,128]{1,0:T(8,128)S(1)}, u32[]{:S(2)}, u32[]{:S(2)}) collective-permute-start(f32[648,128]{1,0:T(8,128)S(1)} %get-tuple-element.22), channel_id=1, source_target_pairs={{0,8},{8,0},{16,24},{24,16},{32,40},{40,32},{48,56},{56,48},{64,72... | collective-permute-start | bytes 995336 | tf_op jit(solution)/shard_map/ppermute | solution.py:478
  37.0 16.2 %all-to-all-start = ((f32[8,8,128]{2,1,0:T(8,128)}), f32[8,8,128]{2,1,0:T(8,128)S(1)}, u32[]{:S(2)}, u32[]{:S(2)}) async-start(f32[8,8,128]{2,1,0:T(8,128)} %get-tuple-element.23), calls=%async_computation | async-start | bytes 65536 | tf_op jit(solution)/shard_map/all_to_all | solution.py:520
  43.8 8.5 %collective-permute-start.4 = (f32[40,128]{1,0:T(8,128)S(1)}, f32[40,128]{1,0:T(8,128)S(1)}, u32[]{:S(2)}, u32[]{:S(2)}) collective-permute-start(f32[40,128]{1,0:T(8,128)S(1)} %get-tuple-element.24), channel_id=1, source_target_pairs={{0,504},{8,16},{16,8},{24,32},{32,24},{40,48},{48,40},{56,64},{64,... | collective-permute-start | bytes 61448 | tf_op jit(solution)/shard_map/ppermute | solution.py:478
  48.4 4.7 %collective-permute-start.5 = (f32[40,128]{1,0:T(8,128)S(1)}, f32[40,128]{1,0:T(8,128)S(1)}, u32[]{:S(2)}, u32[]{:S(2)}) collective-permute-start(f32[40,128]{1,0:T(8,128)S(1)} %get-tuple-element.25), channel_id=1, source_target_pairs={{0,8},{8,0},{16,24},{24,16},{32,40},{40,32},{48,56},{56,48},{64,72... | collective-permute-start | bytes 61448 | tf_op jit(solution)/shard_map/ppermute | solution.py:478
  55.2 20.3 %all-to-all-start.1 = ((f32[64,2,128]{2,1,0:T(2,128)}), f32[64,2,128]{2,1,0:T(2,128)S(1)}, u32[]{:S(2)}, u32[]{:S(2)}) async-start(f32[64,2,128]{2,1,0:T(2,128)} %shard_map.63), calls=%async_computation.1 | async-start | bytes 131072 | tf_op jit(solution)/shard_map/all_to_all | solution.py:533

commit v6 on v5

--- a/solution.py
+++ b/solution.py
@@ -350,8 +350,8 @@
             gains[a, c, :, :modes] = line.real if odd_x else line.imag
             if odd_x:
                 twists[a, c, :modes] = line.imag[0]
-    gains = np.concatenate([gains, gains[:, :, :GROUP]], axis=2)
-    gains = gains.reshape(3, 6, sx + GROUP, TILES, NZ).transpose(0, 1, 3, 2, 4)
+    gains = gains.reshape(3, 6, sx // GROUP, GROUP, TILES, NZ).transpose(0, 1, 4, 3, 2, 5)
+    gains = np.concatenate([gains[:, :, :, :, -1:], gains], axis=4)
     twists = twists.reshape(3, 8, TILES, NZ).transpose(0, 2, 1, 3)
     y = np.repeat(np.arange(2), SZ)
     z = np.tile(np.arange(SZ), 2)
@@ -371,61 +371,68 @@
     return table, tuple(int(start) for start in starts[:4]), tuple(imaginary)
 
 
-def solve_kernel(starts, imaginary, pairs, blocks, table, out, part, field):
-    groups = blocks.shape[0]
-    sx = groups * GROUP
+def solve_kernel(starts, imaginary, pairs, groups, blocks, table, out, part, hat, field):
     at_gain, at_twist, at_turn, at_forward = starts
     me = lax.axis_index("cy")
     mine = lax.rem(lax.axis_index(GX), GROUP)
-    pair = lax.axis_index(GY)
+    upper = lax.axis_index("zh")
+    column = lax.axis_index("cx")
+    columns = pairs // 2
     forward = jnp.concatenate(
         [table[at_forward + k * NZ : at_forward + (k + 1) * NZ, :] for k in range(2 * TILES)], axis=1
     )
     part[...] = jnp.dot(
-        blocks[...].reshape(groups * 8, NZ),
+        blocks[...].reshape(2 * GROUP * 8, NZ),
         forward,
         precision=HIGHEST,
         preferred_element_type=jnp.float32,
-    ).reshape(groups, 8, 2 * TILES * NZ)
-
-    row = lax.broadcasted_iota(jnp.int32, (GROUP, NZ), 0)
-    alternate = jnp.where(lax.rem(row + mine, 2) == 0, 1.0, -1.0)
-    starts_x = [lax.rem(GROUP * (me + groups - g) + sx - mine, sx) for g in range(groups)]
+    ).reshape(2 * GROUP, 8, 2 * TILES * NZ)
+    half = [table[at_turn + columns * (2 * TILES) + k : at_turn + columns * (2 * TILES) + k + 1, :] for k in range(TILES)]
+    half = jnp.concatenate(half + half, axis=1)
+    for r in range(GROUP):
+        hat[r] = part[2 * r + upper] + half * part[2 * r + 1 - upper]
+
+    sign = (1 - 2 * lax.rem(mine, 2)).astype(jnp.float32)
     for k in range(TILES):
         re_lanes = slice(k * NZ, (k + 1) * NZ)
         im_lanes = slice((TILES + k) * NZ, (TILES + k + 1) * NZ)
-        all_re = part[0, :, re_lanes]
-        all_im = part[0, :, im_lanes]
-        for g in range(1, groups):
-            all_re = all_re + part[g, :, re_lanes]
-            all_im = all_im + part[g, :, im_lanes]
+        all_re = hat[0, :, re_lanes]
+        all_im = hat[0, :, im_lanes]
+        for r in range(1, GROUP):
+            all_re = all_re + hat[r, :, re_lanes] if r % 2 == 0 else all_re - hat[r, :, re_lanes]
+            all_im = all_im + hat[r, :, im_lanes] if r % 2 == 0 else all_im - hat[r, :, im_lanes]
         re, im = [], []
         for a in range(3):
             at = at_twist + (a * TILES + k) * 8
-            wave = table[at : at + 8, :]
-            re.append(-alternate * jnp.sum(wave * all_im, axis=0, keepdims=True))
-            im.append(alternate * jnp.sum(wave * all_re, axis=0, keepdims=True))
-        for g in range(groups):
+            wave = sign * table[at : at + 8, :]
+            first_re = -jnp.sum(wave * all_im, axis=0, keepdims=True)
+            first_im = jnp.sum(wave * all_re, axis=0, keepdims=True)
+            re.append(jnp.broadcast_to(first_re, (groups, NZ)))
+            im.append(jnp.broadcast_to(first_im, (groups, NZ)))
+        for r in range(GROUP):
+            apart = mine + GROUP - r
+            ahead = apart // GROUP
+            row = (apart - GROUP * ahead) * (groups + 1) + ahead
             for c in range(6):
-                hat_re = jnp.broadcast_to(part[g, c : c + 1, re_lanes], (GROUP, NZ))
-                hat_im = jnp.broadcast_to(part[g, c : c + 1, im_lanes], (GROUP, NZ))
+                hat_re = jnp.broadcast_to(hat[r, c : c + 1, re_lanes], (groups, NZ))
+                hat_im = jnp.broadcast_to(hat[r, c : c + 1, im_lanes], (groups, NZ))
                 for a in range(3):
-                    at = at_gain + ((a * 6 + c) * TILES + k) * (sx + GROUP)
-                    gain = table[pl.ds(at + starts_x[g], GROUP), :]
+                    at = at_gain + ((a * 6 + c) * TILES + k) * (GROUP * (groups + 1))
+                    gain = table[pl.ds(at + row, groups), :]
                     if imaginary[a * 6 + c]:
                         re[a] = re[a] - gain * hat_im
                         im[a] = im[a] + gain * hat_re
                     else:
                         re[a] = re[a] + gain * hat_re
                         im[a] = im[a] + gain * hat_im
-        for j in range(pairs):
-            d = lax.rem(pairs + j - pair, pairs)
+        for j in range(columns):
+            d = lax.rem(pairs + j - column, pairs)
             cosine = table[pl.ds(at_turn + k + d * (2 * TILES), 1), :]
             sine = table[pl.ds(at_turn + TILES + k + d * (2 * TILES), 1), :]
             for a in range(3):
-                at = (a * pairs + j) * GROUP
-                field[at : at + GROUP, re_lanes] = re[a] * cosine - im[a] * sine
-                field[at : at + GROUP, im_lanes] = re[a] * sine + im[a] * cosine
+                at = (a * columns + j) * groups
+                field[at : at + groups, re_lanes] = re[a] * cosine - im[a] * sine
+                field[at : at + groups, im_lanes] = re[a] * sine + im[a] * cosine
     result = lax.dot_general(
         field[...],
         forward,
@@ -433,14 +440,15 @@
         precision=HIGHEST,
         preferred_element_type=jnp.float32,
     )
-    for j in range(pairs):
+    for j in range(columns):
         first, second, third = [
-            result[(a * pairs + j) * GROUP : (a * pairs + j + 1) * GROUP] for a in range(3)
+            result[(a * columns + j) * groups : (a * columns + j + 1) * groups] for a in range(3)
         ]
         both = first + pltpu.roll(second, 64, 1)
-        for r in range(GROUP):
-            out[r * pairs + j, 0:1, :] = both[r : r + 1]
-            out[r * pairs + j, 1:2, :] = third[r : r + 1]
+        for q in range(groups):
+            target = lax.rem(me + q, groups) * columns + j
+            out[target, 0:1, :] = both[q : q + 1]
+            out[target, 1:2, :] = third[q : q + 1]
 
 
 def last_kernel(parts, out):
@@ -507,7 +515,7 @@
     )(cells, y_far, y_near)
     post3, spread, far, near = call(
         third_kernel,
-        [(19, LX, PACK, NZ), (groups, 8, NZ), (EDGE_ROWS, NZ), (EDGE_ROWS, NZ)],
+        [(19, LX, PACK, NZ), (2 * GROUP, 8, NZ), (EDGE_ROWS, NZ), (EDGE_ROWS, NZ)],
         [
             (2, X_ROWS, NZ),
             (19, LX + 2 * REACH_X, WORK_ROWS, NZ),
@@ -517,7 +525,7 @@
         ],
         20_000_000,
     )(cells, total, packs, x_far, x_near)
-    blocks = lax.all_to_all(spread, "cy", 0, 0, tiled=False)
+    blocks = lax.all_to_all(spread, ("zl", "core", "zh"), 0, 0, tiled=False)
     edge_far, edge_near = swap(far, near, GX)
     blocks, edge_far, edge_near = lax.optimization_barrier((blocks, edge_far, edge_near))
     (momentum,) = call(
@@ -525,12 +533,16 @@
     )(post3, edge_far, edge_near)
     table, starts, imaginary = operator_table(nx, 2 * ny)
     (parts,) = call(
-        functools.partial(solve_kernel, starts, imaginary, ny),
-        [(GROUP * ny, 2, NZ)],
-        [(groups, 8, 2 * TILES * NZ), (3 * ny * GROUP, 2 * TILES * NZ)],
+        functools.partial(solve_kernel, starts, imaginary, ny, groups),
+        [(groups * ny // 2, 2, NZ)],
+        [
+            (2 * GROUP, 8, 2 * TILES * NZ),
+            (GROUP, 8, 2 * TILES * NZ),
+            (3 * groups * ny // 2, 2 * TILES * NZ),
+        ],
         10_000_000,
     )(blocks, table)
-    parts = lax.all_to_all(parts, ("zl", "core", "zh", "cx"), 0, 0, tiled=False)
+    parts = lax.all_to_all(parts, ("cy", "cx"), 0, 0, tiled=False)
     parts, momentum = lax.optimization_barrier((parts, momentum))
     (running,) = call(last_kernel, [(3, 1, 2, SZ)], [], 100_000)(parts)
     return momentum, running

time: 76.6 us -> 75 us (0.979)
  starting transfers between devices: 52 us -> 50.8 us
    all_to_all x2, starting transfers between devices: 17.8 us -> 15.3 us  [the longest x1 8.51 us: local(): blocks = lax.all_to_all(spread, ('zl', 'core', 'zh'), 0, 0, tiled=False)]
    ppermute x3, starting transfers between devices: 11 us -> 13.4 us  [swap(): lax.ppermute(near, axis, near_pairs)]
    ppermute x3, starting transfers between devices: 23.2 us -> 22 us  [swap(): lax.ppermute(far, axis, far_pairs)]
where the time goes in v6:
time: 75 us; the launch traced here: 74.6 us
  starting transfers between devices  50.8 us (68%)
  waiting for transfers between devices  15.2 us (20%)
  Pallas kernels  7.87 us (10%)
    ppermute x3, starting transfers between devices, swap(): lax.ppermute(far, axis, far_pairs)  22 us
    ppermute x3, starting transfers between devices, swap(): lax.ppermute(near, axis, near_pairs)  13.4 us
    all_to_all x1, starting transfers between devices, local(): blocks = lax.all_to_all(spread, ('zl', 'core', 'zh'), 0, 0, tiled=False)  8.51 us
    all_to_all x1, waiting for transfers between devices, local(): parts = lax.all_to_all(parts, ('cy', 'cx'), 0, 0, tiled=False)  7.93 us
    pallas_call x7, Pallas kernels, run(): pl.pallas_call(body, out_shape=shapes, in_specs=[pl.BlockSpec(memory_spac...  7.87 us
    all_to_all x1, starting transfers between devices, local(): parts = lax.all_to_all(parts, ('cy', 'cx'), 0, 0, tiled=False)  6.84 us
    ppermute x3, waiting for transfers between devices, swap(): lax.ppermute(far, axis, far_pairs)  5.97 us
  transfers between devices with their start and end apart: 8, of which 5 were waited for; matrix products, arithmetic and copies ran while one was open for 0% of the time, Pallas kernels for 1%

profile of v6, /device:TPU:1, one launch (start us, length us, event | category | flops | bytes accessed | tf_op | source)
XLA Modules:
  0.0 74.6 jit_solution(11522468016954703437)
XLA Ops:
  0.6 0.0 copy-start
  0.6 1.4 %shard_map.59 = (f32[23,4,8,128]{3,2,1,0:T(8,128)S(1)}, f32[6,8,128]{2,1,0:T(8,128)S(1)}, f32[280,128]{1,0:T(8,128)S(1)}, f32[280,128]{1,0:T(8,128)S(1)}) custom-call(f32[19,4,8,128]{3,2,1,0:T(8,128)} %pops_in.1, s32[4,8,128]{2,1,0:T(8,128)} %label_in.1, f32[3,4,8,128]{3,2,1,0:T(8,128)} %drive_in.1), custom_call_target="tpu_custom_call" | custom-call | flops 2000000 | bytes 2000000 | tf_op jit(solution)/shard_map/pallas_call | solution.py:469
  2.0 13.7 %collective-permute-start = (f32[280,128]{1,0:T(8,128)S(1)}, f32[280,128]{1,0:T(8,128)S(1)}, u32[]{:S(2)}, u32[]{:S(2)}) collective-permute-start(f32[280,128]{1,0:T(8,128)S(1)} %get-tuple-element.19), channel_id=1, source_target_pairs={{0,7},{1,2},{2,1},{3,4},{4,3},{5,6},{6,5},{7,0},{8,15},{9,10},{10,... | collective-permute-start | bytes 430088 | tf_op jit(solution)/shard_map/ppermute | solution.py:486
  15.7 1.9 %collective-permute-start.1 = (f32[280,128]{1,0:T(8,128)S(1)}, f32[280,128]{1,0:T(8,128)S(1)}, u32[]{:S(2)}, u32[]{:S(2)}) collective-permute-start(f32[280,128]{1,0:T(8,128)S(1)} %get-tuple-element.20), channel_id=1, source_target_pairs={{0,1},{1,0},{2,3},{3,2},{4,5},{5,4},{6,7},{7,6},{8,9},{9,8},{10,11... | collective-permute-start | bytes 430088 | tf_op jit(solution)/shard_map/ppermute | solution.py:486
  17.6 3.8 %collective-permute-done.got_far = f32[280,128]{1,0:T(8,128)S(1)} collective-permute-done((f32[280,128]{1,0:T(8,128)S(1)}, f32[280,128]{1,0:T(8,128)S(1)}, u32[]{:S(2)}, u32[]{:S(2)}) %collective-permute-start) | collective-permute-done | bytes 143392 | tf_op jit(solution)/shard_map/ppermute | solution.py:486
  21.4 0.5 collective-permute-done.1.got_near
  21.9 0.2 shard_map.61
  22.1 4.9 %collective-permute-start.2 = (f32[648,128]{1,0:T(8,128)S(1)}, f32[648,128]{1,0:T(8,128)S(1)}, u32[]{:S(2)}, u32[]{:S(2)}) collective-permute-start(f32[648,128]{1,0:T(8,128)S(1)} %get-tuple-element.21), channel_id=1, source_target_pairs={{0,504},{8,16},{16,8},{24,32},{32,24},{40,48},{48,40},{56,64},{64,... | collective-permute-start | bytes 995336 | tf_op jit(solution)/shard_map/ppermute | solution.py:486
  26.9 5.3 %collective-permute-start.3 = (f32[648,128]{1,0:T(8,128)S(1)}, f32[648,128]{1,0:T(8,128)S(1)}, u32[]{:S(2)}, u32[]{:S(2)}) collective-permute-start(f32[648,128]{1,0:T(8,128)S(1)} %get-tuple-element.22), channel_id=1, source_target_pairs={{0,8},{8,0},{16,24},{24,16},{32,40},{40,32},{48,56},{56,48},{64,72... | collective-permute-start | bytes 995336 | tf_op jit(solution)/shard_map/ppermute | solution.py:486
  32.2 0.1 shard_map.60.packs
  32.3 2.2 %collective-permute-done.2.x_far = f32[648,128]{1,0:T(8,128)S(1)} collective-permute-done((f32[648,128]{1,0:T(8,128)S(1)}, f32[648,128]{1,0:T(8,128)S(1)}, u32[]{:S(2)}, u32[]{:S(2)}) %collective-permute-start.2) | collective-permute-done | bytes 331808 | tf_op jit(solution)/shard_map/ppermute | solution.py:486
  34.5 0.0 collective-permute-done.3.x_near
  34.5 2.4 %shard_map.62 = (f32[19,4,16,128]{3,2,1,0:T(8,128)S(1)}, f32[16,8,128]{2,1,0:T(8,128)}, f32[40,128]{1,0:T(8,128)S(1)}, f32[40,128]{1,0:T(8,128)S(1)}) custom-call(f32[23,4,8,128]{3,2,1,0:T(8,128)S(1)} %get-tuple-element.17.cells, f32[6,8,128]{2,1,0:T(8,128)S(1)} %get-tuple-element.18.total, f32[23,4,16,128]{3,2,1,0:T(8,128)S(1)} %shard_map.60.packs, ...), custom_call_target="tpu_custom_call" | custom-call | flops 20000000 | bytes 20000000 | tf_op jit(solution)/shard_map/pallas_call | solution.py:469
  37.0 8.5 %all-to-all-start = ((f32[16,8,128]{2,1,0:T(8,128)}), f32[16,8,128]{2,1,0:T(8,128)S(1)}, u32[]{:S(2)}, u32[]{:S(2)}) async-start(f32[16,8,128]{2,1,0:T(8,128)} %get-tuple-element.23), calls=%async_computation | async-start | bytes 131072 | tf_op jit(solution)/shard_map/all_to_all | solution.py:528
  45.5 3.5 %collective-permute-start.4 = (f32[40,128]{1,0:T(8,128)S(1)}, f32[40,128]{1,0:T(8,128)S(1)}, u32[]{:S(2)}, u32[]{:S(2)}) collective-permute-start(f32[40,128]{1,0:T(8,128)S(1)} %get-tuple-element.24), channel_id=1, source_target_pairs={{0,504},{8,16},{16,8},{24,32},{32,24},{40,48},{48,40},{56,64},{64,... | collective-permute-start | bytes 61448 | tf_op jit(solution)/shard_map/ppermute | solution.py:486
  49.0 6.2 %collective-permute-start.5 = (f32[40,128]{1,0:T(8,128)S(1)}, f32[40,128]{1,0:T(8,128)S(1)}, u32[]{:S(2)}, u32[]{:S(2)}) collective-permute-start(f32[40,128]{1,0:T(8,128)S(1)} %get-tuple-element.25), channel_id=1, source_target_pairs={{0,8},{8,0},{16,24},{24,16},{32,40},{40,32},{48,56},{56,48},{64,72... | collective-permute-start | bytes 61448 | tf_op jit(solution)/shard_map/ppermute | solution.py:486
  55.2 0.0 collective-permute-done.4.x_far
  55.3 0.8 %collective-permute-done.5.x_near = f32[40,128]{1,0:T(8,128)S(1)} collective-permute-done((f32[40,128]{1,0:T(8,128)S(1)}, f32[40,128]{1,0:T(8,128)S(1)}, u32[]{:S(2)}, u32[]{:S(2)}) %collective-permute-start.5) | collective-permute-done | bytes 20512 | tf_op jit(solution)/shard_map/ppermute | solution.py:486
  56.1 0.0 all-to-all-done.blocks
  56.1 2.4 %shard_map.63 = f32[32,2,128]{2,1,0:T(2,128)} custom-call(f32[16,8,128]{2,1,0:T(8,128)S(1)} %all-to-all-done.blocks, f32[4776,128]{1,0:T(8,128)S(1)} %copy-done), custom_call_target="tpu_custom_call" | custom-call | flops 10000000 | bytes 10000000 | tf_op jit(solution)/shard_map/pallas_call | solution.py:469
  58.4 6.8 %all-to-all-start.1 = ((f32[32,2,128]{2,1,0:T(2,128)}), f32[32,2,128]{2,1,0:T(2,128)S(1)}, u32[]{:S(2)}, u32[]{:S(2)}) async-start(f32[32,2,128]{2,1,0:T(2,128)} %shard_map.63), calls=%async_computation.1 | async-start | bytes 65536 | tf_op jit(solution)/shard_map/all_to_all | solution.py:545
  65.3 0.7 shard_map.64
  66.0 7.9 %all-to-all-done.1.parts = f32[32,2,128]{2,1,0:T(2,128)S(1)} async-done(((f32[32,2,128]{2,1,0:T(2,128)}), f32[32,2,128]{2,1,0:T(2,128)S(1)}, u32[]{:S(2)}, u32[]{:S(2)}) %all-to-all-start.1) | async-done | bytes 32800 | tf_op jit(solution)/shard_map/all_to_all | solution.py:545
  73.9 0.7 shard_map.65
  (1 shorter events, 0.0 us)
Async XLA Ops:
  0.6 55.4 %copy-start = (f32[4776,128]{1,0:T(8,128)S(1)}, f32[4776,128]{1,0:T(8,128)}, u32[]{:S(2)}) copy-start(f32[4776,128]{1,0:T(8,128)} %constant.2.clone.table) | copy-start | bytes 7335940
  2.0 19.4 %collective-permute-start = (f32[280,128]{1,0:T(8,128)S(1)}, f32[280,128]{1,0:T(8,128)S(1)}, u32[]{:S(2)}, u32[]{:S(2)}) collective-permute-start(f32[280,128]{1,0:T(8,128)S(1)} %get-tuple-element.19), channel_id=1, source_target_pairs={{0,7},{1,2},{2,1},{3,4},{4,3},{5,6},{6,5},{7,0},{8,15},{9,10},{10,... | collective-permute-start | bytes 430088 | tf_op jit(solution)/shard_map/ppermute | solution.py:486
  15.7 6.2 %collective-permute-start.1 = (f32[280,128]{1,0:T(8,128)S(1)}, f32[280,128]{1,0:T(8,128)S(1)}, u32[]{:S(2)}, u32[]{:S(2)}) collective-permute-start(f32[280,128]{1,0:T(8,128)S(1)} %get-tuple-element.20), channel_id=1, source_target_pairs={{0,1},{1,0},{2,3},{3,2},{4,5},{5,4},{6,7},{7,6},{8,9},{9,8},{10,11... | collective-permute-start | bytes 430088 | tf_op jit(solution)/shard_map/ppermute | solution.py:486
  22.1 12.5 %collective-permute-start.2 = (f32[648,128]{1,0:T(8,128)S(1)}, f32[648,128]{1,0:T(8,128)S(1)}, u32[]{:S(2)}, u32[]{:S(2)}) collective-permute-start(f32[648,128]{1,0:T(8,128)S(1)} %get-tuple-element.21), channel_id=1, source_target_pairs={{0,504},{8,16},{16,8},{24,32},{32,24},{40,48},{48,40},{56,64},{64,... | collective-permute-start | bytes 995336 | tf_op jit(solution)/shard_map/ppermute | solution.py:486
  26.9 7.6 %collective-permute-start.3 = (f32[648,128]{1,0:T(8,128)S(1)}, f32[648,128]{1,0:T(8,128)S(1)}, u32[]{:S(2)}, u32[]{:S(2)}) collective-permute-start(f32[648,128]{1,0:T(8,128)S(1)} %get-tuple-element.22), channel_id=1, source_target_pairs={{0,8},{8,0},{16,24},{24,16},{32,40},{40,32},{48,56},{56,48},{64,72... | collective-permute-start | bytes 995336 | tf_op jit(solution)/shard_map/ppermute | solution.py:486
  37.0 19.1 %all-to-all-start = ((f32[16,8,128]{2,1,0:T(8,128)}), f32[16,8,128]{2,1,0:T(8,128)S(1)}, u32[]{:S(2)}, u32[]{:S(2)}) async-start(f32[16,8,128]{2,1,0:T(8,128)} %get-tuple-element.23), calls=%async_computation | async-start | bytes 131072 | tf_op jit(solution)/shard_map/all_to_all | solution.py:528
  45.5 9.8 %collective-permute-start.4 = (f32[40,128]{1,0:T(8,128)S(1)}, f32[40,128]{1,0:T(8,128)S(1)}, u32[]{:S(2)}, u32[]{:S(2)}) collective-permute-start(f32[40,128]{1,0:T(8,128)S(1)} %get-tuple-element.24), channel_id=1, source_target_pairs={{0,504},{8,16},{16,8},{24,32},{32,24},{40,48},{48,40},{56,64},{64,... | collective-permute-start | bytes 61448 | tf_op jit(solution)/shard_map/ppermute | solution.py:486
  49.0 7.1 %collective-permute-start.5 = (f32[40,128]{1,0:T(8,128)S(1)}, f32[40,128]{1,0:T(8,128)S(1)}, u32[]{:S(2)}, u32[]{:S(2)}) collective-permute-start(f32[40,128]{1,0:T(8,128)S(1)} %get-tuple-element.25), channel_id=1, source_target_pairs={{0,8},{8,0},{16,24},{24,16},{32,40},{40,32},{48,56},{56,48},{64,72... | collective-permute-start | bytes 61448 | tf_op jit(solution)/shard_map/ppermute | solution.py:486
  58.4 15.5 %all-to-all-start.1 = ((f32[32,2,128]{2,1,0:T(2,128)}), f32[32,2,128]{2,1,0:T(2,128)S(1)}, u32[]{:S(2)}, u32[]{:S(2)}) async-start(f32[32,2,128]{2,1,0:T(2,128)} %shard_map.63), calls=%async_computation.1 | async-start | bytes 65536 | tf_op jit(solution)/shard_map/all_to_all | solution.py:545

commit v7 on v6

--- a/solution.py
+++ b/solution.py
@@ -264,18 +264,15 @@
     chosen = jnp.logical_and((r & 7) == (c >> 3), (r >> 3) == ((c & 7) >> 2))
     left = jnp.where(chosen, 1.0, 0.0)
     halves = jnp.dot(left, stacked, precision=HIGHEST, preferred_element_type=jnp.float32)
-    z = lax.broadcasted_iota(jnp.int32, (NZ, NZ), 0)
-    lane = lax.broadcasted_iota(jnp.int32, (NZ, NZ), 1)
-    mean = 1.0 / (STEPS * 64)
-    slow = jnp.zeros((8, NZ), jnp.float32)
-    for half in range(2):
-        table = jnp.where(lane == (z >> 2) + half * SZ, mean, 0.0)
-        slow = slow + jnp.dot(
-            halves[half * 8 : half * 8 + 8],
-            table,
-            precision=HIGHEST,
-            preferred_element_type=jnp.float32,
-        )
+    z = lax.broadcasted_iota(jnp.int32, (2 * NZ, NZ), 0)
+    lane = lax.broadcasted_iota(jnp.int32, (2 * NZ, NZ), 1)
+    table = jnp.where(lane == z >> 2, 1.0 / (STEPS * 64), 0.0)
+    slow = jnp.dot(
+        jnp.concatenate([halves[0:8], halves[8:16]], axis=1),
+        table,
+        precision=HIGHEST,
+        preferred_element_type=jnp.float32,
+    )
     for d in range(spread.shape[0]):
         spread[d] = slow
     for slot, comps, x in ((odd_x, RIGHT, LX - 1), (1 - odd_x, LEFT, 0)):
@@ -285,7 +282,7 @@
     edge_far[...] = box[1]
 
 
-def momentum_kernel(post3, x_far, x_near, out, cols):
+def momentum_of(post3, x_far, x_near, out, cols):
     odd_x = lax.rem(lax.axis_index(GX), 2)
     cols[0] = x_near[...]
     cols[1] = x_far[...]
@@ -371,7 +368,24 @@
     return table, tuple(int(start) for start in starts[:4]), tuple(imaginary)
 
 
-def solve_kernel(starts, imaginary, pairs, groups, blocks, table, out, part, hat, field):
+def solve_kernel(
+    starts,
+    imaginary,
+    pairs,
+    groups,
+    blocks,
+    table,
+    post3,
+    x_far,
+    x_near,
+    out,
+    momentum,
+    part,
+    hat,
+    field,
+    cols,
+):
+    momentum_of(post3, x_far, x_near, momentum, cols)
     at_gain, at_twist, at_turn, at_forward = starts
     me = lax.axis_index("cy")
     mine = lax.rem(lax.axis_index(GX), GROUP)
@@ -528,22 +542,19 @@
     blocks = lax.all_to_all(spread, ("zl", "core", "zh"), 0, 0, tiled=False)
     edge_far, edge_near = swap(far, near, GX)
     blocks, edge_far, edge_near = lax.optimization_barrier((blocks, edge_far, edge_near))
-    (momentum,) = call(
-        momentum_kernel, [(3, LX, LY, NZ)], [(2, EDGE_ROWS, NZ)], 1_000_000
-    )(post3, edge_far, edge_near)
     table, starts, imaginary = operator_table(nx, 2 * ny)
-    (parts,) = call(
+    parts, momentum = call(
         functools.partial(solve_kernel, starts, imaginary, ny, groups),
-        [(groups * ny // 2, 2, NZ)],
+        [(groups * ny // 2, 2, NZ), (3, LX, LY, NZ)],
         [
             (2 * GROUP, 8, 2 * TILES * NZ),
             (GROUP, 8, 2 * TILES * NZ),
             (3 * groups * ny // 2, 2 * TILES * NZ),
+            (2, EDGE_ROWS, NZ),
         ],
         10_000_000,
-    )(blocks, table)
+    )(blocks, table, post3, edge_far, edge_near)
     parts = lax.all_to_all(parts, ("cy", "cx"), 0, 0, tiled=False)
-    parts, momentum = lax.optimization_barrier((parts, momentum))
     (running,) = call(last_kernel, [(3, 1, 2, SZ)], [], 100_000)(parts)
     return momentum, running
 

time: 75 us -> 74.8 us (level)
  blocking collectives: 0 us -> 15.3 us
  waiting for transfers between devices: 15.2 us -> 7.29 us
  starting transfers between devices: 50.8 us -> 44 us
  Pallas kernels: 7.87 us -> 7.12 us
    all_to_all x0 -> x1, blocking collectives: none -> 15.3 us  [local(): parts = lax.all_to_all(parts, ('cy', 'cx'), 0, 0, tiled=False)]
    all_to_all x1 -> x0, waiting for transfers between devices: 7.93 us -> none  [local(): parts = lax.all_to_all(parts, ('cy', 'cx'), 0, 0, tiled=False)]
    all_to_all x1 -> x0, starting transfers between devices: 6.84 us -> none  [local(): parts = lax.all_to_all(parts, ('cy', 'cx'), 0, 0, tiled=False)]
    pallas_call x7 -> x6, Pallas kernels: 7.87 us -> 7.12 us  [run(): pl.pallas_call(body, out_shape=shapes, in_specs=[pl.BlockSpec(memory_spac...]
  transfers between devices with their start and end apart: 8 -> 7, of which waited for: 5 -> 4; matrix products, arithmetic and copies ran while one was open for 0% -> 0% of each run, Pallas kernels for 1% -> 0%
where the time goes in v7:
time: 74.8 us; the launch traced here: 74.4 us
  starting transfers between devices  44 us (59%)
  blocking collectives  15.3 us (20%)
  waiting for transfers between devices  7.29 us (10%)
  Pallas kernels  7.12 us (10%)
    ppermute x3, starting transfers between devices, swap(): lax.ppermute(far, axis, far_pairs)  22 us
    all_to_all x1, blocking collectives, local(): parts = lax.all_to_all(parts, ('cy', 'cx'), 0, 0, tiled=False)  15.3 us
    ppermute x3, starting transfers between devices, swap(): lax.ppermute(near, axis, near_pairs)  13.4 us
    all_to_all x1, starting transfers between devices, local(): blocks = lax.all_to_all(spread, ('zl', 'core', 'zh'), 0, 0, tiled=False)  8.51 us
    pallas_call x6, Pallas kernels, run(): pl.pallas_call(body, out_shape=shapes, in_specs=[pl.BlockSpec(memory_spac...  7.12 us
    ppermute x3, waiting for transfers between devices, swap(): lax.ppermute(far, axis, far_pairs)  5.97 us
  transfers between devices with their start and end apart: 7, of which 4 were waited for; matrix products, arithmetic and copies ran while one was open for 0% of the time, Pallas kernels for 0%

profile of v7, /device:TPU:1, one launch (start us, length us, event | category | flops | bytes accessed | tf_op | source)
XLA Modules:
  0.0 74.4 jit_solution(542073979031773712)
XLA Ops:
  0.6 0.0 copy-start
  0.6 1.4 %shard_map.59 = (f32[23,4,8,128]{3,2,1,0:T(8,128)S(1)}, f32[6,8,128]{2,1,0:T(8,128)S(1)}, f32[280,128]{1,0:T(8,128)S(1)}, f32[280,128]{1,0:T(8,128)S(1)}) custom-call(f32[19,4,8,128]{3,2,1,0:T(8,128)} %pops_in.1, s32[4,8,128]{2,1,0:T(8,128)} %label_in.1, f32[3,4,8,128]{3,2,1,0:T(8,128)} %drive_in.1), custom_call_target="tpu_custom_call" | custom-call | flops 2000000 | bytes 2000000 | tf_op jit(solution)/shard_map/pallas_call | solution.py:483
  2.0 13.7 %collective-permute-start = (f32[280,128]{1,0:T(8,128)S(1)}, f32[280,128]{1,0:T(8,128)S(1)}, u32[]{:S(2)}, u32[]{:S(2)}) collective-permute-start(f32[280,128]{1,0:T(8,128)S(1)} %get-tuple-element.19), channel_id=1, source_target_pairs={{0,7},{1,2},{2,1},{3,4},{4,3},{5,6},{6,5},{7,0},{8,15},{9,10},{10,... | collective-permute-start | bytes 430088 | tf_op jit(solution)/shard_map/ppermute | solution.py:500
  15.7 1.9 %collective-permute-start.1 = (f32[280,128]{1,0:T(8,128)S(1)}, f32[280,128]{1,0:T(8,128)S(1)}, u32[]{:S(2)}, u32[]{:S(2)}) collective-permute-start(f32[280,128]{1,0:T(8,128)S(1)} %get-tuple-element.20), channel_id=1, source_target_pairs={{0,1},{1,0},{2,3},{3,2},{4,5},{5,4},{6,7},{7,6},{8,9},{9,8},{10,11... | collective-permute-start | bytes 430088 | tf_op jit(solution)/shard_map/ppermute | solution.py:500
  17.6 3.8 %collective-permute-done.got_far = f32[280,128]{1,0:T(8,128)S(1)} collective-permute-done((f32[280,128]{1,0:T(8,128)S(1)}, f32[280,128]{1,0:T(8,128)S(1)}, u32[]{:S(2)}, u32[]{:S(2)}) %collective-permute-start) | collective-permute-done | bytes 143392 | tf_op jit(solution)/shard_map/ppermute | solution.py:500
  21.4 0.5 collective-permute-done.1.got_near
  21.9 0.2 shard_map.61
  22.1 4.9 %collective-permute-start.2 = (f32[648,128]{1,0:T(8,128)S(1)}, f32[648,128]{1,0:T(8,128)S(1)}, u32[]{:S(2)}, u32[]{:S(2)}) collective-permute-start(f32[648,128]{1,0:T(8,128)S(1)} %get-tuple-element.21), channel_id=1, source_target_pairs={{0,504},{8,16},{16,8},{24,32},{32,24},{40,48},{48,40},{56,64},{64,... | collective-permute-start | bytes 995336 | tf_op jit(solution)/shard_map/ppermute | solution.py:500
  26.9 5.3 %collective-permute-start.3 = (f32[648,128]{1,0:T(8,128)S(1)}, f32[648,128]{1,0:T(8,128)S(1)}, u32[]{:S(2)}, u32[]{:S(2)}) collective-permute-start(f32[648,128]{1,0:T(8,128)S(1)} %get-tuple-element.22), channel_id=1, source_target_pairs={{0,8},{8,0},{16,24},{24,16},{32,40},{40,32},{48,56},{56,48},{64,72... | collective-permute-start | bytes 995336 | tf_op jit(solution)/shard_map/ppermute | solution.py:500
  32.2 0.1 shard_map.60.packs
  32.3 2.2 %collective-permute-done.2.x_far = f32[648,128]{1,0:T(8,128)S(1)} collective-permute-done((f32[648,128]{1,0:T(8,128)S(1)}, f32[648,128]{1,0:T(8,128)S(1)}, u32[]{:S(2)}, u32[]{:S(2)}) %collective-permute-start.2) | collective-permute-done | bytes 331808 | tf_op jit(solution)/shard_map/ppermute | solution.py:500
  34.5 0.0 collective-permute-done.3.x_near
  34.5 2.4 %shard_map.62 = (f32[19,4,16,128]{3,2,1,0:T(8,128)S(1)}, f32[16,8,128]{2,1,0:T(8,128)}, f32[40,128]{1,0:T(8,128)S(1)}, f32[40,128]{1,0:T(8,128)S(1)}) custom-call(f32[23,4,8,128]{3,2,1,0:T(8,128)S(1)} %get-tuple-element.17.cells, f32[6,8,128]{2,1,0:T(8,128)S(1)} %get-tuple-element.18.total, f32[23,4,16,128]{3,2,1,0:T(8,128)S(1)} %shard_map.60.packs, ...), custom_call_target="tpu_custom_call" | custom-call | flops 20000000 | bytes 20000000 | tf_op jit(solution)/shard_map/pallas_call | solution.py:483
  36.9 8.5 %all-to-all-start = ((f32[16,8,128]{2,1,0:T(8,128)}), f32[16,8,128]{2,1,0:T(8,128)S(1)}, u32[]{:S(2)}, u32[]{:S(2)}) async-start(f32[16,8,128]{2,1,0:T(8,128)} %get-tuple-element.23), calls=%async_computation | async-start | bytes 131072 | tf_op jit(solution)/shard_map/all_to_all | solution.py:542
  45.4 3.5 %collective-permute-start.4 = (f32[40,128]{1,0:T(8,128)S(1)}, f32[40,128]{1,0:T(8,128)S(1)}, u32[]{:S(2)}, u32[]{:S(2)}) collective-permute-start(f32[40,128]{1,0:T(8,128)S(1)} %get-tuple-element.24), channel_id=1, source_target_pairs={{0,504},{8,16},{16,8},{24,32},{32,24},{40,48},{48,40},{56,64},{64,... | collective-permute-start | bytes 61448 | tf_op jit(solution)/shard_map/ppermute | solution.py:500
  49.0 6.2 %collective-permute-start.5 = (f32[40,128]{1,0:T(8,128)S(1)}, f32[40,128]{1,0:T(8,128)S(1)}, u32[]{:S(2)}, u32[]{:S(2)}) collective-permute-start(f32[40,128]{1,0:T(8,128)S(1)} %get-tuple-element.25), channel_id=1, source_target_pairs={{0,8},{8,0},{16,24},{24,16},{32,40},{40,32},{48,56},{56,48},{64,72... | collective-permute-start | bytes 61448 | tf_op jit(solution)/shard_map/ppermute | solution.py:500
  55.2 0.0 collective-permute-done.4.x_far
  55.2 0.8 %collective-permute-done.5.x_near = f32[40,128]{1,0:T(8,128)S(1)} collective-permute-done((f32[40,128]{1,0:T(8,128)S(1)}, f32[40,128]{1,0:T(8,128)S(1)}, u32[]{:S(2)}, u32[]{:S(2)}) %collective-permute-start.5) | collective-permute-done | bytes 20512 | tf_op jit(solution)/shard_map/ppermute | solution.py:500
  56.0 0.0 all-to-all-done.blocks
  56.0 0.0 copy-done
  56.0 2.4 %shard_map.63 = (f32[32,2,128]{2,1,0:T(2,128)S(1)}, f32[3,4,8,128]{3,2,1,0:T(8,128)}) custom-call(f32[16,8,128]{2,1,0:T(8,128)S(1)} %all-to-all-done.blocks, f32[4776,128]{1,0:T(8,128)S(1)} %copy-done, f32[19,4,16,128]{3,2,1,0:T(8,128)S(1)} %get-tuple-element.27.post3, f32[40,128]{1,0:T(8,128)S(1)} %collective-permute-done.4.x_far, ...), custom_call_target="tpu_custom_call" | custom-call | flops 10000000 | bytes 10000000 | tf_op jit(solution)/shard_map/pallas_call | solution.py:483
  58.4 15.3 %all_to_all.10.parts = f32[32,2,128]{2,1,0:T(2,128)S(1)} all-to-all(f32[32,2,128]{2,1,0:T(2,128)S(1)} %get-tuple-element.31), channel_id=1, replica_groups=mesh['cy'=8,'zl'=4,'core'=2,'zh'=2,'cx'=4] {'cy','cx'}, dimensions={0} | all-to-all | bytes 65536 | tf_op jit(solution)/shard_map/all_to_all | solution.py:557
  73.7 0.7 shard_map.64
Async XLA Ops:
  0.6 55.4 %copy-start = (f32[4776,128]{1,0:T(8,128)S(1)}, f32[4776,128]{1,0:T(8,128)}, u32[]{:S(2)}) copy-start(f32[4776,128]{1,0:T(8,128)} %constant.2.clone.table) | copy-start | bytes 7335940
  2.0 19.4 %collective-permute-start = (f32[280,128]{1,0:T(8,128)S(1)}, f32[280,128]{1,0:T(8,128)S(1)}, u32[]{:S(2)}, u32[]{:S(2)}) collective-permute-start(f32[280,128]{1,0:T(8,128)S(1)} %get-tuple-element.19), channel_id=1, source_target_pairs={{0,7},{1,2},{2,1},{3,4},{4,3},{5,6},{6,5},{7,0},{8,15},{9,10},{10,... | collective-permute-start | bytes 430088 | tf_op jit(solution)/shard_map/ppermute | solution.py:500
  15.7 6.2 %collective-permute-start.1 = (f32[280,128]{1,0:T(8,128)S(1)}, f32[280,128]{1,0:T(8,128)S(1)}, u32[]{:S(2)}, u32[]{:S(2)}) collective-permute-start(f32[280,128]{1,0:T(8,128)S(1)} %get-tuple-element.20), channel_id=1, source_target_pairs={{0,1},{1,0},{2,3},{3,2},{4,5},{5,4},{6,7},{7,6},{8,9},{9,8},{10,11... | collective-permute-start | bytes 430088 | tf_op jit(solution)/shard_map/ppermute | solution.py:500
  22.1 12.5 %collective-permute-start.2 = (f32[648,128]{1,0:T(8,128)S(1)}, f32[648,128]{1,0:T(8,128)S(1)}, u32[]{:S(2)}, u32[]{:S(2)}) collective-permute-start(f32[648,128]{1,0:T(8,128)S(1)} %get-tuple-element.21), channel_id=1, source_target_pairs={{0,504},{8,16},{16,8},{24,32},{32,24},{40,48},{48,40},{56,64},{64,... | collective-permute-start | bytes 995336 | tf_op jit(solution)/shard_map/ppermute | solution.py:500
  26.9 7.6 %collective-permute-start.3 = (f32[648,128]{1,0:T(8,128)S(1)}, f32[648,128]{1,0:T(8,128)S(1)}, u32[]{:S(2)}, u32[]{:S(2)}) collective-permute-start(f32[648,128]{1,0:T(8,128)S(1)} %get-tuple-element.22), channel_id=1, source_target_pairs={{0,8},{8,0},{16,24},{24,16},{32,40},{40,32},{48,56},{56,48},{64,72... | collective-permute-start | bytes 995336 | tf_op jit(solution)/shard_map/ppermute | solution.py:500
  36.9 19.1 %all-to-all-start = ((f32[16,8,128]{2,1,0:T(8,128)}), f32[16,8,128]{2,1,0:T(8,128)S(1)}, u32[]{:S(2)}, u32[]{:S(2)}) async-start(f32[16,8,128]{2,1,0:T(8,128)} %get-tuple-element.23), calls=%async_computation | async-start | bytes 131072 | tf_op jit(solution)/shard_map/all_to_all | solution.py:542
  45.4 9.8 %collective-permute-start.4 = (f32[40,128]{1,0:T(8,128)S(1)}, f32[40,128]{1,0:T(8,128)S(1)}, u32[]{:S(2)}, u32[]{:S(2)}) collective-permute-start(f32[40,128]{1,0:T(8,128)S(1)} %get-tuple-element.24), channel_id=1, source_target_pairs={{0,504},{8,16},{16,8},{24,32},{32,24},{40,48},{48,40},{56,64},{64,... | collective-permute-start | bytes 61448 | tf_op jit(solution)/shard_map/ppermute | solution.py:500
  49.0 7.1 %collective-permute-start.5 = (f32[40,128]{1,0:T(8,128)S(1)}, f32[40,128]{1,0:T(8,128)S(1)}, u32[]{:S(2)}, u32[]{:S(2)}) collective-permute-start(f32[40,128]{1,0:T(8,128)S(1)} %get-tuple-element.25), channel_id=1, source_target_pairs={{0,8},{8,0},{16,24},{24,16},{32,40},{40,32},{48,56},{56,48},{64,72... | collective-permute-start | bytes 61448 | tf_op jit(solution)/shard_map/ppermute | solution.py:500

commit v8 on v6

--- a/solution.py
+++ b/solution.py
@@ -264,18 +264,15 @@
     chosen = jnp.logical_and((r & 7) == (c >> 3), (r >> 3) == ((c & 7) >> 2))
     left = jnp.where(chosen, 1.0, 0.0)
     halves = jnp.dot(left, stacked, precision=HIGHEST, preferred_element_type=jnp.float32)
-    z = lax.broadcasted_iota(jnp.int32, (NZ, NZ), 0)
-    lane = lax.broadcasted_iota(jnp.int32, (NZ, NZ), 1)
-    mean = 1.0 / (STEPS * 64)
-    slow = jnp.zeros((8, NZ), jnp.float32)
-    for half in range(2):
-        table = jnp.where(lane == (z >> 2) + half * SZ, mean, 0.0)
-        slow = slow + jnp.dot(
-            halves[half * 8 : half * 8 + 8],
-            table,
-            precision=HIGHEST,
-            preferred_element_type=jnp.float32,
-        )
+    z = lax.broadcasted_iota(jnp.int32, (2 * NZ, NZ), 0)
+    lane = lax.broadcasted_iota(jnp.int32, (2 * NZ, NZ), 1)
+    table = jnp.where(lane == z >> 2, 1.0 / (STEPS * 64), 0.0)
+    slow = jnp.dot(
+        jnp.concatenate([halves[0:8], halves[8:16]], axis=1),
+        table,
+        precision=HIGHEST,
+        preferred_element_type=jnp.float32,
+    )
     for d in range(spread.shape[0]):
         spread[d] = slow
     for slot, comps, x in ((odd_x, RIGHT, LX - 1), (1 - odd_x, LEFT, 0)):
@@ -527,7 +524,6 @@
     )(cells, total, packs, x_far, x_near)
     blocks = lax.all_to_all(spread, ("zl", "core", "zh"), 0, 0, tiled=False)
     edge_far, edge_near = swap(far, near, GX)
-    blocks, edge_far, edge_near = lax.optimization_barrier((blocks, edge_far, edge_near))
     (momentum,) = call(
         momentum_kernel, [(3, LX, LY, NZ)], [(2, EDGE_ROWS, NZ)], 1_000_000
     )(post3, edge_far, edge_near)

time: 75 us -> 74.4 us (level); the launches traced: 74.6 us -> 73.2 us
  blocking collectives: 0 us -> 15.9 us
  starting transfers between devices: 50.8 us -> 42.1 us
  waiting for transfers between devices: 15.2 us -> 7.29 us
    all_to_all x0 -> x1, blocking collectives: none -> 15.9 us  [local(): blocks = lax.all_to_all(spread, ('zl', 'core', 'zh'), 0, 0, tiled=False)]
    all_to_all x1 -> x0, starting transfers between devices: 8.51 us -> none  [local(): blocks = lax.all_to_all(spread, ('zl', 'core', 'zh'), 0, 0, tiled=False)]
    all_to_all x1, waiting for transfers between devices: 7.93 us -> 0.01 us  [local(): parts = lax.all_to_all(parts, ('cy', 'cx'), 0, 0, tiled=False)]
    all_to_all x1, starting transfers between devices: 6.84 us -> 9.22 us  [local(): parts = lax.all_to_all(parts, ('cy', 'cx'), 0, 0, tiled=False)]
    ppermute x3, starting transfers between devices: 13.4 us -> 11.1 us  [swap(): lax.ppermute(near, axis, near_pairs)]
  transfers between devices with their start and end apart: 8 -> 7, of which waited for: 5 -> 4; matrix products, arithmetic and copies ran while one was open for 0% -> 0% of each run, Pallas kernels for 1% -> 1%
where the time goes in v8:
time: 74.4 us; the launch traced here: 73.2 us
  starting transfers between devices  42.1 us (57%)
  blocking collectives  15.9 us (21%)
  waiting for transfers between devices  7.29 us (10%)
  Pallas kernels  7.19 us (10%)
    ppermute x3, starting transfers between devices, swap(): lax.ppermute(far, axis, far_pairs)  21.8 us
    all_to_all x1, blocking collectives, local(): blocks = lax.all_to_all(spread, ('zl', 'core', 'zh'), 0, 0, tiled=False)  15.9 us
    ppermute x3, starting transfers between devices, swap(): lax.ppermute(near, axis, near_pairs)  11.1 us
    all_to_all x1, starting transfers between devices, local(): parts = lax.all_to_all(parts, ('cy', 'cx'), 0, 0, tiled=False)  9.22 us
    pallas_call x7, Pallas kernels, run(): pl.pallas_call(body, out_shape=shapes, in_specs=[pl.BlockSpec(memory_spac...  7.19 us
    ppermute x3, waiting for transfers between devices, swap(): lax.ppermute(far, axis, far_pairs)  5.97 us
  transfers between devices with their start and end apart: 7, of which 4 were waited for; matrix products, arithmetic and copies ran while one was open for 0% of the time, Pallas kernels for 1%

profile of v8, /device:TPU:1, one launch (start us, length us, event | category | flops | bytes accessed | tf_op | source)
XLA Modules:
  0.0 73.2 jit_solution(12429401774601365429)
XLA Ops:
  0.6 0.0 copy-start
  0.6 1.4 %shard_map.59 = (f32[23,4,8,128]{3,2,1,0:T(8,128)S(1)}, f32[6,8,128]{2,1,0:T(8,128)S(1)}, f32[280,128]{1,0:T(8,128)S(1)}, f32[280,128]{1,0:T(8,128)S(1)}) custom-call(f32[19,4,8,128]{3,2,1,0:T(8,128)} %pops_in.1, s32[4,8,128]{2,1,0:T(8,128)} %label_in.1, f32[3,4,8,128]{3,2,1,0:T(8,128)} %drive_in.1), custom_call_target="tpu_custom_call" | custom-call | flops 2000000 | bytes 2000000 | tf_op jit(solution)/shard_map/pallas_call | solution.py:466
  2.0 13.7 %collective-permute-start = (f32[280,128]{1,0:T(8,128)S(1)}, f32[280,128]{1,0:T(8,128)S(1)}, u32[]{:S(2)}, u32[]{:S(2)}) collective-permute-start(f32[280,128]{1,0:T(8,128)S(1)} %get-tuple-element.16), channel_id=1, source_target_pairs={{0,7},{1,2},{2,1},{3,4},{4,3},{5,6},{6,5},{7,0},{8,15},{9,10},{10,... | collective-permute-start | bytes 430088 | tf_op jit(solution)/shard_map/ppermute | solution.py:483
  15.7 1.9 %collective-permute-start.1 = (f32[280,128]{1,0:T(8,128)S(1)}, f32[280,128]{1,0:T(8,128)S(1)}, u32[]{:S(2)}, u32[]{:S(2)}) collective-permute-start(f32[280,128]{1,0:T(8,128)S(1)} %get-tuple-element.17), channel_id=1, source_target_pairs={{0,1},{1,0},{2,3},{3,2},{4,5},{5,4},{6,7},{7,6},{8,9},{9,8},{10,11... | collective-permute-start | bytes 430088 | tf_op jit(solution)/shard_map/ppermute | solution.py:483
  17.6 3.8 %collective-permute-done.got_far = f32[280,128]{1,0:T(8,128)S(1)} collective-permute-done((f32[280,128]{1,0:T(8,128)S(1)}, f32[280,128]{1,0:T(8,128)S(1)}, u32[]{:S(2)}, u32[]{:S(2)}) %collective-permute-start) | collective-permute-done | bytes 143392 | tf_op jit(solution)/shard_map/ppermute | solution.py:483
  21.4 0.5 collective-permute-done.1.got_near
  21.9 0.2 shard_map.61
  22.1 4.9 %collective-permute-start.2 = (f32[648,128]{1,0:T(8,128)S(1)}, f32[648,128]{1,0:T(8,128)S(1)}, u32[]{:S(2)}, u32[]{:S(2)}) collective-permute-start(f32[648,128]{1,0:T(8,128)S(1)} %get-tuple-element.18), channel_id=1, source_target_pairs={{0,504},{8,16},{16,8},{24,32},{32,24},{40,48},{48,40},{56,64},{64,... | collective-permute-start | bytes 995336 | tf_op jit(solution)/shard_map/ppermute | solution.py:483
  26.9 5.3 %collective-permute-start.3 = (f32[648,128]{1,0:T(8,128)S(1)}, f32[648,128]{1,0:T(8,128)S(1)}, u32[]{:S(2)}, u32[]{:S(2)}) collective-permute-start(f32[648,128]{1,0:T(8,128)S(1)} %get-tuple-element.19), channel_id=1, source_target_pairs={{0,8},{8,0},{16,24},{24,16},{32,40},{40,32},{48,56},{56,48},{64,72... | collective-permute-start | bytes 995336 | tf_op jit(solution)/shard_map/ppermute | solution.py:483
  32.2 0.1 shard_map.60.packs
  32.3 2.2 %collective-permute-done.2.x_far = f32[648,128]{1,0:T(8,128)S(1)} collective-permute-done((f32[648,128]{1,0:T(8,128)S(1)}, f32[648,128]{1,0:T(8,128)S(1)}, u32[]{:S(2)}, u32[]{:S(2)}) %collective-permute-start.2) | collective-permute-done | bytes 331808 | tf_op jit(solution)/shard_map/ppermute | solution.py:483
  34.5 0.0 collective-permute-done.3.x_near
  34.5 1.7 %shard_map.62 = (f32[19,4,16,128]{3,2,1,0:T(8,128)S(1)}, f32[16,8,128]{2,1,0:T(8,128)S(1)}, f32[40,128]{1,0:T(8,128)S(1)}, f32[40,128]{1,0:T(8,128)S(1)}) custom-call(f32[23,4,8,128]{3,2,1,0:T(8,128)S(1)} %get-tuple-element.14.cells, f32[6,8,128]{2,1,0:T(8,128)S(1)} %get-tuple-element.15.total, f32[23,4,16,128]{3,2,1,0:T(8,128)S(1)} %shard_map.60.packs, ...), custom_call_target="tpu_custom_call" | custom-call | flops 20000000 | bytes 20000000 | tf_op jit(solution)/shard_map/pallas_call | solution.py:466
  36.3 15.9 %all_to_all.10.blocks = f32[16,8,128]{2,1,0:T(8,128)S(1)} all-to-all(f32[16,8,128]{2,1,0:T(8,128)S(1)} %get-tuple-element.20), channel_id=1, replica_groups=mesh['cy'=8,'zl'=4,'core'=2,'zh'=2,'cx'=4] {'zl','core','zh'}, dimensions={0} | all-to-all | bytes 131072 | tf_op jit(solution)/shard_map/all_to_all | solution.py:525
  52.2 0.0 copy-done
  52.2 2.4 %shard_map.63 = f32[32,2,128]{2,1,0:T(2,128)} custom-call(f32[16,8,128]{2,1,0:T(8,128)S(1)} %all_to_all.10.blocks, f32[4776,128]{1,0:T(8,128)S(1)} %copy-done), custom_call_target="tpu_custom_call" | custom-call | flops 10000000 | bytes 10000000 | tf_op jit(solution)/shard_map/pallas_call | solution.py:466
  54.6 9.2 %all-to-all-start.1 = ((f32[32,2,128]{2,1,0:T(2,128)}), f32[32,2,128]{2,1,0:T(2,128)S(1)}, u32[]{:S(2)}, u32[]{:S(2)}) async-start(f32[32,2,128]{2,1,0:T(2,128)} %shard_map.63), calls=%async_computation.1 | async-start | bytes 65536 | tf_op jit(solution)/shard_map/all_to_all | solution.py:541
  63.8 3.3 %collective-permute-start.4 = (f32[40,128]{1,0:T(8,128)S(1)}, f32[40,128]{1,0:T(8,128)S(1)}, u32[]{:S(2)}, u32[]{:S(2)}) collective-permute-start(f32[40,128]{1,0:T(8,128)S(1)} %get-tuple-element.22), channel_id=1, source_target_pairs={{0,504},{8,16},{16,8},{24,32},{32,24},{40,48},{48,40},{56,64},{64,... | collective-permute-start | bytes 61448 | tf_op jit(solution)/shard_map/ppermute | solution.py:483
  67.1 3.9 %collective-permute-start.5 = (f32[40,128]{1,0:T(8,128)S(1)}, f32[40,128]{1,0:T(8,128)S(1)}, u32[]{:S(2)}, u32[]{:S(2)}) collective-permute-start(f32[40,128]{1,0:T(8,128)S(1)} %get-tuple-element.23), channel_id=1, source_target_pairs={{0,8},{8,0},{16,24},{24,16},{32,40},{40,32},{48,56},{56,48},{64,72... | collective-permute-start | bytes 61448 | tf_op jit(solution)/shard_map/ppermute | solution.py:483
  71.0 0.0 collective-permute-done.4.x_far
  71.0 0.8 %collective-permute-done.5.x_near = f32[40,128]{1,0:T(8,128)S(1)} collective-permute-done((f32[40,128]{1,0:T(8,128)S(1)}, f32[40,128]{1,0:T(8,128)S(1)}, u32[]{:S(2)}, u32[]{:S(2)}) %collective-permute-start.5) | collective-permute-done | bytes 20512 | tf_op jit(solution)/shard_map/ppermute | solution.py:483
  71.8 0.7 %shard_map.64 = f32[3,4,8,128]{3,2,1,0:T(8,128)} custom-call(f32[19,4,16,128]{3,2,1,0:T(8,128)S(1)} %get-tuple-element.21.post3, f32[40,128]{1,0:T(8,128)S(1)} %collective-permute-done.4.x_far, f32[40,128]{1,0:T(8,128)S(1)} %collective-permute-done.5.x_near), custom_call_target="tpu_custom_call" | custom-call | flops 1000000 | bytes 1000000 | tf_op jit(solution)/shard_map/pallas_call | solution.py:466
  72.5 0.0 all-to-all-done.1.parts
  72.5 0.7 shard_map.65
Async XLA Ops:
  0.6 51.6 %copy-start = (f32[4776,128]{1,0:T(8,128)S(1)}, f32[4776,128]{1,0:T(8,128)}, u32[]{:S(2)}) copy-start(f32[4776,128]{1,0:T(8,128)} %constant.2.clone.table) | copy-start | bytes 7335940
  2.0 19.4 %collective-permute-start = (f32[280,128]{1,0:T(8,128)S(1)}, f32[280,128]{1,0:T(8,128)S(1)}, u32[]{:S(2)}, u32[]{:S(2)}) collective-permute-start(f32[280,128]{1,0:T(8,128)S(1)} %get-tuple-element.16), channel_id=1, source_target_pairs={{0,7},{1,2},{2,1},{3,4},{4,3},{5,6},{6,5},{7,0},{8,15},{9,10},{10,... | collective-permute-start | bytes 430088 | tf_op jit(solution)/shard_map/ppermute | solution.py:483
  15.7 6.2 %collective-permute-start.1 = (f32[280,128]{1,0:T(8,128)S(1)}, f32[280,128]{1,0:T(8,128)S(1)}, u32[]{:S(2)}, u32[]{:S(2)}) collective-permute-start(f32[280,128]{1,0:T(8,128)S(1)} %get-tuple-element.17), channel_id=1, source_target_pairs={{0,1},{1,0},{2,3},{3,2},{4,5},{5,4},{6,7},{7,6},{8,9},{9,8},{10,11... | collective-permute-start | bytes 430088 | tf_op jit(solution)/shard_map/ppermute | solution.py:483
  22.1 12.5 %collective-permute-start.2 = (f32[648,128]{1,0:T(8,128)S(1)}, f32[648,128]{1,0:T(8,128)S(1)}, u32[]{:S(2)}, u32[]{:S(2)}) collective-permute-start(f32[648,128]{1,0:T(8,128)S(1)} %get-tuple-element.18), channel_id=1, source_target_pairs={{0,504},{8,16},{16,8},{24,32},{32,24},{40,48},{48,40},{56,64},{64,... | collective-permute-start | bytes 995336 | tf_op jit(solution)/shard_map/ppermute | solution.py:483
  26.9 7.6 %collective-permute-start.3 = (f32[648,128]{1,0:T(8,128)S(1)}, f32[648,128]{1,0:T(8,128)S(1)}, u32[]{:S(2)}, u32[]{:S(2)}) collective-permute-start(f32[648,128]{1,0:T(8,128)S(1)} %get-tuple-element.19), channel_id=1, source_target_pairs={{0,8},{8,0},{16,24},{24,16},{32,40},{40,32},{48,56},{56,48},{64,72... | collective-permute-start | bytes 995336 | tf_op jit(solution)/shard_map/ppermute | solution.py:483
  54.6 17.9 %all-to-all-start.1 = ((f32[32,2,128]{2,1,0:T(2,128)}), f32[32,2,128]{2,1,0:T(2,128)S(1)}, u32[]{:S(2)}, u32[]{:S(2)}) async-start(f32[32,2,128]{2,1,0:T(2,128)} %shard_map.63), calls=%async_computation.1 | async-start | bytes 65536 | tf_op jit(solution)/shard_map/all_to_all | solution.py:541
  63.8 7.2 %collective-permute-start.4 = (f32[40,128]{1,0:T(8,128)S(1)}, f32[40,128]{1,0:T(8,128)S(1)}, u32[]{:S(2)}, u32[]{:S(2)}) collective-permute-start(f32[40,128]{1,0:T(8,128)S(1)} %get-tuple-element.22), channel_id=1, source_target_pairs={{0,504},{8,16},{16,8},{24,32},{32,24},{40,48},{48,40},{56,64},{64,... | collective-permute-start | bytes 61448 | tf_op jit(solution)/shard_map/ppermute | solution.py:483
  67.1 4.7 %collective-permute-start.5 = (f32[40,128]{1,0:T(8,128)S(1)}, f32[40,128]{1,0:T(8,128)S(1)}, u32[]{:S(2)}, u32[]{:S(2)}) collective-permute-start(f32[40,128]{1,0:T(8,128)S(1)} %get-tuple-element.23), channel_id=1, source_target_pairs={{0,8},{8,0},{16,24},{24,16},{32,40},{40,32},{48,56},{56,48},{64,72... | collective-permute-start | bytes 61448 | tf_op jit(solution)/shard_map/ppermute | solution.py:483

commit v9 on v8

--- a/solution.py
+++ b/solution.py
@@ -51,7 +51,7 @@
 GROUP = 8
 
 
-REACH_X = STEPS - 2
+REACH_X = STEPS - 1
 REACH_Y = STEPS - 1
 
 
@@ -84,9 +84,6 @@
 Y_DOWN_AT = {(ch, x): (n, at) for ch, x, _, n, at in Y_DOWN}
 X_RIGHT_AT = {(ch, x): at for ch, x, _, _, at in X_RIGHT}
 X_LEFT_AT = {(ch, x): at for ch, x, _, _, at in X_LEFT}
-RIGHT = [i for i in range(19) if CX[i] == 1]
-LEFT = [i for i in range(19) if CX[i] == -1]
-EDGE_ROWS = len(RIGHT) * LY
 
 
 def collide(f, label, drive, phase):
@@ -218,7 +215,7 @@
 
 
 def third_kernel(
-    cells, total, packs, x_far, x_near, post3, spread, edge_far, edge_near, cols, one, two, sums, box
+    cells, total, packs, x_far, x_near, post3, spread, cols, one, two, sums
 ):
     odd_x = lax.rem(lax.axis_index(GX), 2)
     left_slot, right_slot = 1 - odd_x, odd_x
@@ -275,30 +272,13 @@
     )
     for d in range(spread.shape[0]):
         spread[d] = slow
-    for slot, comps, x in ((odd_x, RIGHT, LX - 1), (1 - odd_x, LEFT, 0)):
-        for k, i in enumerate(comps):
-            box[slot, k * LY : k * LY + LY, :] = post3[i, x, 1 - CY[i] : 1 - CY[i] + LY, :]
-    edge_near[...] = box[0]
-    edge_far[...] = box[1]
-
-
-def momentum_kernel(post3, x_far, x_near, out, cols):
-    odd_x = lax.rem(lax.axis_index(GX), 2)
-    cols[0] = x_near[...]
-    cols[1] = x_far[...]
+
+
+def momentum_of(post3, out):
     for x in range(LX):
-        f = [None]
-        for i in range(1, 19):
-            source = x - CX[i]
-            if source < 0:
-                at = RIGHT.index(i) * LY
-                value = cols[1 - odd_x, at : at + LY, :]
-            elif source >= LX:
-                at = LEFT.index(i) * LY
-                value = cols[odd_x, at : at + LY, :]
-            else:
-                value = post3[i, source, 1 - CY[i] : 1 - CY[i] + LY, :]
-            f.append(spin(value, i))
+        f = [None] + [
+            spin(post3[i, x + 1 - CX[i], 1 - CY[i] : 1 - CY[i] + LY, :], i) for i in range(1, 19)
+        ]
         for axis in range(3):
             total = None
             for i in range(1, 19, 2):
@@ -368,7 +348,10 @@
     return table, tuple(int(start) for start in starts[:4]), tuple(imaginary)
 
 
-def solve_kernel(starts, imaginary, pairs, groups, blocks, table, out, part, hat, field):
+def solve_kernel(
+    starts, imaginary, pairs, groups, blocks, table, post3, out, momentum, part, hat, field
+):
+    momentum_of(post3, momentum)
     at_gain, at_twist, at_turn, at_forward = starts
     me = lax.axis_index("cy")
     mine = lax.rem(lax.axis_index(GX), GROUP)
@@ -510,36 +493,30 @@
     (packs,) = call(
         own_kernel, [(CHANNELS, LX, PACK, NZ)], [(2, Y_ROWS, NZ)], 2_000_000
     )(cells, y_far, y_near)
-    post3, spread, far, near = call(
+    post3, spread = call(
         third_kernel,
-        [(19, LX, PACK, NZ), (2 * GROUP, 8, NZ), (EDGE_ROWS, NZ), (EDGE_ROWS, NZ)],
+        [(19, LX + 2, PACK, NZ), (2 * GROUP, 8, NZ)],
         [
             (2, X_ROWS, NZ),
             (19, LX + 2 * REACH_X, WORK_ROWS, NZ),
             (19, LX + 2 * REACH_X - 2, WORK_ROWS, NZ),
             (18, 16, NZ),
-            (2, EDGE_ROWS, NZ),
         ],
         20_000_000,
     )(cells, total, packs, x_far, x_near)
     blocks = lax.all_to_all(spread, ("zl", "core", "zh"), 0, 0, tiled=False)
-    edge_far, edge_near = swap(far, near, GX)
-    (momentum,) = call(
-        momentum_kernel, [(3, LX, LY, NZ)], [(2, EDGE_ROWS, NZ)], 1_000_000
-    )(post3, edge_far, edge_near)
     table, starts, imaginary = operator_table(nx, 2 * ny)
-    (parts,) = call(
+    parts, momentum = call(
         functools.partial(solve_kernel, starts, imaginary, ny, groups),
-        [(groups * ny // 2, 2, NZ)],
+        [(groups * ny // 2, 2, NZ), (3, LX, LY, NZ)],
         [
             (2 * GROUP, 8, 2 * TILES * NZ),
             (GROUP, 8, 2 * TILES * NZ),
             (3 * groups * ny // 2, 2 * TILES * NZ),
         ],
         10_000_000,
-    )(blocks, table)
+    )(blocks, table, post3)
     parts = lax.all_to_all(parts, ("cy", "cx"), 0, 0, tiled=False)
-    parts, momentum = lax.optimization_barrier((parts, momentum))
     (running,) = call(last_kernel, [(3, 1, 2, SZ)], [], 100_000)(parts)
     return momentum, running
 

time: 74.4 us -> 76.2 us (1.024); the launches traced: 73.2 us -> 75.9 us
  starting transfers between devices: 42.1 us -> 25.7 us
  blocking collectives: 15.9 us -> 32 us
  waiting for transfers between devices: 7.29 us -> 10.7 us
    all_to_all x0 -> x1, blocking collectives: none -> 17.3 us  [local(): parts = lax.all_to_all(parts, ('cy', 'cx'), 0, 0, tiled=False)]
    all_to_all x1 -> x0, starting transfers between devices: 9.22 us -> none  [local(): parts = lax.all_to_all(parts, ('cy', 'cx'), 0, 0, tiled=False)]
    ppermute x3 -> x2, waiting for transfers between devices: 5.97 us -> 10.2 us  [swap(): lax.ppermute(far, axis, far_pairs)]
    ppermute x3 -> x2, starting transfers between devices: 11.1 us -> 7.2 us  [swap(): lax.ppermute(near, axis, near_pairs)]
    ppermute x3 -> x2, starting transfers between devices: 21.8 us -> 18.5 us  [swap(): lax.ppermute(far, axis, far_pairs)]
    all_to_all x1, blocking collectives: 15.9 us -> 14.7 us  [local(): blocks = lax.all_to_all(spread, ('zl', 'core', 'zh'), 0, 0, tiled=False)]
    ppermute x3 -> x2, waiting for transfers between devices: 1.31 us -> 0.5 us  [swap(): lax.ppermute(near, axis, near_pairs)]
    pallas_call x7 -> x6, Pallas kernels: 7.19 us -> 6.76 us  [run(): pl.pallas_call(body, out_shape=shapes, in_specs=[pl.BlockSpec(memory_spac...]
  transfers between devices with their start and end apart: 7 -> 4, of which waited for: 4 -> 3; matrix products, arithmetic and copies ran while one was open for 0% -> 0% of each run, Pallas kernels for 1% -> 0%
where the time goes in v9:
time: 76.2 us; the launch traced here: 75.9 us
  blocking collectives  32 us (42%)
  starting transfers between devices  25.7 us (34%)
  waiting for transfers between devices  10.7 us (14%)
  Pallas kernels  6.76 us (9%)
    ppermute x2, starting transfers between devices, swap(): lax.ppermute(far, axis, far_pairs)  18.5 us
    all_to_all x1, blocking collectives, local(): parts = lax.all_to_all(parts, ('cy', 'cx'), 0, 0, tiled=False)  17.3 us
    all_to_all x1, blocking collectives, local(): blocks = lax.all_to_all(spread, ('zl', 'core', 'zh'), 0, 0, tiled=False)  14.7 us
    ppermute x2, waiting for transfers between devices, swap(): lax.ppermute(far, axis, far_pairs)  10.2 us
    ppermute x2, starting transfers between devices, swap(): lax.ppermute(near, axis, near_pairs)  7.2 us
    pallas_call x6, Pallas kernels, run(): pl.pallas_call(body, out_shape=shapes, in_specs=[pl.BlockSpec(memory_spac...  6.76 us
  transfers between devices with their start and end apart: 4, of which 3 were waited for; matrix products, arithmetic and copies ran while one was open for 0% of the time, Pallas kernels for 0%

profile of v9, /device:TPU:1, one launch (start us, length us, event | category | flops | bytes accessed | tf_op | source)
XLA Modules:
  0.0 75.9 jit_solution(17978524435587062883)
XLA Ops:
  0.6 0.0 copy-start
  0.6 1.4 %shard_map.59 = (f32[23,4,8,128]{3,2,1,0:T(8,128)S(1)}, f32[6,8,128]{2,1,0:T(8,128)S(1)}, f32[280,128]{1,0:T(8,128)S(1)}, f32[280,128]{1,0:T(8,128)S(1)}) custom-call(f32[19,4,8,128]{3,2,1,0:T(8,128)} %pops_in.1, s32[4,8,128]{2,1,0:T(8,128)} %label_in.1, f32[3,4,8,128]{3,2,1,0:T(8,128)} %drive_in.1), custom_call_target="tpu_custom_call" | custom-call | flops 2000000 | bytes 2000000 | tf_op jit(solution)/shard_map/pallas_call | solution.py:449
  2.0 13.7 %collective-permute-start = (f32[280,128]{1,0:T(8,128)S(1)}, f32[280,128]{1,0:T(8,128)S(1)}, u32[]{:S(2)}, u32[]{:S(2)}) collective-permute-start(f32[280,128]{1,0:T(8,128)S(1)} %get-tuple-element.14), channel_id=1, source_target_pairs={{0,7},{1,2},{2,1},{3,4},{4,3},{5,6},{6,5},{7,0},{8,15},{9,10},{10,... | collective-permute-start | bytes 430088 | tf_op jit(solution)/shard_map/ppermute | solution.py:466
  15.7 1.9 %collective-permute-start.1 = (f32[280,128]{1,0:T(8,128)S(1)}, f32[280,128]{1,0:T(8,128)S(1)}, u32[]{:S(2)}, u32[]{:S(2)}) collective-permute-start(f32[280,128]{1,0:T(8,128)S(1)} %get-tuple-element.15), channel_id=1, source_target_pairs={{0,1},{1,0},{2,3},{3,2},{4,5},{5,4},{6,7},{7,6},{8,9},{9,8},{10,11... | collective-permute-start | bytes 430088 | tf_op jit(solution)/shard_map/ppermute | solution.py:466
  17.6 3.8 %collective-permute-done.got_far = f32[280,128]{1,0:T(8,128)S(1)} collective-permute-done((f32[280,128]{1,0:T(8,128)S(1)}, f32[280,128]{1,0:T(8,128)S(1)}, u32[]{:S(2)}, u32[]{:S(2)}) %collective-permute-start) | collective-permute-done | bytes 143392 | tf_op jit(solution)/shard_map/ppermute | solution.py:466
  21.4 0.5 collective-permute-done.1.got_near
  21.9 0.2 shard_map.61
  22.1 4.9 %collective-permute-start.2 = (f32[968,128]{1,0:T(8,128)S(1)}, f32[968,128]{1,0:T(8,128)S(1)}, u32[]{:S(2)}, u32[]{:S(2)}) collective-permute-start(f32[968,128]{1,0:T(8,128)S(1)} %get-tuple-element.16), channel_id=1, source_target_pairs={{0,504},{8,16},{16,8},{24,32},{32,24},{40,48},{48,40},{56,64},{64,... | collective-permute-start | bytes 1486856 | tf_op jit(solution)/shard_map/ppermute | solution.py:466
  27.0 5.3 %collective-permute-start.3 = (f32[968,128]{1,0:T(8,128)S(1)}, f32[968,128]{1,0:T(8,128)S(1)}, u32[]{:S(2)}, u32[]{:S(2)}) collective-permute-start(f32[968,128]{1,0:T(8,128)S(1)} %get-tuple-element.17), channel_id=1, source_target_pairs={{0,8},{8,0},{16,24},{24,16},{32,40},{40,32},{48,56},{56,48},{64,72... | collective-permute-start | bytes 1486856 | tf_op jit(solution)/shard_map/ppermute | solution.py:466
  32.3 0.1 shard_map.60.packs
  32.4 6.4 %collective-permute-done.2.x_far = f32[968,128]{1,0:T(8,128)S(1)} collective-permute-done((f32[968,128]{1,0:T(8,128)S(1)}, f32[968,128]{1,0:T(8,128)S(1)}, u32[]{:S(2)}, u32[]{:S(2)}) %collective-permute-start.2) | collective-permute-done | bytes 495648 | tf_op jit(solution)/shard_map/ppermute | solution.py:466
  38.8 0.0 collective-permute-done.3.x_near
  38.8 2.0 %shard_map.62 = (f32[19,6,16,128]{3,2,1,0:T(8,128)S(1)}, f32[16,8,128]{2,1,0:T(8,128)S(1)}) custom-call(f32[23,4,8,128]{3,2,1,0:T(8,128)S(1)} %get-tuple-element.12.cells, f32[6,8,128]{2,1,0:T(8,128)S(1)} %get-tuple-element.13.total, f32[23,4,16,128]{3,2,1,0:T(8,128)S(1)} %shard_map.60.packs, f32[968,128]{1,0:T(8,128)S(1)} %collective-permute-done.2.x_far, ...), custom_call_target="tpu_custom_call" | custom-call | flops 20000000 | bytes 20000000 | tf_op jit(solution)/shard_map/pallas_call | solution.py:449
  40.8 14.7 %all_to_all.10.blocks = f32[16,8,128]{2,1,0:T(8,128)S(1)} all-to-all(f32[16,8,128]{2,1,0:T(8,128)S(1)} %get-tuple-element.18), channel_id=1, replica_groups=mesh['cy'=8,'zl'=4,'core'=2,'zh'=2,'cx'=4] {'zl','core','zh'}, dimensions={0} | all-to-all | bytes 131072 | tf_op jit(solution)/shard_map/all_to_all | solution.py:507
  55.5 0.0 copy-done
  55.5 2.4 %shard_map.63 = (f32[32,2,128]{2,1,0:T(2,128)S(1)}, f32[3,4,8,128]{3,2,1,0:T(8,128)}) custom-call(f32[16,8,128]{2,1,0:T(8,128)S(1)} %all_to_all.10.blocks, f32[4776,128]{1,0:T(8,128)S(1)} %copy-done, f32[19,6,16,128]{3,2,1,0:T(8,128)S(1)} %get-tuple-element.19.post3), custom_call_target="tpu_custom_call" | custom-call | flops 10000000 | bytes 10000000 | tf_op jit(solution)/shard_map/pallas_call | solution.py:449
  57.9 17.3 %all_to_all.11.parts = f32[32,2,128]{2,1,0:T(2,128)S(1)} all-to-all(f32[32,2,128]{2,1,0:T(2,128)S(1)} %get-tuple-element.21), channel_id=1, replica_groups=mesh['cy'=8,'zl'=4,'core'=2,'zh'=2,'cx'=4] {'cy','cx'}, dimensions={0} | all-to-all | bytes 65536 | tf_op jit(solution)/shard_map/all_to_all | solution.py:519
  75.2 0.7 shard_map.64
Async XLA Ops:
  0.6 54.9 %copy-start = (f32[4776,128]{1,0:T(8,128)S(1)}, f32[4776,128]{1,0:T(8,128)}, u32[]{:S(2)}) copy-start(f32[4776,128]{1,0:T(8,128)} %constant.2.clone.table) | copy-start | bytes 7335940
  2.0 19.4 %collective-permute-start = (f32[280,128]{1,0:T(8,128)S(1)}, f32[280,128]{1,0:T(8,128)S(1)}, u32[]{:S(2)}, u32[]{:S(2)}) collective-permute-start(f32[280,128]{1,0:T(8,128)S(1)} %get-tuple-element.14), channel_id=1, source_target_pairs={{0,7},{1,2},{2,1},{3,4},{4,3},{5,6},{6,5},{7,0},{8,15},{9,10},{10,... | collective-permute-start | bytes 430088 | tf_op jit(solution)/shard_map/ppermute | solution.py:466
  15.7 6.2 %collective-permute-start.1 = (f32[280,128]{1,0:T(8,128)S(1)}, f32[280,128]{1,0:T(8,128)S(1)}, u32[]{:S(2)}, u32[]{:S(2)}) collective-permute-start(f32[280,128]{1,0:T(8,128)S(1)} %get-tuple-element.15), channel_id=1, source_target_pairs={{0,1},{1,0},{2,3},{3,2},{4,5},{5,4},{6,7},{7,6},{8,9},{9,8},{10,11... | collective-permute-start | bytes 430088 | tf_op jit(solution)/shard_map/ppermute | solution.py:466
  22.1 16.7 %collective-permute-start.2 = (f32[968,128]{1,0:T(8,128)S(1)}, f32[968,128]{1,0:T(8,128)S(1)}, u32[]{:S(2)}, u32[]{:S(2)}) collective-permute-start(f32[968,128]{1,0:T(8,128)S(1)} %get-tuple-element.16), channel_id=1, source_target_pairs={{0,504},{8,16},{16,8},{24,32},{32,24},{40,48},{48,40},{56,64},{64,... | collective-permute-start | bytes 1486856 | tf_op jit(solution)/shard_map/ppermute | solution.py:466
  27.0 11.9 %collective-permute-start.3 = (f32[968,128]{1,0:T(8,128)S(1)}, f32[968,128]{1,0:T(8,128)S(1)}, u32[]{:S(2)}, u32[]{:S(2)}) collective-permute-start(f32[968,128]{1,0:T(8,128)S(1)} %get-tuple-element.17), channel_id=1, source_target_pairs={{0,8},{8,0},{16,24},{24,16},{32,40},{40,32},{48,56},{56,48},{64,72... | collective-permute-start | bytes 1486856 | tf_op jit(solution)/shard_map/ppermute | solution.py:466

commit v10 on v9

--- a/solution.py
+++ b/solution.py
@@ -51,7 +51,7 @@
 GROUP = 8
 
 
-REACH_X = STEPS - 1
+REACH_X = STEPS - 2
 REACH_Y = STEPS - 1
 
 
@@ -72,18 +72,22 @@
         for x in range(LX - n, LX) if sign > 0 else range(n):
             out.append((ch, x, REACH_Y + CY[ch], REACH_Y - CY[ch], at))
             at += 2 * REACH_Y + LY
-    return out, -(-at // 8) * 8
+    return out, at
 
 
 SPAN = 2 * REACH_Y + LY
 Y_UP, Y_ROWS = pack_y(1)
 Y_DOWN, _ = pack_y(-1)
-X_RIGHT, X_ROWS = pack_x(1)
+X_RIGHT, NEXT_AT = pack_x(1)
 X_LEFT, _ = pack_x(-1)
 Y_UP_AT = {(ch, x): (n, at) for ch, x, _, n, at in Y_UP}
 Y_DOWN_AT = {(ch, x): (n, at) for ch, x, _, n, at in Y_DOWN}
 X_RIGHT_AT = {(ch, x): at for ch, x, _, _, at in X_RIGHT}
 X_LEFT_AT = {(ch, x): at for ch, x, _, _, at in X_LEFT}
+RIGHT = [i for i in range(19) if CX[i] == 1]
+LEFT = [i for i in range(19) if CX[i] == -1]
+NEXT = SPAN - 2
+X_ROWS = -(-(NEXT_AT + NEXT * len(RIGHT)) // 8) * 8
 
 
 def collide(f, label, drive, phase):
@@ -168,30 +172,25 @@
     far[...] = box[1]
 
 
-def second_kernel(cells, got_far, got_near, far, near, rows, box):
-    odd_y = lax.rem(lax.axis_index(GY), 2)
-    low_slot, high_slot = 1 - odd_y, odd_y
-    right = lax.rem(lax.axis_index(GX), 2)
-    rows[0] = got_near[...]
-    rows[1] = got_far[...]
-    for slot, entries in ((right, X_RIGHT), (1 - right, X_LEFT)):
-        for ch, x, low, high, at in entries:
-            n, source = Y_UP_AT[ch, x]
-            box[slot, at : at + n, :] = rows[low_slot, source : source + n, :]
-            box[slot, at + low : at + low + LY, :] = cells[ch, x]
-            n, source = Y_DOWN_AT[ch, x]
-            box[slot, at + low + LY : at + low + LY + n, :] = rows[high_slot, source : source + n, :]
-    near[...] = box[0]
-    far[...] = box[1]
-
-
 PACK = 16
 ROW0 = 8
 WORK_ROWS = 24
 
 
-def own_kernel(cells, got_far, got_near, packs, rows):
+def spin(value, i):
+    cz = VELOCITY[i][2]
+    return pltpu.roll(value, cz % NZ, 1) if cz else value
+
+
+def arrive(source, x, row, n):
+    return [
+        spin(source[i, x - CX[i], row - CY[i] : row - CY[i] + n, :], i) for i in range(19)
+    ]
+
+
+def second_kernel(cells, got_far, got_near, far, near, packs, rows, box):
     odd_y = lax.rem(lax.axis_index(GY), 2)
+    right = lax.rem(lax.axis_index(GX), 2)
     rows[0] = got_near[...]
     rows[1] = got_far[...]
     for ch in range(CHANNELS):
@@ -201,17 +200,20 @@
             packs[ch, x, low : low + LY, :] = cells[ch, x]
             high, source = Y_DOWN_AT[ch, x]
             packs[ch, x, low + LY : low + LY + high, :] = rows[odd_y, source : source + high, :]
-
-
-def spin(value, i):
-    cz = VELOCITY[i][2]
-    return pltpu.roll(value, cz % NZ, 1) if cz else value
-
-
-def arrive(source, x, row, n):
-    return [
-        spin(source[i, x - CX[i], row - CY[i] : row - CY[i] + n, :], i) for i in range(19)
-    ]
+    for slot, entries, comps, x in (
+        (right, X_RIGHT, RIGHT, LX - 1 - REACH_X),
+        (1 - right, X_LEFT, LEFT, REACH_X),
+    ):
+        for ch, layer, _, _, at in entries:
+            box[slot, at : at + SPAN, :] = packs[ch, layer, 0:SPAN, :]
+        f = [spin(packs[i, x - CX[i], 0:SPAN, :], i) for i in range(19)]
+        lab, *force = [packs[ch, x, 0:SPAN, :] for ch in range(19, CHANNELS)]
+        post, _ = collide(f, lab, force, PHASES[1])
+        for k, i in enumerate(comps):
+            at = NEXT_AT + k * NEXT
+            box[slot, at : at + NEXT, :] = post[i][1 - CY[i] : 1 - CY[i] + NEXT]
+    near[...] = box[0]
+    far[...] = box[1]
 
 
 def third_kernel(
@@ -234,9 +236,18 @@
     def add(first, second):
         return second if first is None else [a + b for a, b in zip(first, second)]
 
+    for slot, comps, x in ((left_slot, RIGHT, 0), (right_slot, LEFT, LX + 2 * REACH_X + 1)):
+        for k, i in enumerate(comps):
+            at = NEXT_AT + k * NEXT
+            low = ROW0 - (REACH_Y - 1) - CY[i]
+            one[i, x, low : low + NEXT, :] = cols[slot, at : at + NEXT, :]
     last = [total[k] for k in range(6)]
-    for step, source, target in ((1, None, one), (2, one, two), (3, two, post3)):
-        near, wide = REACH_X + 1 - step, REACH_Y + 1 - step
+    for step, source, target, near, before, after in (
+        (1, None, one, REACH_X, 0, REACH_X + 1),
+        (2, one, two, REACH_X, REACH_X + 1, REACH_X),
+        (3, two, post3, REACH_X - 1, REACH_X, REACH_X - 1),
+    ):
+        wide = REACH_Y + 1 - step
         n = LY + 2 * wide
         to = 0 if step == 3 else ROW0 - wide
         kept = None
@@ -244,12 +255,12 @@
             if step == 1:
                 f = [spin(packed(i, x - CX[i]), i) for i in range(19)]
             else:
-                f = arrive(source, x + near + 1, ROW0 - wide, n)
+                f = arrive(source, x + before, ROW0 - wide, n)
             at = REACH_Y - wide
             lab, *force = [packed(ch, x)[at : at + n] for ch in range(19, CHANNELS)]
             post, stress = collide(f, lab, force, PHASES[step])
             for i in range(19):
-                target[i, x + near, to : to + n, :] = post[i]
+                target[i, x + after, to : to + n, :] = post[i]
             if 0 <= x < LX:
                 kept = add(kept, stress)
         for k in range(6):
@@ -483,23 +494,20 @@
         ],
     )(*[pltpu.with_memory_space_constraint(value, pltpu.HBM) for value in (pops, label, drive)])
     y_far, y_near = swap(far, near, GY)
-    far, near = call(
+    far, near, packs = call(
         second_kernel,
-        [(X_ROWS, NZ), (X_ROWS, NZ)],
+        [(X_ROWS, NZ), (X_ROWS, NZ), (CHANNELS, LX, PACK, NZ)],
         [(2, Y_ROWS, NZ), (2, X_ROWS, NZ)],
         2_000_000,
     )(cells, y_far, y_near)
     x_far, x_near = swap(far, near, GX)
-    (packs,) = call(
-        own_kernel, [(CHANNELS, LX, PACK, NZ)], [(2, Y_ROWS, NZ)], 2_000_000
-    )(cells, y_far, y_near)
     post3, spread = call(
         third_kernel,
         [(19, LX + 2, PACK, NZ), (2 * GROUP, 8, NZ)],
         [
             (2, X_ROWS, NZ),
+            (19, LX + 2 * REACH_X + 2, WORK_ROWS, NZ),
             (19, LX + 2 * REACH_X, WORK_ROWS, NZ),
-            (19, LX + 2 * REACH_X - 2, WORK_ROWS, NZ),
             (18, 16, NZ),
         ],
         20_000_000,

time: 76.2 us -> 74.1 us (0.972)
  waiting for transfers between devices: 10.7 us -> 7.2 us
  blocking collectives: 32 us -> 33.3 us
    ppermute x2, waiting for transfers between devices: 10.2 us -> 6.7 us  [swap(): lax.ppermute(far, axis, far_pairs)]
    all_to_all x1, blocking collectives: 14.7 us -> 15.6 us  [local(): blocks = lax.all_to_all(spread, ('zl', 'core', 'zh'), 0, 0, tiled=False)]
    pallas_call x6 -> x5, Pallas kernels: 6.76 us -> 6.83 us  [run(): pl.pallas_call(body, out_shape=shapes, in_specs=[pl.BlockSpec(memory_spac...]
where the time goes in v10:
time: 74.1 us; the launch traced here: 73.8 us
  blocking collectives  33.3 us (45%)
  starting transfers between devices  25.7 us (35%)
  waiting for transfers between devices  7.2 us (10%)
  Pallas kernels  6.83 us (9%)
    ppermute x2, starting transfers between devices, swap(): lax.ppermute(far, axis, far_pairs)  18.5 us
    all_to_all x1, blocking collectives, local(): parts = lax.all_to_all(parts, ('cy', 'cx'), 0, 0, tiled=False)  17.7 us
    all_to_all x1, blocking collectives, local(): blocks = lax.all_to_all(spread, ('zl', 'core', 'zh'), 0, 0, tiled=False)  15.6 us
    ppermute x2, starting transfers between devices, swap(): lax.ppermute(near, axis, near_pairs)  7.2 us
    pallas_call x5, Pallas kernels, run(): pl.pallas_call(body, out_shape=shapes, in_specs=[pl.BlockSpec(memory_spac...  6.83 us
    ppermute x2, waiting for transfers between devices, swap(): lax.ppermute(far, axis, far_pairs)  6.7 us
  transfers between devices with their start and end apart: 4, of which 3 were waited for; matrix products, arithmetic and copies ran while one was open for 0% of the time, Pallas kernels for 0%

profile of v10, /device:TPU:1, one launch (start us, length us, event | category | flops | bytes accessed | tf_op | source)
XLA Modules:
  0.0 73.8 jit_solution(15040776094960462643)
XLA Ops:
  0.6 0.0 copy-start
  0.6 1.4 %shard_map.59 = (f32[23,4,8,128]{3,2,1,0:T(8,128)S(1)}, f32[6,8,128]{2,1,0:T(8,128)S(1)}, f32[280,128]{1,0:T(8,128)S(1)}, f32[280,128]{1,0:T(8,128)S(1)}) custom-call(f32[19,4,8,128]{3,2,1,0:T(8,128)} %pops_in.1, s32[4,8,128]{2,1,0:T(8,128)} %label_in.1, f32[3,4,8,128]{3,2,1,0:T(8,128)} %drive_in.1), custom_call_target="tpu_custom_call" | custom-call | flops 2000000 | bytes 2000000 | tf_op jit(solution)/shard_map/pallas_call | solution.py:460
  2.0 13.7 %collective-permute-start = (f32[280,128]{1,0:T(8,128)S(1)}, f32[280,128]{1,0:T(8,128)S(1)}, u32[]{:S(2)}, u32[]{:S(2)}) collective-permute-start(f32[280,128]{1,0:T(8,128)S(1)} %get-tuple-element.15), channel_id=1, source_target_pairs={{0,7},{1,2},{2,1},{3,4},{4,3},{5,6},{6,5},{7,0},{8,15},{9,10},{10,... | collective-permute-start | bytes 430088 | tf_op jit(solution)/shard_map/ppermute | solution.py:477
  15.7 1.9 %collective-permute-start.1 = (f32[280,128]{1,0:T(8,128)S(1)}, f32[280,128]{1,0:T(8,128)S(1)}, u32[]{:S(2)}, u32[]{:S(2)}) collective-permute-start(f32[280,128]{1,0:T(8,128)S(1)} %get-tuple-element.16), channel_id=1, source_target_pairs={{0,1},{1,0},{2,3},{3,2},{4,5},{5,4},{6,7},{7,6},{8,9},{9,8},{10,11... | collective-permute-start | bytes 430088 | tf_op jit(solution)/shard_map/ppermute | solution.py:477
  17.6 3.8 %collective-permute-done.got_far = f32[280,128]{1,0:T(8,128)S(1)} collective-permute-done((f32[280,128]{1,0:T(8,128)S(1)}, f32[280,128]{1,0:T(8,128)S(1)}, u32[]{:S(2)}, u32[]{:S(2)}) %collective-permute-start) | collective-permute-done | bytes 143392 | tf_op jit(solution)/shard_map/ppermute | solution.py:477
  21.4 0.5 collective-permute-done.1.got_near
  21.9 0.4 shard_map.60
  22.3 4.9 %collective-permute-start.2 = (f32[704,128]{1,0:T(8,128)S(1)}, f32[704,128]{1,0:T(8,128)S(1)}, u32[]{:S(2)}, u32[]{:S(2)}) collective-permute-start(f32[704,128]{1,0:T(8,128)S(1)} %get-tuple-element.18), channel_id=1, source_target_pairs={{0,504},{8,16},{16,8},{24,32},{32,24},{40,48},{48,40},{56,64},{64,... | collective-permute-start | bytes 1081352 | tf_op jit(solution)/shard_map/ppermute | solution.py:477
  27.1 5.3 %collective-permute-start.3 = (f32[704,128]{1,0:T(8,128)S(1)}, f32[704,128]{1,0:T(8,128)S(1)}, u32[]{:S(2)}, u32[]{:S(2)}) collective-permute-start(f32[704,128]{1,0:T(8,128)S(1)} %get-tuple-element.19), channel_id=1, source_target_pairs={{0,8},{8,0},{16,24},{24,16},{32,40},{40,32},{48,56},{56,48},{64,72... | collective-permute-start | bytes 1081352 | tf_op jit(solution)/shard_map/ppermute | solution.py:477
  32.4 2.9 %collective-permute-done.2.x_far = f32[704,128]{1,0:T(8,128)S(1)} collective-permute-done((f32[704,128]{1,0:T(8,128)S(1)}, f32[704,128]{1,0:T(8,128)S(1)}, u32[]{:S(2)}, u32[]{:S(2)}) %collective-permute-start.2) | collective-permute-done | bytes 360480 | tf_op jit(solution)/shard_map/ppermute | solution.py:477
  35.4 0.0 collective-permute-done.3.x_near
  35.4 2.0 %shard_map.61 = (f32[19,6,16,128]{3,2,1,0:T(8,128)S(1)}, f32[16,8,128]{2,1,0:T(8,128)S(1)}) custom-call(f32[23,4,8,128]{3,2,1,0:T(8,128)S(1)} %get-tuple-element.13.cells, f32[6,8,128]{2,1,0:T(8,128)S(1)} %get-tuple-element.14.total, f32[23,4,16,128]{3,2,1,0:T(8,128)S(1)} %get-tuple-element.17.packs, f32[704,128]{1,0:T(8,128)S(1)} %collective-permute-done.2.x_far, ...), custom_call_target="tpu_custom_call" | custom-call | flops 20000000 | bytes 20000000 | tf_op jit(solution)/shard_map/pallas_call | solution.py:460
  37.4 15.6 %all_to_all.10.blocks = f32[16,8,128]{2,1,0:T(8,128)S(1)} all-to-all(f32[16,8,128]{2,1,0:T(8,128)S(1)} %get-tuple-element.20), channel_id=1, replica_groups=mesh['cy'=8,'zl'=4,'core'=2,'zh'=2,'cx'=4] {'zl','core','zh'}, dimensions={0} | all-to-all | bytes 131072 | tf_op jit(solution)/shard_map/all_to_all | solution.py:515
  53.0 0.0 copy-done
  53.0 2.4 %shard_map.62 = (f32[32,2,128]{2,1,0:T(2,128)S(1)}, f32[3,4,8,128]{3,2,1,0:T(8,128)}) custom-call(f32[16,8,128]{2,1,0:T(8,128)S(1)} %all_to_all.10.blocks, f32[4776,128]{1,0:T(8,128)S(1)} %copy-done, f32[19,6,16,128]{3,2,1,0:T(8,128)S(1)} %get-tuple-element.21.post3), custom_call_target="tpu_custom_call" | custom-call | flops 10000000 | bytes 10000000 | tf_op jit(solution)/shard_map/pallas_call | solution.py:460
  55.4 17.7 %all_to_all.11.parts = f32[32,2,128]{2,1,0:T(2,128)S(1)} all-to-all(f32[32,2,128]{2,1,0:T(2,128)S(1)} %get-tuple-element.23), channel_id=1, replica_groups=mesh['cy'=8,'zl'=4,'core'=2,'zh'=2,'cx'=4] {'cy','cx'}, dimensions={0} | all-to-all | bytes 65536 | tf_op jit(solution)/shard_map/all_to_all | solution.py:527
  73.1 0.7 shard_map.63
Async XLA Ops:
  0.6 52.4 %copy-start = (f32[4776,128]{1,0:T(8,128)S(1)}, f32[4776,128]{1,0:T(8,128)}, u32[]{:S(2)}) copy-start(f32[4776,128]{1,0:T(8,128)} %constant.2.clone.table) | copy-start | bytes 7335940
  2.0 19.4 %collective-permute-start = (f32[280,128]{1,0:T(8,128)S(1)}, f32[280,128]{1,0:T(8,128)S(1)}, u32[]{:S(2)}, u32[]{:S(2)}) collective-permute-start(f32[280,128]{1,0:T(8,128)S(1)} %get-tuple-element.15), channel_id=1, source_target_pairs={{0,7},{1,2},{2,1},{3,4},{4,3},{5,6},{6,5},{7,0},{8,15},{9,10},{10,... | collective-permute-start | bytes 430088 | tf_op jit(solution)/shard_map/ppermute | solution.py:477
  15.7 6.2 %collective-permute-start.1 = (f32[280,128]{1,0:T(8,128)S(1)}, f32[280,128]{1,0:T(8,128)S(1)}, u32[]{:S(2)}, u32[]{:S(2)}) collective-permute-start(f32[280,128]{1,0:T(8,128)S(1)} %get-tuple-element.16), channel_id=1, source_target_pairs={{0,1},{1,0},{2,3},{3,2},{4,5},{5,4},{6,7},{7,6},{8,9},{9,8},{10,11... | collective-permute-start | bytes 430088 | tf_op jit(solution)/shard_map/ppermute | solution.py:477
  22.3 13.1 %collective-permute-start.2 = (f32[704,128]{1,0:T(8,128)S(1)}, f32[704,128]{1,0:T(8,128)S(1)}, u32[]{:S(2)}, u32[]{:S(2)}) collective-permute-start(f32[704,128]{1,0:T(8,128)S(1)} %get-tuple-element.18), channel_id=1, source_target_pairs={{0,504},{8,16},{16,8},{24,32},{32,24},{40,48},{48,40},{56,64},{64,... | collective-permute-start | bytes 1081352 | tf_op jit(solution)/shard_map/ppermute | solution.py:477
  27.1 8.2 %collective-permute-start.3 = (f32[704,128]{1,0:T(8,128)S(1)}, f32[704,128]{1,0:T(8,128)S(1)}, u32[]{:S(2)}, u32[]{:S(2)}) collective-permute-start(f32[704,128]{1,0:T(8,128)S(1)} %get-tuple-element.19), channel_id=1, source_target_pairs={{0,8},{8,0},{16,24},{24,16},{32,40},{40,32},{48,56},{56,48},{64,72... | collective-permute-start | bytes 1081352 | tf_op jit(solution)/shard_map/ppermute | solution.py:477

commit v11 on v10

--- a/solution.py
+++ b/solution.py
@@ -68,7 +68,7 @@
 def pack_x(sign):
     out, at = [], 0
     for ch in range(CHANNELS):
-        n = REACH_X + sign * CX[ch]
+        n = REACH_X - 1 + sign * CX[ch] if ch < 19 else REACH_X
         for x in range(LX - n, LX) if sign > 0 else range(n):
             out.append((ch, x, REACH_Y + CY[ch], REACH_Y - CY[ch], at))
             at += 2 * REACH_Y + LY
@@ -84,10 +84,22 @@
 Y_DOWN_AT = {(ch, x): (n, at) for ch, x, _, n, at in Y_DOWN}
 X_RIGHT_AT = {(ch, x): at for ch, x, _, _, at in X_RIGHT}
 X_LEFT_AT = {(ch, x): at for ch, x, _, _, at in X_LEFT}
-RIGHT = [i for i in range(19) if CX[i] == 1]
-LEFT = [i for i in range(19) if CX[i] == -1]
 NEXT = SPAN - 2
-X_ROWS = -(-(NEXT_AT + NEXT * len(RIGHT)) // 8) * 8
+INNER = (1, 2)
+
+
+def pack_next(sign):
+    out, at = [], NEXT_AT
+    for depth, x in enumerate(INNER[::-1] if sign > 0 else INNER):
+        for i in range(19):
+            if sign * CX[i] >= depth:
+                out.append((i, x, at))
+                at += NEXT
+    return out, -(-at // 8) * 8
+
+
+NEXT_RIGHT, X_ROWS = pack_next(1)
+NEXT_LEFT, _ = pack_next(-1)
 
 
 def collide(f, label, drive, phase):
@@ -200,18 +212,16 @@
             packs[ch, x, low : low + LY, :] = cells[ch, x]
             high, source = Y_DOWN_AT[ch, x]
             packs[ch, x, low + LY : low + LY + high, :] = rows[odd_y, source : source + high, :]
-    for slot, entries, comps, x in (
-        (right, X_RIGHT, RIGHT, LX - 1 - REACH_X),
-        (1 - right, X_LEFT, LEFT, REACH_X),
-    ):
-        for ch, layer, _, _, at in entries:
-            box[slot, at : at + SPAN, :] = packs[ch, layer, 0:SPAN, :]
+    after = {}
+    for x in INNER:
         f = [spin(packs[i, x - CX[i], 0:SPAN, :], i) for i in range(19)]
         lab, *force = [packs[ch, x, 0:SPAN, :] for ch in range(19, CHANNELS)]
-        post, _ = collide(f, lab, force, PHASES[1])
-        for k, i in enumerate(comps):
-            at = NEXT_AT + k * NEXT
-            box[slot, at : at + NEXT, :] = post[i][1 - CY[i] : 1 - CY[i] + NEXT]
+        after[x], _ = collide(f, lab, force, PHASES[1])
+    for slot, entries, following in ((right, X_RIGHT, NEXT_RIGHT), (1 - right, X_LEFT, NEXT_LEFT)):
+        for ch, x, _, _, at in entries:
+            box[slot, at : at + SPAN, :] = packs[ch, x, 0:SPAN, :]
+        for i, x, at in following:
+            box[slot, at : at + NEXT, :] = after[x][i][1 - CY[i] : 1 - CY[i] + NEXT]
     near[...] = box[0]
     far[...] = box[1]
 
@@ -236,14 +246,13 @@
     def add(first, second):
         return second if first is None else [a + b for a, b in zip(first, second)]
 
-    for slot, comps, x in ((left_slot, RIGHT, 0), (right_slot, LEFT, LX + 2 * REACH_X + 1)):
-        for k, i in enumerate(comps):
-            at = NEXT_AT + k * NEXT
+    for slot, following, shift in ((left_slot, NEXT_RIGHT, -LX), (right_slot, NEXT_LEFT, LX)):
+        for i, x, at in following:
             low = ROW0 - (REACH_Y - 1) - CY[i]
-            one[i, x, low : low + NEXT, :] = cols[slot, at : at + NEXT, :]
+            one[i, x + shift + REACH_X + 1, low : low + NEXT, :] = cols[slot, at : at + NEXT, :]
     last = [total[k] for k in range(6)]
     for step, source, target, near, before, after in (
-        (1, None, one, REACH_X, 0, REACH_X + 1),
+        (1, None, one, REACH_X - 1, 0, REACH_X + 1),
         (2, one, two, REACH_X, REACH_X + 1, REACH_X),
         (3, two, post3, REACH_X - 1, REACH_X, REACH_X - 1),
     ):

time: 74.1 us -> 73.4 us (level)
  waiting for transfers between devices: 7.2 us -> 6.15 us
    ppermute x2, waiting for transfers between devices: 6.7 us -> 5.65 us  [swap(): lax.ppermute(far, axis, far_pairs)]
where the time goes in v11:
time: 73.4 us; the launch traced here: 73.1 us
  blocking collectives  33.8 us (46%)
  starting transfers between devices  25.7 us (35%)
  Pallas kernels  6.72 us (9%)
  waiting for transfers between devices  6.15 us (8%)
    ppermute x2, starting transfers between devices, swap(): lax.ppermute(far, axis, far_pairs)  18.5 us
    all_to_all x1, blocking collectives, local(): parts = lax.all_to_all(parts, ('cy', 'cx'), 0, 0, tiled=False)  17.7 us
    all_to_all x1, blocking collectives, local(): blocks = lax.all_to_all(spread, ('zl', 'core', 'zh'), 0, 0, tiled=False)  16.2 us
    ppermute x2, starting transfers between devices, swap(): lax.ppermute(near, axis, near_pairs)  7.2 us
    pallas_call x5, Pallas kernels, run(): pl.pallas_call(body, out_shape=shapes, in_specs=[pl.BlockSpec(memory_spac...  6.72 us
    ppermute x2, waiting for transfers between devices, swap(): lax.ppermute(far, axis, far_pairs)  5.65 us
  transfers between devices with their start and end apart: 4, of which 3 were waited for; matrix products, arithmetic and copies ran while one was open for 0% of the time, Pallas kernels for 0%

profile of v11, /device:TPU:1, one launch (start us, length us, event | category | flops | bytes accessed | tf_op | source)
XLA Modules:
  0.0 73.1 jit_solution(4489142911409490577)
XLA Ops:
  0.6 0.0 copy-start
  0.6 1.4 %shard_map.59 = (f32[23,4,8,128]{3,2,1,0:T(8,128)S(1)}, f32[6,8,128]{2,1,0:T(8,128)S(1)}, f32[280,128]{1,0:T(8,128)S(1)}, f32[280,128]{1,0:T(8,128)S(1)}) custom-call(f32[19,4,8,128]{3,2,1,0:T(8,128)} %pops_in.1, s32[4,8,128]{2,1,0:T(8,128)} %label_in.1, f32[3,4,8,128]{3,2,1,0:T(8,128)} %drive_in.1), custom_call_target="tpu_custom_call" | custom-call | flops 2000000 | bytes 2000000 | tf_op jit(solution)/shard_map/pallas_call | solution.py:469
  2.0 13.7 %collective-permute-start = (f32[280,128]{1,0:T(8,128)S(1)}, f32[280,128]{1,0:T(8,128)S(1)}, u32[]{:S(2)}, u32[]{:S(2)}) collective-permute-start(f32[280,128]{1,0:T(8,128)S(1)} %get-tuple-element.15), channel_id=1, source_target_pairs={{0,7},{1,2},{2,1},{3,4},{4,3},{5,6},{6,5},{7,0},{8,15},{9,10},{10,... | collective-permute-start | bytes 430088 | tf_op jit(solution)/shard_map/ppermute | solution.py:486
  15.7 1.9 %collective-permute-start.1 = (f32[280,128]{1,0:T(8,128)S(1)}, f32[280,128]{1,0:T(8,128)S(1)}, u32[]{:S(2)}, u32[]{:S(2)}) collective-permute-start(f32[280,128]{1,0:T(8,128)S(1)} %get-tuple-element.16), channel_id=1, source_target_pairs={{0,1},{1,0},{2,3},{3,2},{4,5},{5,4},{6,7},{7,6},{8,9},{9,8},{10,11... | collective-permute-start | bytes 430088 | tf_op jit(solution)/shard_map/ppermute | solution.py:486
  17.6 3.8 %collective-permute-done.got_far = f32[280,128]{1,0:T(8,128)S(1)} collective-permute-done((f32[280,128]{1,0:T(8,128)S(1)}, f32[280,128]{1,0:T(8,128)S(1)}, u32[]{:S(2)}, u32[]{:S(2)}) %collective-permute-start) | collective-permute-done | bytes 143392 | tf_op jit(solution)/shard_map/ppermute | solution.py:486
  21.4 0.5 collective-permute-done.1.got_near
  21.9 0.4 shard_map.60
  22.3 4.8 %collective-permute-start.2 = (f32[608,128]{1,0:T(8,128)S(1)}, f32[608,128]{1,0:T(8,128)S(1)}, u32[]{:S(2)}, u32[]{:S(2)}) collective-permute-start(f32[608,128]{1,0:T(8,128)S(1)} %get-tuple-element.18), channel_id=1, source_target_pairs={{0,504},{8,16},{16,8},{24,32},{32,24},{40,48},{48,40},{56,64},{64,... | collective-permute-start | bytes 933896 | tf_op jit(solution)/shard_map/ppermute | solution.py:486
  27.1 5.3 %collective-permute-start.3 = (f32[608,128]{1,0:T(8,128)S(1)}, f32[608,128]{1,0:T(8,128)S(1)}, u32[]{:S(2)}, u32[]{:S(2)}) collective-permute-start(f32[608,128]{1,0:T(8,128)S(1)} %get-tuple-element.19), channel_id=1, source_target_pairs={{0,8},{8,0},{16,24},{24,16},{32,40},{40,32},{48,56},{56,48},{64,72... | collective-permute-start | bytes 933896 | tf_op jit(solution)/shard_map/ppermute | solution.py:486
  32.4 1.9 %collective-permute-done.2.x_far = f32[608,128]{1,0:T(8,128)S(1)} collective-permute-done((f32[608,128]{1,0:T(8,128)S(1)}, f32[608,128]{1,0:T(8,128)S(1)}, u32[]{:S(2)}, u32[]{:S(2)}) %collective-permute-start.2) | collective-permute-done | bytes 311328 | tf_op jit(solution)/shard_map/ppermute | solution.py:486
  34.3 0.0 collective-permute-done.3.x_near
  34.3 1.9 %shard_map.61 = (f32[19,6,16,128]{3,2,1,0:T(8,128)S(1)}, f32[16,8,128]{2,1,0:T(8,128)S(1)}) custom-call(f32[23,4,8,128]{3,2,1,0:T(8,128)S(1)} %get-tuple-element.13.cells, f32[6,8,128]{2,1,0:T(8,128)S(1)} %get-tuple-element.14.total, f32[23,4,16,128]{3,2,1,0:T(8,128)S(1)} %get-tuple-element.17.packs, f32[608,128]{1,0:T(8,128)S(1)} %collective-permute-done.2.x_far, ...), custom_call_target="tpu_custom_call" | custom-call | flops 20000000 | bytes 20000000 | tf_op jit(solution)/shard_map/pallas_call | solution.py:469
  36.2 16.2 %all_to_all.10.blocks = f32[16,8,128]{2,1,0:T(8,128)S(1)} all-to-all(f32[16,8,128]{2,1,0:T(8,128)S(1)} %get-tuple-element.20), channel_id=1, replica_groups=mesh['cy'=8,'zl'=4,'core'=2,'zh'=2,'cx'=4] {'zl','core','zh'}, dimensions={0} | all-to-all | bytes 131072 | tf_op jit(solution)/shard_map/all_to_all | solution.py:524
  52.4 0.0 copy-done
  52.4 2.4 %shard_map.62 = (f32[32,2,128]{2,1,0:T(2,128)S(1)}, f32[3,4,8,128]{3,2,1,0:T(8,128)}) custom-call(f32[16,8,128]{2,1,0:T(8,128)S(1)} %all_to_all.10.blocks, f32[4776,128]{1,0:T(8,128)S(1)} %copy-done, f32[19,6,16,128]{3,2,1,0:T(8,128)S(1)} %get-tuple-element.21.post3), custom_call_target="tpu_custom_call" | custom-call | flops 10000000 | bytes 10000000 | tf_op jit(solution)/shard_map/pallas_call | solution.py:469
  54.7 17.7 %all_to_all.11.parts = f32[32,2,128]{2,1,0:T(2,128)S(1)} all-to-all(f32[32,2,128]{2,1,0:T(2,128)S(1)} %get-tuple-element.23), channel_id=1, replica_groups=mesh['cy'=8,'zl'=4,'core'=2,'zh'=2,'cx'=4] {'cy','cx'}, dimensions={0} | all-to-all | bytes 65536 | tf_op jit(solution)/shard_map/all_to_all | solution.py:536
  72.4 0.7 shard_map.63
Async XLA Ops:
  0.6 51.7 %copy-start = (f32[4776,128]{1,0:T(8,128)S(1)}, f32[4776,128]{1,0:T(8,128)}, u32[]{:S(2)}) copy-start(f32[4776,128]{1,0:T(8,128)} %constant.2.clone.table) | copy-start | bytes 7335940
  2.0 19.4 %collective-permute-start = (f32[280,128]{1,0:T(8,128)S(1)}, f32[280,128]{1,0:T(8,128)S(1)}, u32[]{:S(2)}, u32[]{:S(2)}) collective-permute-start(f32[280,128]{1,0:T(8,128)S(1)} %get-tuple-element.15), channel_id=1, source_target_pairs={{0,7},{1,2},{2,1},{3,4},{4,3},{5,6},{6,5},{7,0},{8,15},{9,10},{10,... | collective-permute-start | bytes 430088 | tf_op jit(solution)/shard_map/ppermute | solution.py:486
  15.7 6.2 %collective-permute-start.1 = (f32[280,128]{1,0:T(8,128)S(1)}, f32[280,128]{1,0:T(8,128)S(1)}, u32[]{:S(2)}, u32[]{:S(2)}) collective-permute-start(f32[280,128]{1,0:T(8,128)S(1)} %get-tuple-element.16), channel_id=1, source_target_pairs={{0,1},{1,0},{2,3},{3,2},{4,5},{5,4},{6,7},{7,6},{8,9},{9,8},{10,11... | collective-permute-start | bytes 430088 | tf_op jit(solution)/shard_map/ppermute | solution.py:486
  22.3 12.0 %collective-permute-start.2 = (f32[608,128]{1,0:T(8,128)S(1)}, f32[608,128]{1,0:T(8,128)S(1)}, u32[]{:S(2)}, u32[]{:S(2)}) collective-permute-start(f32[608,128]{1,0:T(8,128)S(1)} %get-tuple-element.18), channel_id=1, source_target_pairs={{0,504},{8,16},{16,8},{24,32},{32,24},{40,48},{48,40},{56,64},{64,... | collective-permute-start | bytes 933896 | tf_op jit(solution)/shard_map/ppermute | solution.py:486
  27.1 7.2 %collective-permute-start.3 = (f32[608,128]{1,0:T(8,128)S(1)}, f32[608,128]{1,0:T(8,128)S(1)}, u32[]{:S(2)}, u32[]{:S(2)}) collective-permute-start(f32[608,128]{1,0:T(8,128)S(1)} %get-tuple-element.19), channel_id=1, source_target_pairs={{0,8},{8,0},{16,24},{24,16},{32,40},{40,32},{48,56},{56,48},{64,72... | collective-permute-start | bytes 933896 | tf_op jit(solution)/shard_map/ppermute | solution.py:486
